TPU v7x, 256 devices: a whole 4x4x8 slice. The times are simulated.
256 devices in a mesh: hyp: 4 (over z_lo), row: 16 (over x, z_hi, core), col: 4 (over y).
Axes of the slice: x: 4, y: 4, z: 8 (z_hi: 2, z_lo: 4; z = z_hi * 4 + z_lo), core: 2. Of those that a mesh axis runs over, the one named last changes fastest.
Arguments:
- front_orig: bfloat16 [40960, 10240], P(('hyp', 'row'), 'col'), parts along dimension 0, as said below
- child_updates: bfloat16 [65536, 8192], P(('hyp', 'row'), 'col'), parts along dimension 0, as said below
- child_map: int32 [8, 64], P('hyp'), parts along dimension 0, may hold values from 0 to 79, as said below
- panel_inverse: bfloat16 [1024, 256], P('hyp'), parts along dimension 0, as said below
Outputs:
- schur: bfloat16 [40960, 10240], P(('hyp', 'row'), 'col'), parts along dimension 0
- panel: bfloat16 [40960, 256], P(('hyp', 'row')), parts along dimension 0
There are 4 independent parts, one for each index of `hyp`. A program takes and returns all parts, laid end to end along the dimension named above; each array names one. Nothing has to cross between parts.
Inputs may be any that keep to these rules, and one draw needn't show every extreme that they name: `child_map`: each child's entries are distinct. Parent block p lies on row index p // 5 and column index p // 20. Of the 8 blocks of a child on one row index (child c on row indices c * 8 to (c + 1) * 8 - 1, in order), at most 1 lie on one parent row index; of the 16 blocks on one column index, at most 4 lie on one parent column index. Every parent row index receives the same number of blocks of each child. `child_updates`: each child's update block is symmetric. `front_orig`: Symmetric. `panel_inverse`: upper triangular with a positive diagonal.
All inputs are finite; a program needn't handle non-finite values.
Results may differ from a plain program's by a relative error of at most 0.0052.
Values may be sent and summed in bfloat16 or wider, within the bound.
No kernel may reach another device: no remote copies, remote signals or barrier semaphores. Data moves between devices by JAX's collectives and lax.ppermute only.
A program may use at most 128 MiB of HBM per device.

v0:
```python
import jax
import jax.numpy as jnp
from jax import lax
from jax.experimental import pallas as pl
from jax.experimental.pallas import tpu as pltpu
from jax.sharding import Mesh, PartitionSpec as P


SMEM = pltpu.MemorySpace.SMEM
VMEM = pltpu.MemorySpace.VMEM
CB = 64
MB = 5
QB = 20
FB = 80
PLACES = [(x, z, core) for x in range(4) for z in range(2) for core in range(2)]


def params(mib):
    return pltpu.CompilerParams(vmem_limit_bytes=mib << 20)


def tables_kernel(map_ref, pos_ref, sel_ref, jsel_ref, jl_ref, krow_ref, kcol_ref, inv_ref, cnt_ref):
    row = pos_ref[0]
    col = pos_ref[1]
    x = row // 4
    zk = row % 4
    child = row // 8
    group = (row % 8) // 2

    def clear(i, _):
        inv_ref[i] = -1
        return 0

    lax.fori_loop(0, 2 * FB, clear, 0, unroll=8)
    for c in range(2):

        def invert(i, _):
            inv_ref[c * FB + map_ref[c, i]] = i
            return 0

        lax.fori_loop(0, CB, invert, 0, unroll=8)
    for y in range(4):

        def pick(q, counts):
            v = inv_ref[child * FB + y * QB + q]
            hit = jnp.logical_and(v >= 0, v // 16 == group)
            sel_ref[jnp.where(hit, y * 4 + counts[0], 16)] = v % 16
            hit_j = jnp.logical_and(v >= 0, v // 16 == col)
            jsel_ref[jnp.where(hit_j, y * 4 + counts[1], 16)] = v % 16
            return counts[0] + hit.astype(jnp.int32), counts[1] + hit_j.astype(jnp.int32)

        lax.fori_loop(0, QB, pick, (jnp.int32(0), jnp.int32(0)))
    for c in range(2):
        count = 0
        for p in range(MB):
            hit = inv_ref[c * FB + row * MB + p] >= 0
            krow_ref[c * MB + p] = jnp.where(hit, count, -1)
            count = count + hit.astype(jnp.int32)
        for g in range(10):
            cnt_ref[g] = 0

        def arrive(q, _):
            v = inv_ref[c * FB + col * QB + q]
            hit = v >= 0
            g = jnp.where(hit, v // 16, 4)
            rank = cnt_ref[g]
            cnt_ref[g] = rank + 1
            sender = ((g % 2) * 2 + rank % 2) ^ zk
            kcol_ref[c * QB + q] = jnp.where(hit, ((rank // 2) * 4 + sender) * 4 + c * 2 + g // 2, -1)
            return 0

        lax.fori_loop(0, QB, arrive, 0)
        for d in range(4):

            def pass_on(q, count):
                v = inv_ref[c * FB + x * QB + d * MB + q]
                hit = v >= 0
                g = jnp.where(hit, v // 16, 4)
                slot = cnt_ref[5 + g]
                cnt_ref[5 + g] = slot + 1
                jl_ref[jnp.where(hit, c * 16 + d * 4 + count, 32)] = g * 4 + slot
                return count + hit.astype(jnp.int32)

            lax.fori_loop(0, MB, pass_on, jnp.int32(0))


def tables(child_map, pos):
    shapes = [32, 32, 48, 16, 48]
    return pl.pallas_call(
        tables_kernel,
        out_shape=[jax.ShapeDtypeStruct((n,), jnp.int32) for n in shapes],
        in_specs=[pl.BlockSpec(memory_space=SMEM)] * 2,
        out_specs=[pl.BlockSpec(memory_space=SMEM)] * 5,
        scratch_shapes=[pltpu.SMEM((2 * FB,), jnp.int32), pltpu.SMEM((16,), jnp.int32)],
        compiler_params=params(63),
        name="tables",
    )(child_map, pos)


def pack_first(sel, jsel, pos, own, other, chunk):
    block = own.shape[0] // 8
    half = block // 2

    def kernel(sel_ref, jsel_ref, pos_ref, own_ref, other_ref, out_ref, sem):
        core = pos_ref[0] % 2
        for y in range(4):
            index = sel_ref[y * 4 + 2 * (chunk // 2) + core]
            rows = pl.ds(pl.multiple_of((index % 8) * block + (chunk % 2) * half, half), half)
            mine = index // 8 == core

            def copy(ref):
                for x in range(4):
                    for k in range(4):
                        cols = pl.ds(pl.multiple_of(jsel_ref[x * 4 + k] * block, block), block)
                        pltpu.make_async_copy(
                            ref.at[rows, cols],
                            out_ref.at[x * 4 + y, :, pl.ds(k * block, block)],
                            sem,
                        ).start()

            pl.when(mine)(lambda: copy(own_ref))
            pl.when(jnp.logical_not(mine))(lambda: copy(other_ref))

        pltpu.make_async_copy(out_ref, out_ref, sem).wait()

    return pl.pallas_call(
        kernel,
        out_shape=jax.ShapeDtypeStruct((16, half, 4 * block), own.dtype),
        in_specs=[pl.BlockSpec(memory_space=SMEM)] * 3 + [pl.BlockSpec(memory_space=pltpu.MemorySpace.HBM)] * 2,
        out_specs=pl.BlockSpec(memory_space=VMEM),
        scratch_shapes=[pltpu.SemaphoreType.DMA(())],
        compiler_params=params(63),
    )(sel, jsel, pos, own, other)


def pack_second(jl, pos, arrived):
    block = arrived.shape[2] // 4

    def kernel(jl_ref, pos_ref, in_ref, *out_refs):
        zk = pos_ref[0] % 4
        for d in range(4):
            for xs in range(4):
                for k in range(4):
                    code = jl_ref[(xs // 2) * 16 + (zk ^ d) * 4 + k]
                    cols = pl.ds(pl.multiple_of((code % 4) * block, block), block)
                    out_refs[d][xs, :, k * block : (k + 1) * block] = in_ref[
                        xs * 4 + code // 4, :, cols
                    ]

    return pl.pallas_call(
        kernel,
        out_shape=[jax.ShapeDtypeStruct((4,) + arrived.shape[1:], arrived.dtype)] * 4,
        in_specs=[pl.BlockSpec(memory_space=SMEM)] * 2 + [pl.BlockSpec(memory_space=VMEM)],
        out_specs=[pl.BlockSpec(memory_space=VMEM)] * 4,
        compiler_params=params(63),
    )(jl, pos, arrived)


def fill_eyes(eye_ref):
    block = eye_ref.shape[1]
    i = lax.broadcasted_iota(jnp.int32, (block, block), 0)
    j = lax.broadcasted_iota(jnp.int32, (block, block), 1)
    eye = (i == j).astype(jnp.float32).astype(jnp.bfloat16)
    zero = jnp.zeros((block, block), jnp.bfloat16)
    for v in range(4):
        eye_ref[v, :, :block] = eye if v & 1 else zero
        eye_ref[v, :, block:] = eye if v & 2 else zero


def front_tile(orig, buf_ref, krow_ref, kcol_ref, eye_ref, p, q):
    block = orig.shape[0]
    parts = []
    bits = 0
    for c in range(2):
        k = krow_ref[c * MB + p]
        e = kcol_ref[c * QB + q]
        bits = bits + jnp.where(jnp.logical_and(k >= 0, e >= 0), 1 << c, 0)
        start = pl.multiple_of(jnp.maximum(k, 0) * block, block)
        parts.append(buf_ref[jnp.maximum(e, 0), :, pl.ds(start, block)])
    both = jnp.concatenate(parts, axis=1)
    added = lax.dot_general(
        eye_ref[bits], both, (((1,), (1,)), ((), ())), preferred_element_type=jnp.float32
    )
    return (orig.astype(jnp.float32) + added).astype(jnp.bfloat16)


def gather(refs, buf_ref, sem, meanwhile):
    half = buf_ref.shape[1] // 2
    copies = [
        pltpu.make_async_copy(
            ref,
            buf_ref.at[pl.ds((n // 8) * 16 + (n % 4) * 4, 4), pl.ds((n // 4 % 2) * half, half)],
            sem.at[n],
        )
        for n, ref in enumerate(refs)
    ]
    for copy in copies:
        copy.start()
    meanwhile()
    for copy in copies:
        copy.wait()


def strip_panel(krow, kcol, arrived, front_orig, panel_inverse):
    block = arrived[0].shape[2] // 4
    rows = front_orig.shape[0]

    def kernel(krow_ref, kcol_ref, *refs):
        orig_ref, inverse_ref, out_ref, buf_ref, eye_ref, sem = refs[8:]
        gather(refs[:8], buf_ref, sem, lambda: fill_eyes(eye_ref))
        for p in range(MB):
            here = slice(p * block, (p + 1) * block)
            tiles = [
                front_tile(
                    orig_ref[here, q * block : (q + 1) * block],
                    buf_ref, krow_ref, kcol_ref, eye_ref, p, q,
                )
                for q in range(2)
            ]
            out_ref[here, :] = jnp.dot(
                jnp.concatenate(tiles, axis=1), inverse_ref[...], preferred_element_type=jnp.float32
            ).astype(jnp.bfloat16)

    return pl.pallas_call(
        kernel,
        grid=(1,),
        out_shape=jax.ShapeDtypeStruct((rows, 2 * block), jnp.bfloat16),
        in_specs=[pl.BlockSpec(memory_space=SMEM)] * 2
        + [pl.BlockSpec(memory_space=pl.ANY)] * 8
        + [
            pl.BlockSpec((rows, 2 * block), lambda i: (0, 0)),
            pl.BlockSpec(memory_space=VMEM),
        ],
        out_specs=pl.BlockSpec(memory_space=VMEM),
        scratch_shapes=[
            pltpu.VMEM((16, block, 4 * block), jnp.bfloat16),
            pltpu.VMEM((4, block, 2 * block), jnp.bfloat16),
            pltpu.SemaphoreType.DMA((8,)),
        ],
        compiler_params=params(63),
        name="strip_panel",
    )(krow, kcol, *arrived, front_orig, panel_inverse)


def assemble(krow, kcol, arrived, front_orig):
    block = arrived[0].shape[2] // 4

    def kernel(krow_ref, kcol_ref, *refs):
        orig_ref, out_ref, buf_ref, eye_ref, sem = refs[16:]
        gather(refs[:16], buf_ref, sem, lambda: fill_eyes(eye_ref))

        def column(q, _):
            cols = pl.ds(pl.multiple_of(q * block, block), block)
            for p in range(MB):
                here = slice(p * block, (p + 1) * block)
                out_ref[here, cols] = front_tile(
                    orig_ref[here, cols], buf_ref, krow_ref, kcol_ref, eye_ref, p, q
                )
            return 0

        lax.fori_loop(0, QB, column, 0)

    return pl.pallas_call(
        kernel,
        out_shape=jax.ShapeDtypeStruct(front_orig.shape, jnp.bfloat16),
        in_specs=[pl.BlockSpec(memory_space=SMEM)] * 2
        + [pl.BlockSpec(memory_space=pl.ANY)] * 16
        + [pl.BlockSpec(memory_space=VMEM)],
        out_specs=pl.BlockSpec(memory_space=VMEM),
        scratch_shapes=[
            pltpu.VMEM((32, block, 4 * block), jnp.bfloat16),
            pltpu.VMEM((4, block, 2 * block), jnp.bfloat16),
            pltpu.SemaphoreType.DMA((16,)),
        ],
        compiler_params=params(63),
        name="assemble",
    )(krow, kcol, *arrived, front_orig)


def finish(pos, front, row_panel, pieces):
    _, cols = front.shape
    wide = cols // 4

    def kernel(pos_ref, front_ref, row_ref, p0, p1, p2, p3, out_ref):
        zk = pos_ref[0] % 4
        for w, ref in enumerate((p0, p1, p2, p3)):
            here = pl.ds(pl.multiple_of((zk ^ w) * wide, wide), wide)
            update = lax.dot_general(
                row_ref[...], ref[...], (((1,), (1,)), ((), ())), preferred_element_type=jnp.float32
            )
            out_ref[:, here] = (front_ref[:, here].astype(jnp.float32) - update).astype(jnp.bfloat16)

    return pl.pallas_call(
        kernel,
        out_shape=jax.ShapeDtypeStruct(front.shape, jnp.bfloat16),
        in_specs=[pl.BlockSpec(memory_space=SMEM)] + [pl.BlockSpec(memory_space=VMEM)] * 6,
        out_specs=pl.BlockSpec(memory_space=VMEM),
        compiler_params=params(63),
        name="finish",
    )(pos, front, row_panel, *pieces)


def device(x, z, core, y):
    return ((x * 2 + z) * 2 + core) * 4 + y


def moved(array, pairs):
    return lax.ppermute(array, ("x", "z", "core", "col"), pairs)


def over_zk(array, d):
    return lax.ppermute(array, ("z", "core"), [(r, r ^ d) for r in range(4)])


def local(front_orig, child_updates, child_map, panel_inverse):
    me_x = lax.axis_index("x")
    me_z = lax.axis_index("z")
    me_core = lax.axis_index("core")
    me_col = lax.axis_index("col")
    pos = jnp.stack([me_x * 4 + me_z * 2 + me_core, me_col]).astype(jnp.int32)
    other = over_zk(child_updates, 1)
    sel, jsel, jl, krow, kcol = tables(child_map, pos)

    arrived = []
    for chunk in range(4):
        sent = pack_first(sel, jsel, pos, child_updates, other, chunk)
        part = lax.all_to_all(sent, ("x", "col"), 0, 0, tiled=True)
        out = pack_second(jl, pos, part)
        arrived += [out[0]] + [over_zk(out[d], d) for d in (1, 2, 3)]
    first = arrived[:8]

    panel_0 = strip_panel(krow, kcol, first, front_orig, panel_inverse)
    spread = [
        moved(panel_0, [(device(x, z, k, 0), device(x, z, k, y)) for x, z, k in PLACES])
        for y in range(1, 4)
    ]
    sides = [
        moved(panel_0, [(device(x, z, k, 0), device((x + d) % 4, z, k, x)) for x, z, k in PLACES])
        for d in range(1, 4)
    ]
    row_panel = jnp.where(me_col == 0, panel_0, spread[0] + spread[1] + spread[2])
    piece = jnp.where(me_x == me_col, row_panel, sides[0] + sides[1] + sides[2])
    across = over_zk(piece, 2)
    pieces = [piece, over_zk(piece, 1), across, over_zk(across, 1)]

    front = assemble(krow, kcol, arrived, front_orig)
    return (finish(pos, front, row_panel, pieces), row_panel)


def solution(mesh):
    rows = ("hyp", "x", "z", "core")
    split = Mesh(mesh.devices.reshape(-1, 4, 2, 2, 4), rows + ("col",))
    in_specs = (P(rows, "col"), P(rows, "col"), P("hyp", None), P("hyp", None))
    out_specs = (P(rows, "col"), P(rows, None))
    return jax.shard_map(local, mesh=split, in_specs=in_specs, out_specs=out_specs, check_vma=False)
```

profile of v0, /device:TPU:47, one launch (start us, length us, event | category | flops | bytes accessed | tf_op | source)
XLA Modules:
  0.0 252.1 jit_solution(14591690864097812530)
XLA Ops:
  0.6 0.8 collective-permute-start
  1.4 0.6 pad_add_fusion.pos_ref
  2.0 5.0 %tables.1 = (s32[32]{0:T(128)}, s32[32]{0:T(128)}, s32[48]{0:T(128)}, s32[16]{0:T(128)}, s32[48]{0:T(128)}) custom-call(s32[2,64]{1,0:T(2,128)} %map_ref.1, s32[2]{0:T(128)} %pad_add_fusion.pos_ref), custom_call_target="tpu_custom_call" | custom-call | tf_op jit(solution)/shard_map/tables/pallas_call | solution.py:89
  7.0 1.6 collective-permute-done.other_ref
  8.5 2.9 %shard_map.59 = bf16[16,64,512]{2,1,0:T(8,128)(2,1)} custom-call(s32[32]{0:T(128)} %get-tuple-element.26.sel_ref, s32[32]{0:T(128)} %get-tuple-element.27.jsel_ref, s32[2]{0:T(128)} %pad_add_fusion.pos_ref, bf16[1024,2048]{1,0:T(8,128)(2,1)} %own_ref.7, bf16[1024,2048]{1,0:T(8,128)(2,1)} %collective-permute-done.other_ref), custom_call_target="tpu_custom_call" | custom-call | tf_op jit(solution)/shard_map/pallas_call | solution.py:126
  11.4 6.8 %all-to-all-start = ((bf16[16,64,512]{2,1,0:T(8,128)(2,1)}), bf16[16,64,512]{2,1,0:T(8,128)(2,1)}, u32[]{:S(2)}, u32[]{:S(2)}) async-start(bf16[16,64,512]{2,1,0:T(8,128)(2,1)} %shard_map.59), calls=%async_computation | async-start | bytes 2097152 | tf_op jit(solution)/shard_map/all_to_all | solution.py:327
  18.2 2.9 %shard_map.61 = bf16[16,64,512]{2,1,0:T(8,128)(2,1)} custom-call(s32[32]{0:T(128)} %get-tuple-element.26.sel_ref, s32[32]{0:T(128)} %get-tuple-element.27.jsel_ref, s32[2]{0:T(128)} %pad_add_fusion.pos_ref, bf16[1024,2048]{1,0:T(8,128)(2,1)} %own_ref.7, bf16[1024,2048]{1,0:T(8,128)(2,1)} %collective-permute-done.other_ref), custom_call_target="tpu_custom_call" | custom-call | tf_op jit(solution)/shard_map/pallas_call | solution.py:126
  21.1 10.8 %all-to-all-done.in_ref = bf16[16,64,512]{2,1,0:T(8,128)(2,1)} async-done(((bf16[16,64,512]{2,1,0:T(8,128)(2,1)}), bf16[16,64,512]{2,1,0:T(8,128)(2,1)}, u32[]{:S(2)}, u32[]{:S(2)}) %all-to-all-start) | async-done | bytes 1048608 | tf_op jit(solution)/shard_map/all_to_all | solution.py:327
  31.9 6.6 %all-to-all-start.1 = ((bf16[16,64,512]{2,1,0:T(8,128)(2,1)}), bf16[16,64,512]{2,1,0:T(8,128)(2,1)}, u32[]{:S(2)}, u32[]{:S(2)}) async-start(bf16[16,64,512]{2,1,0:T(8,128)(2,1)} %shard_map.61), calls=%async_computation.1 | async-start | bytes 2097152 | tf_op jit(solution)/shard_map/all_to_all | solution.py:327
  38.5 2.9 %shard_map.65 = bf16[16,64,512]{2,1,0:T(8,128)(2,1)} custom-call(s32[32]{0:T(128)} %get-tuple-element.26.sel_ref, s32[32]{0:T(128)} %get-tuple-element.27.jsel_ref, s32[2]{0:T(128)} %pad_add_fusion.pos_ref, bf16[1024,2048]{1,0:T(8,128)(2,1)} %own_ref.7, bf16[1024,2048]{1,0:T(8,128)(2,1)} %collective-permute-done.other_ref), custom_call_target="tpu_custom_call" | custom-call | tf_op jit(solution)/shard_map/pallas_call | solution.py:126
  41.4 9.4 %all-to-all-done.1.in_ref = bf16[16,64,512]{2,1,0:T(8,128)(2,1)} async-done(((bf16[16,64,512]{2,1,0:T(8,128)(2,1)}), bf16[16,64,512]{2,1,0:T(8,128)(2,1)}, u32[]{:S(2)}, u32[]{:S(2)}) %all-to-all-start.1) | async-done | bytes 1048608 | tf_op jit(solution)/shard_map/all_to_all | solution.py:327
  50.8 7.4 %all-to-all-start.3 = ((bf16[16,64,512]{2,1,0:T(8,128)(2,1)}), bf16[16,64,512]{2,1,0:T(8,128)(2,1)}, u32[]{:S(2)}, u32[]{:S(2)}) async-start(bf16[16,64,512]{2,1,0:T(8,128)(2,1)} %shard_map.65), calls=%async_computation.3 | async-start | bytes 2097152 | tf_op jit(solution)/shard_map/all_to_all | solution.py:327
  58.2 2.8 %shard_map.62 = (bf16[4,64,512]{2,1,0:T(8,128)(2,1)}, bf16[4,64,512]{2,1,0:T(8,128)(2,1)}, bf16[4,64,512]{2,1,0:T(8,128)(2,1)}, bf16[4,64,512]{2,1,0:T(8,128)(2,1)}) custom-call(s32[48]{0:T(128)} %get-tuple-element.25.jl_ref, s32[2]{0:T(128)} %pad_add_fusion.pos_ref, bf16[16,64,512]{2,1,0:T(8,128)(2,1)} %all-to-all-done.1.in_ref), custom_call_target="tpu_custom_call" | custom-call | tf_op jit(solution)/shard_map/pallas_call | solution.py:150
  61.0 2.9 %collective-permute-start.4 = (bf16[4,64,512]{2,1,0:T(8,128)(2,1)}, bf16[4,64,512]{2,1,0:T(8,128)(2,1)S(1)}, u32[]{:S(2)}, u32[]{:S(2)}) collective-permute-start(bf16[4,64,512]{2,1,0:T(8,128)(2,1)} %get-tuple-element.33), channel_id=1, source_target_pairs={{0,4},{4,0},{8,12},{12,8},{1,5},{5,1},{9,13},{13,9},{2,6},{6,2},{1... | collective-permute-start | bytes 786440 | tf_op jit(solution)/shard_map/ppermute | solution.py:312
  63.9 6.0 %collective-permute-start.5 = (bf16[4,64,512]{2,1,0:T(8,128)(2,1)}, bf16[4,64,512]{2,1,0:T(8,128)(2,1)S(1)}, u32[]{:S(2)}, u32[]{:S(2)}) collective-permute-start(bf16[4,64,512]{2,1,0:T(8,128)(2,1)} %get-tuple-element.34), channel_id=1, source_target_pairs={{0,8},{4,12},{8,0},{12,4},{1,9},{5,13},{9,1},{13,5},{2,10},{6,14},... | collective-permute-start | bytes 786440 | tf_op jit(solution)/shard_map/ppermute | solution.py:312
  70.0 0.0 collective-permute-start.6
  70.0 2.8 %shard_map.60 = (bf16[4,64,512]{2,1,0:T(8,128)(2,1)}, bf16[4,64,512]{2,1,0:T(8,128)(2,1)}, bf16[4,64,512]{2,1,0:T(8,128)(2,1)}, bf16[4,64,512]{2,1,0:T(8,128)(2,1)}) custom-call(s32[48]{0:T(128)} %get-tuple-element.25.jl_ref, s32[2]{0:T(128)} %pad_add_fusion.pos_ref, bf16[16,64,512]{2,1,0:T(8,128)(2,1)} %all-to-all-done.in_ref), custom_call_target="tpu_custom_call" | custom-call | tf_op jit(solution)/shard_map/pallas_call | solution.py:150
  72.7 0.4 collective-permute-start.1
  73.1 5.4 %collective-permute-start.2 = (bf16[4,64,512]{2,1,0:T(8,128)(2,1)}, bf16[4,64,512]{2,1,0:T(8,128)(2,1)}, u32[]{:S(2)}, u32[]{:S(2)}) collective-permute-start(bf16[4,64,512]{2,1,0:T(8,128)(2,1)} %get-tuple-element.30), channel_id=1, source_target_pairs={{0,8},{4,12},{8,0},{12,4},{1,9},{5,13},{9,1},{13,5},{2,10},{6,14},... | collective-permute-start | bytes 786440 | tf_op jit(solution)/shard_map/ppermute | solution.py:312
  78.5 0.3 collective-permute-start.3
  78.8 4.4 %collective-permute-done.5.refs_6_ = bf16[4,64,512]{2,1,0:T(8,128)(2,1)S(1)} collective-permute-done((bf16[4,64,512]{2,1,0:T(8,128)(2,1)}, bf16[4,64,512]{2,1,0:T(8,128)(2,1)S(1)}, u32[]{:S(2)}, u32[]{:S(2)}) %collective-permute-start.5) | collective-permute-done | bytes 262176 | tf_op jit(solution)/shard_map/ppermute | solution.py:312
  83.2 14.9 %collective-permute-done.6.refs_7_ = bf16[4,64,512]{2,1,0:T(8,128)(2,1)S(1)} collective-permute-done((bf16[4,64,512]{2,1,0:T(8,128)(2,1)}, bf16[4,64,512]{2,1,0:T(8,128)(2,1)S(1)}, u32[]{:S(2)}, u32[]{:S(2)}) %collective-permute-start.6) | collective-permute-done | bytes 262176 | tf_op jit(solution)/shard_map/ppermute | solution.py:312
  98.2 0.0 collective-permute-done.1.refs_1_
  98.2 11.3 %collective-permute-done.2.refs_2_ = bf16[4,64,512]{2,1,0:T(8,128)(2,1)} collective-permute-done((bf16[4,64,512]{2,1,0:T(8,128)(2,1)}, bf16[4,64,512]{2,1,0:T(8,128)(2,1)}, u32[]{:S(2)}, u32[]{:S(2)}) %collective-permute-start.2) | collective-permute-done | bytes 262176 | tf_op jit(solution)/shard_map/ppermute | solution.py:312
  109.5 6.9 %collective-permute-done.3.refs_3_ = bf16[4,64,512]{2,1,0:T(8,128)(2,1)} collective-permute-done((bf16[4,64,512]{2,1,0:T(8,128)(2,1)}, bf16[4,64,512]{2,1,0:T(8,128)(2,1)}, u32[]{:S(2)}, u32[]{:S(2)}) %collective-permute-start.3) | collective-permute-done | bytes 262176 | tf_op jit(solution)/shard_map/ppermute | solution.py:312
  116.4 4.3 %strip_panel.1 = bf16[640,256]{1,0:T(8,128)(2,1)} custom-call(s32[16]{0:T(128)} %get-tuple-element.23.krow_ref, s32[48]{0:T(128)} %get-tuple-element.24.kcol_ref, bf16[4,64,512]{2,1,0:T(8,128)(2,1)} %get-tuple-element.28.refs_0_, bf16[4,64,512]{2,1,0:T(8,128)(2,1)} %collective-permute-done.1.refs_1_, bf16[4,64,512]{2,1,0:T(8,128)(2,1)} %collective-permute-done.2.refs_2_, ...), custom_call_target="tpu_custom_call" | custom-call | tf_op jit(solution)/shard_map/strip_panel/pallas_call | solution.py:224
  120.7 0.0 copy-start.1
  120.7 0.8 collective-permute-start.18
  121.5 1.3 collective-permute-start.17
  122.8 1.4 collective-permute-start.16
  124.2 1.4 collective-permute-start.15
  125.6 1.4 collective-permute-start.14
  127.0 0.0 collective-permute-done.18
  127.0 1.3 collective-permute-start.13
  128.3 2.9 %shard_map.63 = bf16[16,64,512]{2,1,0:T(8,128)(2,1)} custom-call(s32[32]{0:T(128)} %get-tuple-element.26.sel_ref, s32[32]{0:T(128)} %get-tuple-element.27.jsel_ref, s32[2]{0:T(128)} %pad_add_fusion.pos_ref, bf16[1024,2048]{1,0:T(8,128)(2,1)} %own_ref.7, bf16[1024,2048]{1,0:T(8,128)(2,1)} %collective-permute-done.other_ref), custom_call_target="tpu_custom_call" | custom-call | tf_op jit(solution)/shard_map/pallas_call | solution.py:126
  131.2 0.0 all-to-all-done.3.in_ref
  131.2 14.2 %all-to-all-start.2 = ((bf16[16,64,512]{2,1,0:T(8,128)(2,1)}), bf16[16,64,512]{2,1,0:T(8,128)(2,1)}, u32[]{:S(2)}, u32[]{:S(2)}) async-start(bf16[16,64,512]{2,1,0:T(8,128)(2,1)} %shard_map.63), calls=%async_computation.2 | async-start | bytes 2097152 | tf_op jit(solution)/shard_map/all_to_all | solution.py:327
  145.4 0.0 collective-permute-done.16
  145.4 0.0 collective-permute-done.15
  145.5 0.7 copy-done.7
  146.2 23.7 %collective-permute-done.13 = bf16[640,256]{1,0:T(8,128)(2,1)} collective-permute-done((bf16[640,256]{1,0:T(8,128)(2,1)}, bf16[640,256]{1,0:T(8,128)(2,1)}, u32[]{:S(2)}, u32[]{:S(2)}) %collective-permute-start.13) | collective-permute-done | bytes 327712 | tf_op jit(solution)/shard_map/ppermute | solution.py:308
  169.9 2.2 add_select_fusion
  172.1 6.3 %collective-permute-start.20 = (bf16[640,256]{1,0:T(8,128)(2,1)S(1)}, bf16[640,256]{1,0:T(8,128)(2,1)S(1)}, u32[]{:S(2)}, u32[]{:S(2)}) collective-permute-start(bf16[640,256]{1,0:T(8,128)(2,1)S(1)} %get-tuple-element.44.p0), channel_id=1, source_target_pairs={{0,8},{4,12},{8,0},{12,4},{1,9},{5,13},{9,1},{13,5},{2,10},{6,14},... | collective-permute-start | bytes 983048 | tf_op jit(solution)/shard_map/ppermute | solution.py:312
  178.4 2.8 %shard_map.66 = (bf16[4,64,512]{2,1,0:T(8,128)(2,1)}, bf16[4,64,512]{2,1,0:T(8,128)(2,1)}, bf16[4,64,512]{2,1,0:T(8,128)(2,1)}, bf16[4,64,512]{2,1,0:T(8,128)(2,1)}) custom-call(s32[48]{0:T(128)} %get-tuple-element.25.jl_ref, s32[2]{0:T(128)} %pad_add_fusion.pos_ref, bf16[16,64,512]{2,1,0:T(8,128)(2,1)} %all-to-all-done.3.in_ref), custom_call_target="tpu_custom_call" | custom-call | tf_op jit(solution)/shard_map/pallas_call | solution.py:150
  181.2 1.4 collective-permute-start.10
  182.6 0.0 collective-permute-start.11
  182.6 5.6 %collective-permute-start.12 = (bf16[4,64,512]{2,1,0:T(8,128)(2,1)}, bf16[4,64,512]{2,1,0:T(8,128)(2,1)}, u32[]{:S(2)}, u32[]{:S(2)}) collective-permute-start(bf16[4,64,512]{2,1,0:T(8,128)(2,1)} %get-tuple-element.43), channel_id=1, source_target_pairs={{0,12},{4,8},{8,4},{12,0},{1,13},{5,9},{9,5},{13,1},{2,14},{6,10},... | collective-permute-start | bytes 786440 | tf_op jit(solution)/shard_map/ppermute | solution.py:312
  188.3 0.1 collective-permute-start.19
  188.4 9.0 %collective-permute-done.20.p2 = bf16[640,256]{1,0:T(8,128)(2,1)S(1)} collective-permute-done((bf16[640,256]{1,0:T(8,128)(2,1)S(1)}, bf16[640,256]{1,0:T(8,128)(2,1)S(1)}, u32[]{:S(2)}, u32[]{:S(2)}) %collective-permute-start.20) | collective-permute-done | bytes 327712 | tf_op jit(solution)/shard_map/ppermute | solution.py:312
  197.4 0.7 collective-permute-start.21
  198.1 0.0 all-to-all-done.2.in_ref
  198.1 2.8 %shard_map.64 = (bf16[4,64,512]{2,1,0:T(8,128)(2,1)}, bf16[4,64,512]{2,1,0:T(8,128)(2,1)}, bf16[4,64,512]{2,1,0:T(8,128)(2,1)}, bf16[4,64,512]{2,1,0:T(8,128)(2,1)}) custom-call(s32[48]{0:T(128)} %get-tuple-element.25.jl_ref, s32[2]{0:T(128)} %pad_add_fusion.pos_ref, bf16[16,64,512]{2,1,0:T(8,128)(2,1)} %all-to-all-done.2.in_ref), custom_call_target="tpu_custom_call" | custom-call | tf_op jit(solution)/shard_map/pallas_call | solution.py:150
  200.9 0.0 collective-permute-done.10.refs_13_
  200.9 0.1 collective-permute-start.7
  201.0 8.0 %collective-permute-done.11.refs_14_ = bf16[4,64,512]{2,1,0:T(8,128)(2,1)} collective-permute-done((bf16[4,64,512]{2,1,0:T(8,128)(2,1)}, bf16[4,64,512]{2,1,0:T(8,128)(2,1)}, u32[]{:S(2)}, u32[]{:S(2)}) %collective-permute-start.11) | collective-permute-done | bytes 262176 | tf_op jit(solution)/shard_map/ppermute | solution.py:312
  209.0 5.1 %collective-permute-start.8 = (bf16[4,64,512]{2,1,0:T(8,128)(2,1)}, bf16[4,64,512]{2,1,0:T(8,128)(2,1)}, u32[]{:S(2)}, u32[]{:S(2)}) collective-permute-start(bf16[4,64,512]{2,1,0:T(8,128)(2,1)} %get-tuple-element.38), channel_id=1, source_target_pairs={{0,8},{4,12},{8,0},{12,4},{1,9},{5,13},{9,1},{13,5},{2,10},{6,14},... | collective-permute-start | bytes 786440 | tf_op jit(solution)/shard_map/ppermute | solution.py:312
  214.1 7.9 %collective-permute-done.12.refs_15_ = bf16[4,64,512]{2,1,0:T(8,128)(2,1)} collective-permute-done((bf16[4,64,512]{2,1,0:T(8,128)(2,1)}, bf16[4,64,512]{2,1,0:T(8,128)(2,1)}, u32[]{:S(2)}, u32[]{:S(2)}) %collective-permute-start.12) | collective-permute-done | bytes 262176 | tf_op jit(solution)/shard_map/ppermute | solution.py:312
  222.1 4.6 %collective-permute-start.9 = (bf16[4,64,512]{2,1,0:T(8,128)(2,1)}, bf16[4,64,512]{2,1,0:T(8,128)(2,1)}, u32[]{:S(2)}, u32[]{:S(2)}) collective-permute-start(bf16[4,64,512]{2,1,0:T(8,128)(2,1)} %get-tuple-element.39), channel_id=1, source_target_pairs={{0,12},{4,8},{8,4},{12,0},{1,13},{5,9},{9,5},{13,1},{2,14},{6,10},... | collective-permute-start | bytes 786440 | tf_op jit(solution)/shard_map/ppermute | solution.py:312
  226.6 0.0 collective-permute-done.7.refs_9_
  226.7 1.1 collective-permute-done.8.refs_10_
  227.7 7.1 %collective-permute-done.9.refs_11_ = bf16[4,64,512]{2,1,0:T(8,128)(2,1)} collective-permute-done((bf16[4,64,512]{2,1,0:T(8,128)(2,1)}, bf16[4,64,512]{2,1,0:T(8,128)(2,1)}, u32[]{:S(2)}, u32[]{:S(2)}) %collective-permute-start.9) | collective-permute-done | bytes 262176 | tf_op jit(solution)/shard_map/ppermute | solution.py:312
  234.8 11.2 %assemble.1.front_ref = bf16[640,2560]{1,0:T(8,128)(2,1)} custom-call(s32[16]{0:T(128)} %get-tuple-element.23.krow_ref, s32[48]{0:T(128)} %get-tuple-element.24.kcol_ref, bf16[4,64,512]{2,1,0:T(8,128)(2,1)} %get-tuple-element.28.refs_0_, bf16[4,64,512]{2,1,0:T(8,128)(2,1)} %collective-permute-done.1.refs_1_, ...), custom_call_target="tpu_custom_call" | custom-call | tf_op jit(solution)/shard_map/assemble/pallas_call | solution.py:263
  246.0 0.7 copy-done.6
  246.7 5.4 %finish.1 = bf16[640,2560]{1,0:T(8,128)(2,1)} custom-call(s32[2]{0:T(128)} %pad_add_fusion.pos_ref, bf16[640,2560]{1,0:T(8,128)(2,1)} %assemble.1.front_ref, bf16[640,256]{1,0:T(8,128)(2,1)} %get-tuple-element.45.row_ref, bf16[640,256]{1,0:T(8,128)(2,1)} %copy-done, bf16[640,256]{1,0:T(8,128)(2,1)} %copy-done.6, bf16[640,256]{1,0:T(8,128)(2,1)} %copy-done.5, ...), custom_call_target="tpu_custom_call" | custom-call | tf_op jit(solution)/shard_map/finish/pallas_call | solution.py:293
  (18 shorter events, 0.0 us)
Async XLA Ops:
  0.6 7.9 %collective-permute-start = (bf16[1024,2048]{1,0:T(8,128)(2,1)}, bf16[1024,2048]{1,0:T(8,128)(2,1)}, u32[]{:S(2)}, u32[]{:S(2)}) collective-permute-start(bf16[1024,2048]{1,0:T(8,128)(2,1)} %own_ref.7), channel_id=1, source_target_pairs={{0,4},{4,0},{8,12},{12,8},{1,5},{5,1},{9,13},{13,9},{2,6},{6,2},{1... | collective-permute-start | bytes 12582920 | tf_op jit(solution)/shard_map/ppermute | solution.py:312
  11.4 20.5 %all-to-all-start = ((bf16[16,64,512]{2,1,0:T(8,128)(2,1)}), bf16[16,64,512]{2,1,0:T(8,128)(2,1)}, u32[]{:S(2)}, u32[]{:S(2)}) async-start(bf16[16,64,512]{2,1,0:T(8,128)(2,1)} %shard_map.59), calls=%async_computation | async-start | bytes 2097152 | tf_op jit(solution)/shard_map/all_to_all | solution.py:327
  31.9 18.9 %all-to-all-start.1 = ((bf16[16,64,512]{2,1,0:T(8,128)(2,1)}), bf16[16,64,512]{2,1,0:T(8,128)(2,1)}, u32[]{:S(2)}, u32[]{:S(2)}) async-start(bf16[16,64,512]{2,1,0:T(8,128)(2,1)} %shard_map.61), calls=%async_computation.1 | async-start | bytes 2097152 | tf_op jit(solution)/shard_map/all_to_all | solution.py:327
  50.8 80.4 %all-to-all-start.3 = ((bf16[16,64,512]{2,1,0:T(8,128)(2,1)}), bf16[16,64,512]{2,1,0:T(8,128)(2,1)}, u32[]{:S(2)}, u32[]{:S(2)}) async-start(bf16[16,64,512]{2,1,0:T(8,128)(2,1)} %shard_map.65), calls=%async_computation.3 | async-start | bytes 2097152 | tf_op jit(solution)/shard_map/all_to_all | solution.py:327
  61.0 17.5 %collective-permute-start.4 = (bf16[4,64,512]{2,1,0:T(8,128)(2,1)}, bf16[4,64,512]{2,1,0:T(8,128)(2,1)S(1)}, u32[]{:S(2)}, u32[]{:S(2)}) collective-permute-start(bf16[4,64,512]{2,1,0:T(8,128)(2,1)} %get-tuple-element.33), channel_id=1, source_target_pairs={{0,4},{4,0},{8,12},{12,8},{1,5},{5,1},{9,13},{13,9},{2,6},{6,2},{1... | collective-permute-start | bytes 786440 | tf_op jit(solution)/shard_map/ppermute | solution.py:312
  63.9 19.3 %collective-permute-start.5 = (bf16[4,64,512]{2,1,0:T(8,128)(2,1)}, bf16[4,64,512]{2,1,0:T(8,128)(2,1)S(1)}, u32[]{:S(2)}, u32[]{:S(2)}) collective-permute-start(bf16[4,64,512]{2,1,0:T(8,128)(2,1)} %get-tuple-element.34), channel_id=1, source_target_pairs={{0,8},{4,12},{8,0},{12,4},{1,9},{5,13},{9,1},{13,5},{2,10},{6,14},... | collective-permute-start | bytes 786440 | tf_op jit(solution)/shard_map/ppermute | solution.py:312
  70.0 28.2 %collective-permute-start.6 = (bf16[4,64,512]{2,1,0:T(8,128)(2,1)}, bf16[4,64,512]{2,1,0:T(8,128)(2,1)S(1)}, u32[]{:S(2)}, u32[]{:S(2)}) collective-permute-start(bf16[4,64,512]{2,1,0:T(8,128)(2,1)} %get-tuple-element.35), channel_id=1, source_target_pairs={{0,12},{4,8},{8,4},{12,0},{1,13},{5,9},{9,5},{13,1},{2,14},{6,10},... | collective-permute-start | bytes 786440 | tf_op jit(solution)/shard_map/ppermute | solution.py:312
  72.7 25.4 %collective-permute-start.1 = (bf16[4,64,512]{2,1,0:T(8,128)(2,1)}, bf16[4,64,512]{2,1,0:T(8,128)(2,1)}, u32[]{:S(2)}, u32[]{:S(2)}) collective-permute-start(bf16[4,64,512]{2,1,0:T(8,128)(2,1)} %get-tuple-element.29), channel_id=1, source_target_pairs={{0,4},{4,0},{8,12},{12,8},{1,5},{5,1},{9,13},{13,9},{2,6},{6,2},{1... | collective-permute-start | bytes 786440 | tf_op jit(solution)/shard_map/ppermute | solution.py:312
  73.1 36.4 %collective-permute-start.2 = (bf16[4,64,512]{2,1,0:T(8,128)(2,1)}, bf16[4,64,512]{2,1,0:T(8,128)(2,1)}, u32[]{:S(2)}, u32[]{:S(2)}) collective-permute-start(bf16[4,64,512]{2,1,0:T(8,128)(2,1)} %get-tuple-element.30), channel_id=1, source_target_pairs={{0,8},{4,12},{8,0},{12,4},{1,9},{5,13},{9,1},{13,5},{2,10},{6,14},... | collective-permute-start | bytes 786440 | tf_op jit(solution)/shard_map/ppermute | solution.py:312
  78.5 37.9 %copy-start.2 = (bf16[4,64,512]{2,1,0:T(8,128)(2,1)}, bf16[4,64,512]{2,1,0:T(8,128)(2,1)S(1)}, u32[]{:S(2)}) copy-start(bf16[4,64,512]{2,1,0:T(8,128)(2,1)S(1)} %collective-permute-done.4.refs_5_) | copy-start | bytes 786436
  78.5 37.9 %collective-permute-start.3 = (bf16[4,64,512]{2,1,0:T(8,128)(2,1)}, bf16[4,64,512]{2,1,0:T(8,128)(2,1)}, u32[]{:S(2)}, u32[]{:S(2)}) collective-permute-start(bf16[4,64,512]{2,1,0:T(8,128)(2,1)} %get-tuple-element.31), channel_id=1, source_target_pairs={{0,12},{4,8},{8,4},{12,0},{1,13},{5,9},{9,5},{13,1},{2,14},{6,10},... | collective-permute-start | bytes 786440 | tf_op jit(solution)/shard_map/ppermute | solution.py:312
  83.2 33.2 %copy-start.3 = (bf16[4,64,512]{2,1,0:T(8,128)(2,1)}, bf16[4,64,512]{2,1,0:T(8,128)(2,1)S(1)}, u32[]{:S(2)}) copy-start(bf16[4,64,512]{2,1,0:T(8,128)(2,1)S(1)} %collective-permute-done.5.refs_6_) | copy-start | bytes 786436
  98.2 18.2 %copy-start.4 = (bf16[4,64,512]{2,1,0:T(8,128)(2,1)}, bf16[4,64,512]{2,1,0:T(8,128)(2,1)S(1)}, u32[]{:S(2)}) copy-start(bf16[4,64,512]{2,1,0:T(8,128)(2,1)S(1)} %collective-permute-done.6.refs_7_) | copy-start | bytes 786436
  120.7 49.2 %copy-start.1 = (bf16[640,256]{1,0:T(8,128)(2,1)S(1)}, bf16[640,256]{1,0:T(8,128)(2,1)}, u32[]{:S(2)}) copy-start(bf16[640,256]{1,0:T(8,128)(2,1)} %strip_panel.1) | copy-start | bytes 983044
  120.7 6.3 %collective-permute-start.18 = (bf16[640,256]{1,0:T(8,128)(2,1)}, bf16[640,256]{1,0:T(8,128)(2,1)S(1)}, u32[]{:S(2)}, u32[]{:S(2)}) collective-permute-start(bf16[640,256]{1,0:T(8,128)(2,1)} %strip_panel.1), channel_id=1, source_target_pairs={{0,48},{4,52},{8,56},{12,60},{16,1},{20,5},{24,9},{28,13},{32,18},... | collective-permute-start | bytes 983048 | tf_op jit(solution)/shard_map/ppermute | solution.py:308
  121.5 23.9 %collective-permute-start.17 = (bf16[640,256]{1,0:T(8,128)(2,1)}, bf16[640,256]{1,0:T(8,128)(2,1)S(1)}, u32[]{:S(2)}, u32[]{:S(2)}) collective-permute-start(bf16[640,256]{1,0:T(8,128)(2,1)} %strip_panel.1), channel_id=1, source_target_pairs={{0,32},{4,36},{8,40},{12,44},{16,49},{20,53},{24,57},{28,61},{32,2... | collective-permute-start | bytes 983048 | tf_op jit(solution)/shard_map/ppermute | solution.py:308
  122.8 22.6 %collective-permute-start.16 = (bf16[640,256]{1,0:T(8,128)(2,1)}, bf16[640,256]{1,0:T(8,128)(2,1)}, u32[]{:S(2)}, u32[]{:S(2)}) collective-permute-start(bf16[640,256]{1,0:T(8,128)(2,1)} %strip_panel.1), channel_id=1, source_target_pairs={{0,16},{4,20},{8,24},{12,28},{16,33},{20,37},{24,41},{28,45},{32,5... | collective-permute-start | bytes 983048 | tf_op jit(solution)/shard_map/ppermute | solution.py:308
  124.2 21.2 %collective-permute-start.15 = (bf16[640,256]{1,0:T(8,128)(2,1)}, bf16[640,256]{1,0:T(8,128)(2,1)}, u32[]{:S(2)}, u32[]{:S(2)}) collective-permute-start(bf16[640,256]{1,0:T(8,128)(2,1)} %strip_panel.1), channel_id=1, source_target_pairs={{0,3},{4,7},{8,11},{12,15},{16,19},{20,23},{24,27},{28,31},{32,35}... | collective-permute-start | bytes 983048 | tf_op jit(solution)/shard_map/ppermute | solution.py:308
  125.6 19.9 %collective-permute-start.14 = (bf16[640,256]{1,0:T(8,128)(2,1)}, bf16[640,256]{1,0:T(8,128)(2,1)}, u32[]{:S(2)}, u32[]{:S(2)}) collective-permute-start(bf16[640,256]{1,0:T(8,128)(2,1)} %strip_panel.1), channel_id=1, source_target_pairs={{0,2},{4,6},{8,10},{12,14},{16,18},{20,22},{24,26},{28,30},{32,34}... | collective-permute-start | bytes 983048 | tf_op jit(solution)/shard_map/ppermute | solution.py:308
  127.0 42.9 %collective-permute-start.13 = (bf16[640,256]{1,0:T(8,128)(2,1)}, bf16[640,256]{1,0:T(8,128)(2,1)}, u32[]{:S(2)}, u32[]{:S(2)}) collective-permute-start(bf16[640,256]{1,0:T(8,128)(2,1)} %strip_panel.1), channel_id=1, source_target_pairs={{0,1},{4,5},{8,9},{12,13},{16,17},{20,21},{24,25},{28,29},{32,33},... | collective-permute-start | bytes 983048 | tf_op jit(solution)/shard_map/ppermute | solution.py:308
  131.2 66.9 %all-to-all-start.2 = ((bf16[16,64,512]{2,1,0:T(8,128)(2,1)}), bf16[16,64,512]{2,1,0:T(8,128)(2,1)}, u32[]{:S(2)}, u32[]{:S(2)}) async-start(bf16[16,64,512]{2,1,0:T(8,128)(2,1)} %shard_map.63), calls=%async_computation.2 | async-start | bytes 2097152 | tf_op jit(solution)/shard_map/all_to_all | solution.py:327
  145.4 0.7 copy-start.7
  172.1 73.9 %copy-start = (bf16[640,256]{1,0:T(8,128)(2,1)}, bf16[640,256]{1,0:T(8,128)(2,1)S(1)}, u32[]{:S(2)}) copy-start(bf16[640,256]{1,0:T(8,128)(2,1)S(1)} %get-tuple-element.44.p0) | copy-start | bytes 983044
  172.1 25.3 %collective-permute-start.20 = (bf16[640,256]{1,0:T(8,128)(2,1)S(1)}, bf16[640,256]{1,0:T(8,128)(2,1)S(1)}, u32[]{:S(2)}, u32[]{:S(2)}) collective-permute-start(bf16[640,256]{1,0:T(8,128)(2,1)S(1)} %get-tuple-element.44.p0), channel_id=1, source_target_pairs={{0,8},{4,12},{8,0},{12,4},{1,9},{5,13},{9,1},{13,5},{2,10},{6,14},... | collective-permute-start | bytes 983048 | tf_op jit(solution)/shard_map/ppermute | solution.py:312
  181.2 19.7 %collective-permute-start.10 = (bf16[4,64,512]{2,1,0:T(8,128)(2,1)}, bf16[4,64,512]{2,1,0:T(8,128)(2,1)}, u32[]{:S(2)}, u32[]{:S(2)}) collective-permute-start(bf16[4,64,512]{2,1,0:T(8,128)(2,1)} %get-tuple-element.41), channel_id=1, source_target_pairs={{0,4},{4,0},{8,12},{12,8},{1,5},{5,1},{9,13},{13,9},{2,6},{6,2},{1... | collective-permute-start | bytes 786440 | tf_op jit(solution)/shard_map/ppermute | solution.py:312
  182.6 26.4 %collective-permute-start.11 = (bf16[4,64,512]{2,1,0:T(8,128)(2,1)}, bf16[4,64,512]{2,1,0:T(8,128)(2,1)}, u32[]{:S(2)}, u32[]{:S(2)}) collective-permute-start(bf16[4,64,512]{2,1,0:T(8,128)(2,1)} %get-tuple-element.42), channel_id=1, source_target_pairs={{0,8},{4,12},{8,0},{12,4},{1,9},{5,13},{9,1},{13,5},{2,10},{6,14},... | collective-permute-start | bytes 786440 | tf_op jit(solution)/shard_map/ppermute | solution.py:312
  182.6 39.4 %collective-permute-start.12 = (bf16[4,64,512]{2,1,0:T(8,128)(2,1)}, bf16[4,64,512]{2,1,0:T(8,128)(2,1)}, u32[]{:S(2)}, u32[]{:S(2)}) collective-permute-start(bf16[4,64,512]{2,1,0:T(8,128)(2,1)} %get-tuple-element.43), channel_id=1, source_target_pairs={{0,12},{4,8},{8,4},{12,0},{1,13},{5,9},{9,5},{13,1},{2,14},{6,10},... | collective-permute-start | bytes 786440 | tf_op jit(solution)/shard_map/ppermute | solution.py:312
  188.3 57.7 %collective-permute-start.19 = (bf16[640,256]{1,0:T(8,128)(2,1)S(1)}, bf16[640,256]{1,0:T(8,128)(2,1)S(1)}, u32[]{:S(2)}, u32[]{:S(2)}) collective-permute-start(bf16[640,256]{1,0:T(8,128)(2,1)S(1)} %get-tuple-element.44.p0), channel_id=1, source_target_pairs={{0,4},{4,0},{8,12},{12,8},{1,5},{5,1},{9,13},{13,9},{2,6},{6,2},{1... | collective-permute-start | bytes 983048 | tf_op jit(solution)/shard_map/ppermute | solution.py:312
  197.4 48.6 %copy-start.5 = (bf16[640,256]{1,0:T(8,128)(2,1)}, bf16[640,256]{1,0:T(8,128)(2,1)S(1)}, u32[]{:S(2)}) copy-start(bf16[640,256]{1,0:T(8,128)(2,1)S(1)} %collective-permute-done.20.p2) | copy-start | bytes 983044
  197.4 48.6 %collective-permute-start.21 = (bf16[640,256]{1,0:T(8,128)(2,1)S(1)}, bf16[640,256]{1,0:T(8,128)(2,1)}, u32[]{:S(2)}, u32[]{:S(2)}) collective-permute-start(bf16[640,256]{1,0:T(8,128)(2,1)S(1)} %collective-permute-done.20.p2), channel_id=1, source_target_pairs={{0,4},{4,0},{8,12},{12,8},{1,5},{5,1},{9,13},{13,9},{2,6},{6,2},{1... | collective-permute-start | bytes 983048 | tf_op jit(solution)/shard_map/ppermute | solution.py:312
  200.9 25.8 %collective-permute-start.7 = (bf16[4,64,512]{2,1,0:T(8,128)(2,1)}, bf16[4,64,512]{2,1,0:T(8,128)(2,1)}, u32[]{:S(2)}, u32[]{:S(2)}) collective-permute-start(bf16[4,64,512]{2,1,0:T(8,128)(2,1)} %get-tuple-element.37), channel_id=1, source_target_pairs={{0,4},{4,0},{8,12},{12,8},{1,5},{5,1},{9,13},{13,9},{2,6},{6,2},{1... | collective-permute-start | bytes 786440 | tf_op jit(solution)/shard_map/ppermute | solution.py:312
  209.0 18.7 %collective-permute-start.8 = (bf16[4,64,512]{2,1,0:T(8,128)(2,1)}, bf16[4,64,512]{2,1,0:T(8,128)(2,1)}, u32[]{:S(2)}, u32[]{:S(2)}) collective-permute-start(bf16[4,64,512]{2,1,0:T(8,128)(2,1)} %get-tuple-element.38), channel_id=1, source_target_pairs={{0,8},{4,12},{8,0},{12,4},{1,9},{5,13},{9,1},{13,5},{2,10},{6,14},... | collective-permute-start | bytes 786440 | tf_op jit(solution)/shard_map/ppermute | solution.py:312
  222.1 12.7 %collective-permute-start.9 = (bf16[4,64,512]{2,1,0:T(8,128)(2,1)}, bf16[4,64,512]{2,1,0:T(8,128)(2,1)}, u32[]{:S(2)}, u32[]{:S(2)}) collective-permute-start(bf16[4,64,512]{2,1,0:T(8,128)(2,1)} %get-tuple-element.39), channel_id=1, source_target_pairs={{0,12},{4,8},{8,4},{12,0},{1,13},{5,9},{9,5},{13,1},{2,14},{6,10},... | collective-permute-start | bytes 786440 | tf_op jit(solution)/shard_map/ppermute | solution.py:312
  246.0 0.7 copy-start.6
where the time goes:
time: 253 us; the launch traced here: 252 us
  waiting for transfers between devices  116 us (46%)
  starting transfers between devices  82.4 us (33%)
  Pallas kernels  48.6 us (19%)
  other arithmetic  2.77 us (1%)
    ppermute x16, waiting for transfers between devices, over_zk(): return lax.ppermute(array, ('z', 'core'), [(r, r ^ d) for r in range(4)])  72.2 us
    ppermute x16, starting transfers between devices, over_zk(): return lax.ppermute(array, ('z', 'core'), [(r, r ^ d) for r in range(4)])  39.8 us
    all_to_all x4, starting transfers between devices, local(): part = lax.all_to_all(sent, ('x', 'col'), 0, 0, tiled=True)  35 us
    ppermute x6, waiting for transfers between devices, moved(): return lax.ppermute(array, ('x', 'z', 'core', 'col'), pairs)  23.8 us
    all_to_all x4, waiting for transfers between devices, local(): part = lax.all_to_all(sent, ('x', 'col'), 0, 0, tiled=True)  20.2 us
    pallas_call x4, Pallas kernels, pack_first(): pl.pallas_call(kernel, out_shape=jax.ShapeDtypeStruct((16, half, 4 * bloc...  11.6 us
    pallas_call x1, Pallas kernels, assemble(): pl.pallas_call(kernel, out_shape=jax.ShapeDtypeStruct(front_orig.shape, j...  11.2 us
    pallas_call x4, Pallas kernels, pack_second(): pl.pallas_call(kernel, out_shape=[jax.ShapeDtypeStruct((4,) + arrived.sha...  11.1 us
  transfers between devices with their start and end apart: 26, of which 13 were waited for; matrix products, arithmetic and copies ran while one was open for 1% of the time, Pallas kernels for 16%

commit v1 on v0

--- a/solution.py
+++ b/solution.py
@@ -12,6 +12,7 @@
 MB = 5
 QB = 20
 FB = 80
+CHUNKS = ((0, 0, 1), (0, 1, 2), (1, 0, 2))
 PLACES = [(x, z, core) for x in range(4) for z in range(2) for core in range(2)]
 
 
@@ -99,13 +100,13 @@
 
 def pack_first(sel, jsel, pos, own, other, chunk):
     block = own.shape[0] // 8
-    half = block // 2
+    turn, first, last = (n * block // 2 if i else n for i, n in enumerate(CHUNKS[chunk]))
 
     def kernel(sel_ref, jsel_ref, pos_ref, own_ref, other_ref, out_ref, sem):
         core = pos_ref[0] % 2
         for y in range(4):
-            index = sel_ref[y * 4 + 2 * (chunk // 2) + core]
-            rows = pl.ds(pl.multiple_of((index % 8) * block + (chunk % 2) * half, half), half)
+            index = sel_ref[y * 4 + 2 * turn + core]
+            rows = pl.ds(pl.multiple_of((index % 8) * block + first, block // 2), last - first)
             mine = index // 8 == core
 
             def copy(ref):
@@ -125,7 +126,7 @@
 
     return pl.pallas_call(
         kernel,
-        out_shape=jax.ShapeDtypeStruct((16, half, 4 * block), own.dtype),
+        out_shape=jax.ShapeDtypeStruct((16, last - first, 4 * block), own.dtype),
         in_specs=[pl.BlockSpec(memory_space=SMEM)] * 3 + [pl.BlockSpec(memory_space=pltpu.MemorySpace.HBM)] * 2,
         out_specs=pl.BlockSpec(memory_space=VMEM),
         scratch_shapes=[pltpu.SemaphoreType.DMA(())],
@@ -143,15 +144,17 @@
                 for k in range(4):
                     code = jl_ref[(xs // 2) * 16 + (zk ^ d) * 4 + k]
                     cols = pl.ds(pl.multiple_of((code % 4) * block, block), block)
-                    out_refs[d][xs, :, k * block : (k + 1) * block] = in_ref[
+                    out_refs[min(d, 2)][xs + 4 * (d == 3), :, k * block : (k + 1) * block] = in_ref[
                         xs * 4 + code // 4, :, cols
                     ]
 
     return pl.pallas_call(
         kernel,
-        out_shape=[jax.ShapeDtypeStruct((4,) + arrived.shape[1:], arrived.dtype)] * 4,
+        out_shape=[
+            jax.ShapeDtypeStruct((n,) + arrived.shape[1:], arrived.dtype) for n in (4, 4, 8)
+        ],
         in_specs=[pl.BlockSpec(memory_space=SMEM)] * 2 + [pl.BlockSpec(memory_space=VMEM)],
-        out_specs=[pl.BlockSpec(memory_space=VMEM)] * 4,
+        out_specs=[pl.BlockSpec(memory_space=VMEM)] * 3,
         compiler_params=params(63),
     )(jl, pos, arrived)
 
@@ -186,14 +189,13 @@
 
 def gather(refs, buf_ref, sem, meanwhile):
     half = buf_ref.shape[1] // 2
-    copies = [
-        pltpu.make_async_copy(
-            ref,
-            buf_ref.at[pl.ds((n // 8) * 16 + (n % 4) * 4, 4), pl.ds((n // 4 % 2) * half, half)],
-            sem.at[n],
-        )
-        for n, ref in enumerate(refs)
-    ]
+    copies = []
+    for n, ref in enumerate(refs):
+        turn, first, last = CHUNKS[n // 4]
+        d = n % 4
+        source = ref.at[pl.ds(4, 4)] if d == 3 else ref.at[pl.ds(0, 4)]
+        target = buf_ref.at[pl.ds(turn * 16 + d * 4, 4), pl.ds(first * half, (last - first) * half)]
+        copies.append(pltpu.make_async_copy(source, target, sem.at[n]))
     for copy in copies:
         copy.start()
     meanwhile()
@@ -244,33 +246,36 @@
 
 def assemble(krow, kcol, arrived, front_orig):
     block = arrived[0].shape[2] // 4
+    rows, cols = front_orig.shape
 
     def kernel(krow_ref, kcol_ref, *refs):
-        orig_ref, out_ref, buf_ref, eye_ref, sem = refs[16:]
-        gather(refs[:16], buf_ref, sem, lambda: fill_eyes(eye_ref))
-
-        def column(q, _):
-            cols = pl.ds(pl.multiple_of(q * block, block), block)
+        orig_ref, out_ref, buf_ref, eye_ref, sem = refs[12:]
+        step = pl.program_id(0)
+
+        @pl.when(step == 0)
+        def _():
+            gather(refs[:12], buf_ref, sem, lambda: fill_eyes(eye_ref))
+
+        for q in range(QB // 4):
+            side = slice(q * block, (q + 1) * block)
             for p in range(MB):
                 here = slice(p * block, (p + 1) * block)
-                out_ref[here, cols] = front_tile(
-                    orig_ref[here, cols], buf_ref, krow_ref, kcol_ref, eye_ref, p, q
+                out_ref[here, side] = front_tile(
+                    orig_ref[here, side], buf_ref, krow_ref, kcol_ref, eye_ref, p, step * (QB // 4) + q
                 )
-            return 0
-
-        lax.fori_loop(0, QB, column, 0)
-
-    return pl.pallas_call(
-        kernel,
+
+    return pl.pallas_call(
+        kernel,
+        grid=(4,),
         out_shape=jax.ShapeDtypeStruct(front_orig.shape, jnp.bfloat16),
         in_specs=[pl.BlockSpec(memory_space=SMEM)] * 2
-        + [pl.BlockSpec(memory_space=pl.ANY)] * 16
-        + [pl.BlockSpec(memory_space=VMEM)],
-        out_specs=pl.BlockSpec(memory_space=VMEM),
+        + [pl.BlockSpec(memory_space=pl.ANY)] * 12
+        + [pl.BlockSpec((rows, cols // 4), lambda i: (0, i))],
+        out_specs=pl.BlockSpec((rows, cols // 4), lambda i: (0, i)),
         scratch_shapes=[
             pltpu.VMEM((32, block, 4 * block), jnp.bfloat16),
             pltpu.VMEM((4, block, 2 * block), jnp.bfloat16),
-            pltpu.SemaphoreType.DMA((16,)),
+            pltpu.SemaphoreType.DMA((12,)),
         ],
         compiler_params=params(63),
         name="assemble",
@@ -278,23 +283,32 @@
 
 
 def finish(pos, front, row_panel, pieces):
-    _, cols = front.shape
+    rows, cols = front.shape
     wide = cols // 4
 
-    def kernel(pos_ref, front_ref, row_ref, p0, p1, p2, p3, out_ref):
-        zk = pos_ref[0] % 4
-        for w, ref in enumerate((p0, p1, p2, p3)):
-            here = pl.ds(pl.multiple_of((zk ^ w) * wide, wide), wide)
-            update = lax.dot_general(
-                row_ref[...], ref[...], (((1,), (1,)), ((), ())), preferred_element_type=jnp.float32
-            )
-            out_ref[:, here] = (front_ref[:, here].astype(jnp.float32) - update).astype(jnp.bfloat16)
-
-    return pl.pallas_call(
-        kernel,
+    def kernel(pos_ref, front_ref, row_ref, *refs):
+        out_ref = refs[4]
+        for w in range(4):
+
+            @pl.when(pl.program_id(0) == w)
+            def _():
+                update = lax.dot_general(
+                    row_ref[...], refs[w][...], (((1,), (1,)), ((), ())),
+                    preferred_element_type=jnp.float32,
+                )
+                out_ref[...] = (front_ref[...].astype(jnp.float32) - update).astype(jnp.bfloat16)
+
+    whole = pl.BlockSpec(row_panel.shape, lambda w, pos_ref: (0, 0))
+    turned = pl.BlockSpec((rows, wide), lambda w, pos_ref: (0, (pos_ref[0] % 4) ^ w))
+    return pl.pallas_call(
+        kernel,
+        grid_spec=pltpu.PrefetchScalarGridSpec(
+            num_scalar_prefetch=1,
+            grid=(4,),
+            in_specs=[turned] + [whole] * 5,
+            out_specs=turned,
+        ),
         out_shape=jax.ShapeDtypeStruct(front.shape, jnp.bfloat16),
-        in_specs=[pl.BlockSpec(memory_space=SMEM)] + [pl.BlockSpec(memory_space=VMEM)] * 6,
-        out_specs=pl.BlockSpec(memory_space=VMEM),
         compiler_params=params(63),
         name="finish",
     )(pos, front, row_panel, *pieces)
@@ -322,11 +336,12 @@
     sel, jsel, jl, krow, kcol = tables(child_map, pos)
 
     arrived = []
-    for chunk in range(4):
+    for chunk in range(len(CHUNKS)):
         sent = pack_first(sel, jsel, pos, child_updates, other, chunk)
         part = lax.all_to_all(sent, ("x", "col"), 0, 0, tiled=True)
-        out = pack_second(jl, pos, part)
-        arrived += [out[0]] + [over_zk(out[d], d) for d in (1, 2, 3)]
+        stay, swap, out = pack_second(jl, pos, part)
+        crossed = over_zk(out, 2)
+        arrived += [stay, over_zk(swap, 1), crossed, over_zk(crossed, 1)]
     first = arrived[:8]
 
     panel_0 = strip_panel(krow, kcol, first, front_orig, panel_inverse)

time: 253 us -> 209 us (0.83)
  the two profiles are of different devices: /device:TPU:47 before, /device:TPU:67 now
where the time goes in v1:
time: 209 us; the launch traced here: 208 us
  waiting for transfers between devices  107 us (51%)
  starting transfers between devices  54.4 us (26%)
  Pallas kernels  41.9 us (20%)
  other arithmetic  2.47 us (1%)
    ppermute x13, waiting for transfers between devices, over_zk(): return lax.ppermute(array, ('z', 'core'), [(r, r ^ d) for r in range(4)])  81.2 us
    ppermute x13, starting transfers between devices, over_zk(): return lax.ppermute(array, ('z', 'core'), [(r, r ^ d) for r in range(4)])  20.5 us
    all_to_all x3, waiting for transfers between devices, local(): part = lax.all_to_all(sent, ('x', 'col'), 0, 0, tiled=True)  20.4 us
    all_to_all x3, starting transfers between devices, local(): part = lax.all_to_all(sent, ('x', 'col'), 0, 0, tiled=True)  20.1 us
    ppermute x6, starting transfers between devices, moved(): return lax.ppermute(array, ('x', 'z', 'core', 'col'), pairs)  13.8 us
    pallas_call x3, Pallas kernels, pack_first(): pl.pallas_call(kernel, out_shape=jax.ShapeDtypeStruct((16, last - first,...  9.35 us
    pallas_call x3, Pallas kernels, pack_second(): pl.pallas_call(kernel, out_shape=[jax.ShapeDtypeStruct((n,) + arrived.sha...  9.25 us
    pallas_call x1, Pallas kernels, assemble(): pl.pallas_call(kernel, grid=(4,), out_shape=jax.ShapeDtypeStruct(front_or...  7.87 us
  transfers between devices with their start and end apart: 22, of which 11 were waited for; matrix products, arithmetic and copies ran while one was open for 1% of the time, Pallas kernels for 16%

profile of v1, /device:TPU:67, one launch (start us, length us, event | category | flops | bytes accessed | tf_op | source)
XLA Modules:
  0.0 207.8 jit_solution(9711104825385848725)
XLA Ops:
  0.6 0.8 collective-permute-start
  1.4 0.7 pad_add_fusion.pos_ref
  2.0 5.0 %tables.1 = (s32[32]{0:T(128)}, s32[32]{0:T(128)}, s32[48]{0:T(128)}, s32[16]{0:T(128)}, s32[48]{0:T(128)}) custom-call(s32[2,64]{1,0:T(2,128)} %map_ref.1, s32[2]{0:T(128)} %pad_add_fusion.pos_ref), custom_call_target="tpu_custom_call" | custom-call | tf_op jit(solution)/shard_map/tables/pallas_call | solution.py:90
  7.0 1.5 collective-permute-done.other_ref
  8.5 2.9 %shard_map.59 = bf16[16,64,512]{2,1,0:T(8,128)(2,1)} custom-call(s32[32]{0:T(128)} %get-tuple-element.19.sel_ref, s32[32]{0:T(128)} %get-tuple-element.20.jsel_ref, s32[2]{0:T(128)} %pad_add_fusion.pos_ref, bf16[1024,2048]{1,0:T(8,128)(2,1)} %own_ref.5, bf16[1024,2048]{1,0:T(8,128)(2,1)} %collective-permute-done.other_ref), custom_call_target="tpu_custom_call" | custom-call | tf_op jit(solution)/shard_map/pallas_call | solution.py:127
  11.4 6.9 %all-to-all-start = ((bf16[16,64,512]{2,1,0:T(8,128)(2,1)}), bf16[16,64,512]{2,1,0:T(8,128)(2,1)}, u32[]{:S(2)}, u32[]{:S(2)}) async-start(bf16[16,64,512]{2,1,0:T(8,128)(2,1)} %shard_map.59), calls=%async_computation | async-start | bytes 2097152 | tf_op jit(solution)/shard_map/all_to_all | solution.py:341
  18.3 2.9 %shard_map.61 = bf16[16,64,512]{2,1,0:T(8,128)(2,1)} custom-call(s32[32]{0:T(128)} %get-tuple-element.19.sel_ref, s32[32]{0:T(128)} %get-tuple-element.20.jsel_ref, s32[2]{0:T(128)} %pad_add_fusion.pos_ref, bf16[1024,2048]{1,0:T(8,128)(2,1)} %own_ref.5, bf16[1024,2048]{1,0:T(8,128)(2,1)} %collective-permute-done.other_ref), custom_call_target="tpu_custom_call" | custom-call | tf_op jit(solution)/shard_map/pallas_call | solution.py:127
  21.2 11.3 %all-to-all-done.in_ref = bf16[16,64,512]{2,1,0:T(8,128)(2,1)} async-done(((bf16[16,64,512]{2,1,0:T(8,128)(2,1)}), bf16[16,64,512]{2,1,0:T(8,128)(2,1)}, u32[]{:S(2)}, u32[]{:S(2)}) %all-to-all-start) | async-done | bytes 1048608 | tf_op jit(solution)/shard_map/all_to_all | solution.py:341
  32.5 6.1 %all-to-all-start.1 = ((bf16[16,64,512]{2,1,0:T(8,128)(2,1)}), bf16[16,64,512]{2,1,0:T(8,128)(2,1)}, u32[]{:S(2)}, u32[]{:S(2)}) async-start(bf16[16,64,512]{2,1,0:T(8,128)(2,1)} %shard_map.61), calls=%async_computation.1 | async-start | bytes 2097152 | tf_op jit(solution)/shard_map/all_to_all | solution.py:341
  38.6 3.6 %shard_map.63 = bf16[16,128,512]{2,1,0:T(8,128)(2,1)} custom-call(s32[32]{0:T(128)} %get-tuple-element.19.sel_ref, s32[32]{0:T(128)} %get-tuple-element.20.jsel_ref, s32[2]{0:T(128)} %pad_add_fusion.pos_ref, bf16[1024,2048]{1,0:T(8,128)(2,1)} %own_ref.5, bf16[1024,2048]{1,0:T(8,128)(2,1)} %collective-permute-done.other_ref), custom_call_target="tpu_custom_call" | custom-call | tf_op jit(solution)/shard_map/pallas_call | solution.py:127
  42.2 9.1 %all-to-all-done.1.in_ref = bf16[16,64,512]{2,1,0:T(8,128)(2,1)} async-done(((bf16[16,64,512]{2,1,0:T(8,128)(2,1)}), bf16[16,64,512]{2,1,0:T(8,128)(2,1)}, u32[]{:S(2)}, u32[]{:S(2)}) %all-to-all-start.1) | async-done | bytes 1048608 | tf_op jit(solution)/shard_map/all_to_all | solution.py:341
  51.3 7.1 %all-to-all-start.2 = ((bf16[16,128,512]{2,1,0:T(8,128)(2,1)}), bf16[16,128,512]{2,1,0:T(8,128)(2,1)}, u32[]{:S(2)}, u32[]{:S(2)}) async-start(bf16[16,128,512]{2,1,0:T(8,128)(2,1)} %shard_map.63), calls=%async_computation.2 | async-start | bytes 4194304 | tf_op jit(solution)/shard_map/all_to_all | solution.py:341
  58.4 2.8 %shard_map.60 = (bf16[4,64,512]{2,1,0:T(8,128)(2,1)}, bf16[4,64,512]{2,1,0:T(8,128)(2,1)}, bf16[8,64,512]{2,1,0:T(8,128)(2,1)}) custom-call(s32[48]{0:T(128)} %get-tuple-element.18.jl_ref, s32[2]{0:T(128)} %pad_add_fusion.pos_ref, bf16[16,64,512]{2,1,0:T(8,128)(2,1)} %all-to-all-done.in_ref), custom_call_target="tpu_custom_call" | custom-call | tf_op jit(solution)/shard_map/pallas_call | solution.py:151
  61.1 5.1 %collective-permute-start.2 = (bf16[8,64,512]{2,1,0:T(8,128)(2,1)}, bf16[8,64,512]{2,1,0:T(8,128)(2,1)S(1)}, u32[]{:S(2)}, u32[]{:S(2)}) collective-permute-start(bf16[8,64,512]{2,1,0:T(8,128)(2,1)} %get-tuple-element.23), channel_id=1, source_target_pairs={{0,8},{4,12},{8,0},{12,4},{1,9},{5,13},{9,1},{13,5},{2,10},{6,14},... | collective-permute-start | bytes 1572872 | tf_op jit(solution)/shard_map/ppermute | solution.py:326
  66.3 2.8 %shard_map.62 = (bf16[4,64,512]{2,1,0:T(8,128)(2,1)}, bf16[4,64,512]{2,1,0:T(8,128)(2,1)}, bf16[8,64,512]{2,1,0:T(8,128)(2,1)}) custom-call(s32[48]{0:T(128)} %get-tuple-element.18.jl_ref, s32[2]{0:T(128)} %pad_add_fusion.pos_ref, bf16[16,64,512]{2,1,0:T(8,128)(2,1)} %all-to-all-done.1.in_ref), custom_call_target="tpu_custom_call" | custom-call | tf_op jit(solution)/shard_map/pallas_call | solution.py:151
  69.1 0.3 collective-permute-start.5
  69.3 31.7 %collective-permute-done.2.refs_2_ = bf16[8,64,512]{2,1,0:T(8,128)(2,1)S(1)} collective-permute-done((bf16[8,64,512]{2,1,0:T(8,128)(2,1)}, bf16[8,64,512]{2,1,0:T(8,128)(2,1)S(1)}, u32[]{:S(2)}, u32[]{:S(2)}) %collective-permute-start.2) | collective-permute-done | bytes 524320 | tf_op jit(solution)/shard_map/ppermute | solution.py:326
  101.0 0.0 copy-start
  101.0 2.0 collective-permute-start.3
  103.0 9.3 %collective-permute-done.5.refs_6_ = bf16[8,64,512]{2,1,0:T(8,128)(2,1)} collective-permute-done((bf16[8,64,512]{2,1,0:T(8,128)(2,1)}, bf16[8,64,512]{2,1,0:T(8,128)(2,1)}, u32[]{:S(2)}, u32[]{:S(2)}) %collective-permute-start.5) | collective-permute-done | bytes 524320 | tf_op jit(solution)/shard_map/ppermute | solution.py:326
  112.3 1.3 collective-permute-start.6
  113.6 0.0 all-to-all-done.2.in_ref
  113.6 3.7 %shard_map.64 = (bf16[4,128,512]{2,1,0:T(8,128)(2,1)}, bf16[4,128,512]{2,1,0:T(8,128)(2,1)}, bf16[8,128,512]{2,1,0:T(8,128)(2,1)}) custom-call(s32[48]{0:T(128)} %get-tuple-element.18.jl_ref, s32[2]{0:T(128)} %pad_add_fusion.pos_ref, bf16[16,128,512]{2,1,0:T(8,128)(2,1)} %all-to-all-done.2.in_ref), custom_call_target="tpu_custom_call" | custom-call | tf_op jit(solution)/shard_map/pallas_call | solution.py:151
  117.3 4.7 %collective-permute-start.8 = (bf16[8,128,512]{2,1,0:T(8,128)(2,1)}, bf16[8,128,512]{2,1,0:T(8,128)(2,1)}, u32[]{:S(2)}, u32[]{:S(2)}) collective-permute-start(bf16[8,128,512]{2,1,0:T(8,128)(2,1)} %get-tuple-element.29), channel_id=1, source_target_pairs={{0,8},{4,12},{8,0},{12,4},{1,9},{5,13},{9,1},{13,5},{2,10},{6,14},... | collective-permute-start | bytes 3145736 | tf_op jit(solution)/shard_map/ppermute | solution.py:326
  122.0 0.3 collective-permute-start.1
  122.2 0.2 collective-permute-start.4
  122.5 1.2 collective-permute-done.1.refs_1_
  123.7 0.0 copy-start.2
  123.7 0.4 collective-permute-done.4.refs_5_
  124.1 0.0 copy-start.3
  124.1 0.0 collective-permute-done.3.refs_3_
  124.1 0.7 copy-done.3
  124.8 0.0 collective-permute-done.6.refs_7_
  124.8 0.0 copy-done
  124.8 0.0 copy-done.2
  124.8 4.3 %strip_panel.1 = bf16[640,256]{1,0:T(8,128)(2,1)} custom-call(s32[16]{0:T(128)} %get-tuple-element.16.krow_ref, s32[48]{0:T(128)} %get-tuple-element.17.kcol_ref, bf16[4,64,512]{2,1,0:T(8,128)(2,1)} %get-tuple-element.21.refs_0_, bf16[4,64,512]{2,1,0:T(8,128)(2,1)} %copy-done.2, bf16[8,64,512]{2,1,0:T(8,128)(2,1)} %copy-done, ...), custom_call_target="tpu_custom_call" | custom-call | tf_op jit(solution)/shard_map/strip_panel/pallas_call | solution.py:226
  129.1 3.1 %collective-permute-start.15 = (bf16[640,256]{1,0:T(8,128)(2,1)}, bf16[640,256]{1,0:T(8,128)(2,1)S(1)}, u32[]{:S(2)}, u32[]{:S(2)}) collective-permute-start(bf16[640,256]{1,0:T(8,128)(2,1)} %strip_panel.1), channel_id=1, source_target_pairs={{0,48},{4,52},{8,56},{12,60},{16,1},{20,5},{24,9},{28,13},{32,18},... | collective-permute-start | bytes 983048 | tf_op jit(solution)/shard_map/ppermute | solution.py:322
  132.2 1.9 collective-permute-start.13
  134.1 1.3 collective-permute-start.14
  135.4 1.3 collective-permute-start.12
  136.7 2.5 %collective-permute-done.15 = bf16[640,256]{1,0:T(8,128)(2,1)S(1)} collective-permute-done((bf16[640,256]{1,0:T(8,128)(2,1)}, bf16[640,256]{1,0:T(8,128)(2,1)S(1)}, u32[]{:S(2)}, u32[]{:S(2)}) %collective-permute-start.15) | collective-permute-done | bytes 327712 | tf_op jit(solution)/shard_map/ppermute | solution.py:322
  139.2 1.3 collective-permute-start.10
  140.5 2.5 %collective-permute-done.13 = bf16[640,256]{1,0:T(8,128)(2,1)S(1)} collective-permute-done((bf16[640,256]{1,0:T(8,128)(2,1)}, bf16[640,256]{1,0:T(8,128)(2,1)S(1)}, u32[]{:S(2)}, u32[]{:S(2)}) %collective-permute-start.13) | collective-permute-done | bytes 327712 | tf_op jit(solution)/shard_map/ppermute | solution.py:322
  143.1 4.9 %collective-permute-start.11 = (bf16[640,256]{1,0:T(8,128)(2,1)}, bf16[640,256]{1,0:T(8,128)(2,1)S(1)}, u32[]{:S(2)}, u32[]{:S(2)}) collective-permute-start(bf16[640,256]{1,0:T(8,128)(2,1)} %strip_panel.1), channel_id=1, source_target_pairs={{0,2},{4,6},{8,10},{12,14},{16,18},{20,22},{24,26},{28,30},{32,34}... | collective-permute-start | bytes 983048 | tf_op jit(solution)/shard_map/ppermute | solution.py:322
  148.0 21.1 %collective-permute-done.8.refs_10_ = bf16[8,128,512]{2,1,0:T(8,128)(2,1)} collective-permute-done((bf16[8,128,512]{2,1,0:T(8,128)(2,1)}, bf16[8,128,512]{2,1,0:T(8,128)(2,1)}, u32[]{:S(2)}, u32[]{:S(2)}) %collective-permute-start.8) | collective-permute-done | bytes 1048608 | tf_op jit(solution)/shard_map/ppermute | solution.py:326
  169.1 0.6 collective-permute-start.9
  169.7 0.0 collective-permute-done.14
  169.7 0.0 collective-permute-done.12
  169.7 0.0 collective-permute-done.10
  169.7 0.0 collective-permute-done.11
  169.7 1.8 add_select_fusion
  171.5 4.2 %collective-permute-start.17 = (bf16[640,256]{1,0:T(8,128)(2,1)S(1)}, bf16[640,256]{1,0:T(8,128)(2,1)}, u32[]{:S(2)}, u32[]{:S(2)}) collective-permute-start(bf16[640,256]{1,0:T(8,128)(2,1)S(1)} %get-tuple-element.30.refs_0_), channel_id=1, source_target_pairs={{0,8},{4,12},{8,0},{12,4},{1,9},{5,13},{9,1},{13,5},{2,10},{6,14},... | collective-permute-start | bytes 983048 | tf_op jit(solution)/shard_map/ppermute | solution.py:326
  175.8 0.3 collective-permute-start.7
  176.1 0.2 collective-permute-start.16
  176.3 16.0 %collective-permute-done.17.refs_2_ = bf16[640,256]{1,0:T(8,128)(2,1)} collective-permute-done((bf16[640,256]{1,0:T(8,128)(2,1)S(1)}, bf16[640,256]{1,0:T(8,128)(2,1)}, u32[]{:S(2)}, u32[]{:S(2)}) %collective-permute-start.17) | collective-permute-done | bytes 327712 | tf_op jit(solution)/shard_map/ppermute | solution.py:326
  192.3 0.6 collective-permute-start.18
  192.8 0.0 collective-permute-done.7.refs_9_
  192.9 0.0 collective-permute-done.9.refs_11_
  192.9 0.8 copy-done.4
  193.6 7.9 %assemble.1.front_ref = bf16[640,2560]{1,0:T(8,128)(2,1)} custom-call(s32[16]{0:T(128)} %get-tuple-element.16.krow_ref, s32[48]{0:T(128)} %get-tuple-element.17.kcol_ref, bf16[4,64,512]{2,1,0:T(8,128)(2,1)} %get-tuple-element.21.refs_0_, bf16[4,64,512]{2,1,0:T(8,128)(2,1)} %copy-done.2, bf16[8,64,512]{2,1,0:T(8,128)(2,1)} %copy-done, ...), custom_call_target="tpu_custom_call" | custom-call | tf_op jit(solution)/shard_map/assemble/pallas_call | solution.py:267
  201.5 0.0 copy-done.1
  201.5 0.0 collective-permute-done.16.refs_1_
  201.5 0.0 collective-permute-done.18.refs_3_
  201.6 6.2 %finish.1 = bf16[640,2560]{1,0:T(8,128)(2,1)} custom-call(s32[2]{0:T(128)} %pad_add_fusion.pos_ref, bf16[640,2560]{1,0:T(8,128)(2,1)} %assemble.1.front_ref, bf16[640,256]{1,0:T(8,128)(2,1)} %get-tuple-element.31.row_ref, bf16[640,256]{1,0:T(8,128)(2,1)} %copy-done.1, bf16[640,256]{1,0:T(8,128)(2,1)} %collective-permute-done.16.refs_1_, ...), custom_call_target="tpu_custom_call" | custom-call | tf_op jit(solution)/shard_map/finish/pallas_call | solution.py:303
  (2 shorter events, 0.0 us)
Async XLA Ops:
  0.6 7.9 %collective-permute-start = (bf16[1024,2048]{1,0:T(8,128)(2,1)}, bf16[1024,2048]{1,0:T(8,128)(2,1)}, u32[]{:S(2)}, u32[]{:S(2)}) collective-permute-start(bf16[1024,2048]{1,0:T(8,128)(2,1)} %own_ref.5), channel_id=1, source_target_pairs={{0,4},{4,0},{8,12},{12,8},{1,5},{5,1},{9,13},{13,9},{2,6},{6,2},{1... | collective-permute-start | bytes 12582920 | tf_op jit(solution)/shard_map/ppermute | solution.py:326
  11.4 21.1 %all-to-all-start = ((bf16[16,64,512]{2,1,0:T(8,128)(2,1)}), bf16[16,64,512]{2,1,0:T(8,128)(2,1)}, u32[]{:S(2)}, u32[]{:S(2)}) async-start(bf16[16,64,512]{2,1,0:T(8,128)(2,1)} %shard_map.59), calls=%async_computation | async-start | bytes 2097152 | tf_op jit(solution)/shard_map/all_to_all | solution.py:341
  32.5 18.8 %all-to-all-start.1 = ((bf16[16,64,512]{2,1,0:T(8,128)(2,1)}), bf16[16,64,512]{2,1,0:T(8,128)(2,1)}, u32[]{:S(2)}, u32[]{:S(2)}) async-start(bf16[16,64,512]{2,1,0:T(8,128)(2,1)} %shard_map.61), calls=%async_computation.1 | async-start | bytes 2097152 | tf_op jit(solution)/shard_map/all_to_all | solution.py:341
  51.3 62.3 %all-to-all-start.2 = ((bf16[16,128,512]{2,1,0:T(8,128)(2,1)}), bf16[16,128,512]{2,1,0:T(8,128)(2,1)}, u32[]{:S(2)}, u32[]{:S(2)}) async-start(bf16[16,128,512]{2,1,0:T(8,128)(2,1)} %shard_map.63), calls=%async_computation.2 | async-start | bytes 4194304 | tf_op jit(solution)/shard_map/all_to_all | solution.py:341
  61.1 39.8 %collective-permute-start.2 = (bf16[8,64,512]{2,1,0:T(8,128)(2,1)}, bf16[8,64,512]{2,1,0:T(8,128)(2,1)S(1)}, u32[]{:S(2)}, u32[]{:S(2)}) collective-permute-start(bf16[8,64,512]{2,1,0:T(8,128)(2,1)} %get-tuple-element.23), channel_id=1, source_target_pairs={{0,8},{4,12},{8,0},{12,4},{1,9},{5,13},{9,1},{13,5},{2,10},{6,14},... | collective-permute-start | bytes 1572872 | tf_op jit(solution)/shard_map/ppermute | solution.py:326
  69.1 43.3 %collective-permute-start.5 = (bf16[8,64,512]{2,1,0:T(8,128)(2,1)}, bf16[8,64,512]{2,1,0:T(8,128)(2,1)}, u32[]{:S(2)}, u32[]{:S(2)}) collective-permute-start(bf16[8,64,512]{2,1,0:T(8,128)(2,1)} %get-tuple-element.26), channel_id=1, source_target_pairs={{0,8},{4,12},{8,0},{12,4},{1,9},{5,13},{9,1},{13,5},{2,10},{6,14},... | collective-permute-start | bytes 1572872 | tf_op jit(solution)/shard_map/ppermute | solution.py:326
  101.0 23.8 %copy-start = (bf16[8,64,512]{2,1,0:T(8,128)(2,1)}, bf16[8,64,512]{2,1,0:T(8,128)(2,1)S(1)}, u32[]{:S(2)}) copy-start(bf16[8,64,512]{2,1,0:T(8,128)(2,1)S(1)} %collective-permute-done.2.refs_2_) | copy-start | bytes 1572868
  101.0 23.1 %collective-permute-start.3 = (bf16[8,64,512]{2,1,0:T(8,128)(2,1)S(1)}, bf16[8,64,512]{2,1,0:T(8,128)(2,1)}, u32[]{:S(2)}, u32[]{:S(2)}) collective-permute-start(bf16[8,64,512]{2,1,0:T(8,128)(2,1)S(1)} %collective-permute-done.2.refs_2_), channel_id=1, source_target_pairs={{0,4},{4,0},{8,12},{12,8},{1,5},{5,1},{9,13},{13,9},{2,6},{6,2},{1... | collective-permute-start | bytes 1572872 | tf_op jit(solution)/shard_map/ppermute | solution.py:326
  112.3 12.5 %collective-permute-start.6 = (bf16[8,64,512]{2,1,0:T(8,128)(2,1)}, bf16[8,64,512]{2,1,0:T(8,128)(2,1)}, u32[]{:S(2)}, u32[]{:S(2)}) collective-permute-start(bf16[8,64,512]{2,1,0:T(8,128)(2,1)} %collective-permute-done.5.refs_6_), channel_id=1, source_target_pairs={{0,4},{4,0},{8,12},{12,8},{1,5},{5,1},{9,13},{13,9},{2,6},{6,2},{1... | collective-permute-start | bytes 1572872 | tf_op jit(solution)/shard_map/ppermute | solution.py:326
  117.3 51.8 %collective-permute-start.8 = (bf16[8,128,512]{2,1,0:T(8,128)(2,1)}, bf16[8,128,512]{2,1,0:T(8,128)(2,1)}, u32[]{:S(2)}, u32[]{:S(2)}) collective-permute-start(bf16[8,128,512]{2,1,0:T(8,128)(2,1)} %get-tuple-element.29), channel_id=1, source_target_pairs={{0,8},{4,12},{8,0},{12,4},{1,9},{5,13},{9,1},{13,5},{2,10},{6,14},... | collective-permute-start | bytes 3145736 | tf_op jit(solution)/shard_map/ppermute | solution.py:326
  122.0 1.7 collective-permute-start.1
  122.2 1.8 collective-permute-start.4
  123.7 1.1 copy-start.2
  124.1 0.7 copy-start.3
  129.1 10.2 %collective-permute-start.15 = (bf16[640,256]{1,0:T(8,128)(2,1)}, bf16[640,256]{1,0:T(8,128)(2,1)S(1)}, u32[]{:S(2)}, u32[]{:S(2)}) collective-permute-start(bf16[640,256]{1,0:T(8,128)(2,1)} %strip_panel.1), channel_id=1, source_target_pairs={{0,48},{4,52},{8,56},{12,60},{16,1},{20,5},{24,9},{28,13},{32,18},... | collective-permute-start | bytes 983048 | tf_op jit(solution)/shard_map/ppermute | solution.py:322
  132.2 10.9 %collective-permute-start.13 = (bf16[640,256]{1,0:T(8,128)(2,1)}, bf16[640,256]{1,0:T(8,128)(2,1)S(1)}, u32[]{:S(2)}, u32[]{:S(2)}) collective-permute-start(bf16[640,256]{1,0:T(8,128)(2,1)} %strip_panel.1), channel_id=1, source_target_pairs={{0,16},{4,20},{8,24},{12,28},{16,33},{20,37},{24,41},{28,45},{32,5... | collective-permute-start | bytes 983048 | tf_op jit(solution)/shard_map/ppermute | solution.py:322
  134.1 35.6 %collective-permute-start.14 = (bf16[640,256]{1,0:T(8,128)(2,1)}, bf16[640,256]{1,0:T(8,128)(2,1)S(1)}, u32[]{:S(2)}, u32[]{:S(2)}) collective-permute-start(bf16[640,256]{1,0:T(8,128)(2,1)} %strip_panel.1), channel_id=1, source_target_pairs={{0,32},{4,36},{8,40},{12,44},{16,49},{20,53},{24,57},{28,61},{32,2... | collective-permute-start | bytes 983048 | tf_op jit(solution)/shard_map/ppermute | solution.py:322
  135.4 34.3 %collective-permute-start.12 = (bf16[640,256]{1,0:T(8,128)(2,1)}, bf16[640,256]{1,0:T(8,128)(2,1)S(1)}, u32[]{:S(2)}, u32[]{:S(2)}) collective-permute-start(bf16[640,256]{1,0:T(8,128)(2,1)} %strip_panel.1), channel_id=1, source_target_pairs={{0,3},{4,7},{8,11},{12,15},{16,19},{20,23},{24,27},{28,31},{32,35}... | collective-permute-start | bytes 983048 | tf_op jit(solution)/shard_map/ppermute | solution.py:322
  139.2 30.5 %collective-permute-start.10 = (bf16[640,256]{1,0:T(8,128)(2,1)}, bf16[640,256]{1,0:T(8,128)(2,1)S(1)}, u32[]{:S(2)}, u32[]{:S(2)}) collective-permute-start(bf16[640,256]{1,0:T(8,128)(2,1)} %strip_panel.1), channel_id=1, source_target_pairs={{0,1},{4,5},{8,9},{12,13},{16,17},{20,21},{24,25},{28,29},{32,33},... | collective-permute-start | bytes 983048 | tf_op jit(solution)/shard_map/ppermute | solution.py:322
  143.1 26.6 %collective-permute-start.11 = (bf16[640,256]{1,0:T(8,128)(2,1)}, bf16[640,256]{1,0:T(8,128)(2,1)S(1)}, u32[]{:S(2)}, u32[]{:S(2)}) collective-permute-start(bf16[640,256]{1,0:T(8,128)(2,1)} %strip_panel.1), channel_id=1, source_target_pairs={{0,2},{4,6},{8,10},{12,14},{16,18},{20,22},{24,26},{28,30},{32,34}... | collective-permute-start | bytes 983048 | tf_op jit(solution)/shard_map/ppermute | solution.py:322
  169.1 23.8 %collective-permute-start.9 = (bf16[8,128,512]{2,1,0:T(8,128)(2,1)}, bf16[8,128,512]{2,1,0:T(8,128)(2,1)}, u32[]{:S(2)}, u32[]{:S(2)}) collective-permute-start(bf16[8,128,512]{2,1,0:T(8,128)(2,1)} %collective-permute-done.8.refs_10_), channel_id=1, source_target_pairs={{0,4},{4,0},{8,12},{12,8},{1,5},{5,1},{9,13},{13,9},{2,6},{6,2},{1... | collective-permute-start | bytes 3145736 | tf_op jit(solution)/shard_map/ppermute | solution.py:326
  171.5 30.0 %copy-start.1 = (bf16[640,256]{1,0:T(8,128)(2,1)}, bf16[640,256]{1,0:T(8,128)(2,1)S(1)}, u32[]{:S(2)}) copy-start(bf16[640,256]{1,0:T(8,128)(2,1)S(1)} %get-tuple-element.30.refs_0_) | copy-start | bytes 983044
  171.5 20.7 %collective-permute-start.17 = (bf16[640,256]{1,0:T(8,128)(2,1)S(1)}, bf16[640,256]{1,0:T(8,128)(2,1)}, u32[]{:S(2)}, u32[]{:S(2)}) collective-permute-start(bf16[640,256]{1,0:T(8,128)(2,1)S(1)} %get-tuple-element.30.refs_0_), channel_id=1, source_target_pairs={{0,8},{4,12},{8,0},{12,4},{1,9},{5,13},{9,1},{13,5},{2,10},{6,14},... | collective-permute-start | bytes 983048 | tf_op jit(solution)/shard_map/ppermute | solution.py:326
  175.8 17.1 %collective-permute-start.7 = (bf16[4,128,512]{2,1,0:T(8,128)(2,1)}, bf16[4,128,512]{2,1,0:T(8,128)(2,1)S(1)}, u32[]{:S(2)}, u32[]{:S(2)}) collective-permute-start(bf16[4,128,512]{2,1,0:T(8,128)(2,1)} %get-tuple-element.28), channel_id=1, source_target_pairs={{0,4},{4,0},{8,12},{12,8},{1,5},{5,1},{9,13},{13,9},{2,6},{6,2},{1... | collective-permute-start | bytes 1572872 | tf_op jit(solution)/shard_map/ppermute | solution.py:326
  176.1 25.5 %collective-permute-start.16 = (bf16[640,256]{1,0:T(8,128)(2,1)S(1)}, bf16[640,256]{1,0:T(8,128)(2,1)}, u32[]{:S(2)}, u32[]{:S(2)}) collective-permute-start(bf16[640,256]{1,0:T(8,128)(2,1)S(1)} %get-tuple-element.30.refs_0_), channel_id=1, source_target_pairs={{0,4},{4,0},{8,12},{12,8},{1,5},{5,1},{9,13},{13,9},{2,6},{6,2},{1... | collective-permute-start | bytes 983048 | tf_op jit(solution)/shard_map/ppermute | solution.py:326
  192.3 9.3 %collective-permute-start.18 = (bf16[640,256]{1,0:T(8,128)(2,1)}, bf16[640,256]{1,0:T(8,128)(2,1)}, u32[]{:S(2)}, u32[]{:S(2)}) collective-permute-start(bf16[640,256]{1,0:T(8,128)(2,1)} %collective-permute-done.17.refs_2_), channel_id=1, source_target_pairs={{0,4},{4,0},{8,12},{12,8},{1,5},{5,1},{9,13},{13,9},{2,6},{6,2},{1... | collective-permute-start | bytes 983048 | tf_op jit(solution)/shard_map/ppermute | solution.py:326
  192.9 0.8 copy-start.4

commit v2 on v1

--- a/solution.py
+++ b/solution.py
@@ -244,13 +244,14 @@
     )(krow, kcol, *arrived, front_orig, panel_inverse)
 
 
-def assemble(krow, kcol, arrived, front_orig):
+def assemble(pos, krow, kcol, arrived, front_orig, row_panel, pieces):
     block = arrived[0].shape[2] // 4
     rows, cols = front_orig.shape
 
-    def kernel(krow_ref, kcol_ref, *refs):
-        orig_ref, out_ref, buf_ref, eye_ref, sem = refs[12:]
+    def kernel(pos_ref, krow_ref, kcol_ref, *refs):
+        orig_ref, row_ref, own_ref, twin_ref, out_ref, buf_ref, eye_ref, sem = refs[12:]
         step = pl.program_id(0)
+        first = ((pos_ref[0] % 4) ^ step) * (QB // 4)
 
         @pl.when(step == 0)
         def _():
@@ -261,54 +262,67 @@
             for p in range(MB):
                 here = slice(p * block, (p + 1) * block)
                 out_ref[here, side] = front_tile(
-                    orig_ref[here, side], buf_ref, krow_ref, kcol_ref, eye_ref, p, step * (QB // 4) + q
+                    orig_ref[here, side], buf_ref, krow_ref, kcol_ref, eye_ref, p, first + q
                 )
-
-    return pl.pallas_call(
-        kernel,
-        grid=(4,),
-        out_shape=jax.ShapeDtypeStruct(front_orig.shape, jnp.bfloat16),
-        in_specs=[pl.BlockSpec(memory_space=SMEM)] * 2
-        + [pl.BlockSpec(memory_space=pl.ANY)] * 12
-        + [pl.BlockSpec((rows, cols // 4), lambda i: (0, i))],
-        out_specs=pl.BlockSpec((rows, cols // 4), lambda i: (0, i)),
-        scratch_shapes=[
-            pltpu.VMEM((32, block, 4 * block), jnp.bfloat16),
-            pltpu.VMEM((4, block, 2 * block), jnp.bfloat16),
-            pltpu.SemaphoreType.DMA((12,)),
-        ],
-        compiler_params=params(63),
-        name="assemble",
-    )(krow, kcol, *arrived, front_orig)
-
-
-def finish(pos, front, row_panel, pieces):
-    rows, cols = front.shape
-    wide = cols // 4
-
-    def kernel(pos_ref, front_ref, row_ref, *refs):
-        out_ref = refs[4]
-        for w in range(4):
-
-            @pl.when(pl.program_id(0) == w)
+        for w, ref in enumerate((own_ref, twin_ref)):
+
+            @pl.when(step == w)
             def _():
-                update = lax.dot_general(
-                    row_ref[...], refs[w][...], (((1,), (1,)), ((), ())),
-                    preferred_element_type=jnp.float32,
-                )
-                out_ref[...] = (front_ref[...].astype(jnp.float32) - update).astype(jnp.bfloat16)
+                subtract(out_ref, out_ref, row_ref, ref)
 
     whole = pl.BlockSpec(row_panel.shape, lambda w, pos_ref: (0, 0))
-    turned = pl.BlockSpec((rows, wide), lambda w, pos_ref: (0, (pos_ref[0] % 4) ^ w))
+    turned = pl.BlockSpec((rows, cols // 4), lambda w, pos_ref: (0, (pos_ref[0] % 4) ^ w))
     return pl.pallas_call(
         kernel,
         grid_spec=pltpu.PrefetchScalarGridSpec(
             num_scalar_prefetch=1,
             grid=(4,),
-            in_specs=[turned] + [whole] * 5,
+            in_specs=[pl.BlockSpec(memory_space=SMEM)] * 2
+            + [pl.BlockSpec(memory_space=pl.ANY)] * 12
+            + [turned]
+            + [whole] * 3,
+            out_specs=turned,
+            scratch_shapes=[
+                pltpu.VMEM((32, block, 4 * block), jnp.bfloat16),
+                pltpu.VMEM((4, block, 2 * block), jnp.bfloat16),
+                pltpu.SemaphoreType.DMA((12,)),
+            ],
+        ),
+        out_shape=jax.ShapeDtypeStruct(front_orig.shape, jnp.bfloat16),
+        compiler_params=params(63),
+        name="assemble",
+    )(pos, krow, kcol, *arrived, front_orig, row_panel, *pieces)
+
+
+def subtract(out_ref, front_ref, row_ref, piece_ref):
+    update = lax.dot_general(
+        row_ref[...], piece_ref[...], (((1,), (1,)), ((), ())), preferred_element_type=jnp.float32
+    )
+    out_ref[...] = (front_ref[...].astype(jnp.float32) - update).astype(jnp.bfloat16)
+
+
+def finish(pos, front, row_panel, pieces):
+    rows, cols = front.shape
+
+    def kernel(pos_ref, front_ref, row_ref, own_ref, twin_ref, out_ref):
+        for w, ref in enumerate((own_ref, twin_ref)):
+
+            @pl.when(pl.program_id(0) == w)
+            def _():
+                subtract(out_ref, front_ref, row_ref, ref)
+
+    whole = pl.BlockSpec(row_panel.shape, lambda w, pos_ref: (0, 0))
+    turned = pl.BlockSpec((rows, cols // 4), lambda w, pos_ref: (0, (pos_ref[0] % 4) ^ (w + 2)))
+    return pl.pallas_call(
+        kernel,
+        grid_spec=pltpu.PrefetchScalarGridSpec(
+            num_scalar_prefetch=1,
+            grid=(2,),
+            in_specs=[turned] + [whole] * 3,
             out_specs=turned,
         ),
         out_shape=jax.ShapeDtypeStruct(front.shape, jnp.bfloat16),
+        input_output_aliases={1: 0},
         compiler_params=params(63),
         name="finish",
     )(pos, front, row_panel, *pieces)
@@ -341,7 +355,8 @@
         part = lax.all_to_all(sent, ("x", "col"), 0, 0, tiled=True)
         stay, swap, out = pack_second(jl, pos, part)
         crossed = over_zk(out, 2)
-        arrived += [stay, over_zk(swap, 1), crossed, over_zk(crossed, 1)]
+        near = over_zk(swap, 1)
+        arrived += [stay, near, crossed, over_zk(crossed, 1)]
     first = arrived[:8]
 
     panel_0 = strip_panel(krow, kcol, first, front_orig, panel_inverse)
@@ -356,10 +371,10 @@
     row_panel = jnp.where(me_col == 0, panel_0, spread[0] + spread[1] + spread[2])
     piece = jnp.where(me_x == me_col, row_panel, sides[0] + sides[1] + sides[2])
     across = over_zk(piece, 2)
-    pieces = [piece, over_zk(piece, 1), across, over_zk(across, 1)]
-
-    front = assemble(krow, kcol, arrived, front_orig)
-    return (finish(pos, front, row_panel, pieces), row_panel)
+    near = [piece, over_zk(piece, 1)]
+    far = [across, over_zk(across, 1)]
+    front = assemble(pos, krow, kcol, arrived, front_orig, row_panel, near)
+    return (finish(pos, front, row_panel, far), row_panel)
 
 
 def solution(mesh):

time: 209 us -> 209 us (level)
  waiting for transfers between devices: 107 us -> 98.1 us
  starting transfers between devices: 54.4 us -> 63.1 us
    ppermute x6, starting transfers between devices: 13.8 us -> 22.5 us  [moved(): return lax.ppermute(array, ('x', 'z', 'core', 'col'), pairs)]
    ppermute x13, waiting for transfers between devices: 81.2 us -> 76 us  [over_zk(): return lax.ppermute(array, ('z', 'core'), [(r, r ^ d) for r in range(4)])]
    ppermute x6, waiting for transfers between devices: 5.05 us -> 1.65 us  [moved(): return lax.ppermute(array, ('x', 'z', 'core', 'col'), pairs)]
    pallas_call x1, Pallas kernels: 6.23 us -> 3.98 us  [finish(): pl.pallas_call(kernel, grid_spec=pltpu.PrefetchScalarGridSpec(num_scalar_...]
  transfers between devices with their start and end apart: 22 -> 22, of which waited for: 11 -> 10; matrix products, arithmetic and copies ran while one was open for 1% -> 1% of each run, Pallas kernels for 16% -> 17%
where the time goes in v2:
time: 209 us; the launch traced here: 208 us
  waiting for transfers between devices  98.1 us (47%)
  starting transfers between devices  63.1 us (30%)
  Pallas kernels  41.6 us (20%)
  other arithmetic  2.4 us (1%)
    ppermute x13, waiting for transfers between devices, over_zk(): return lax.ppermute(array, ('z', 'core'), [(r, r ^ d) for r in range(4)])  76 us
    ppermute x6, starting transfers between devices, moved(): return lax.ppermute(array, ('x', 'z', 'core', 'col'), pairs)  22.5 us
    ppermute x13, starting transfers between devices, over_zk(): return lax.ppermute(array, ('z', 'core'), [(r, r ^ d) for r in range(4)])  20.5 us
    all_to_all x3, waiting for transfers between devices, local(): part = lax.all_to_all(sent, ('x', 'col'), 0, 0, tiled=True)  20.4 us
    all_to_all x3, starting transfers between devices, local(): part = lax.all_to_all(sent, ('x', 'col'), 0, 0, tiled=True)  20.1 us
    pallas_call x1, Pallas kernels, assemble(): pl.pallas_call(kernel, grid_spec=pltpu.PrefetchScalarGridSpec(num_scalar_...  9.79 us
    pallas_call x3, Pallas kernels, pack_first(): pl.pallas_call(kernel, out_shape=jax.ShapeDtypeStruct((16, last - first,...  9.36 us
    pallas_call x3, Pallas kernels, pack_second(): pl.pallas_call(kernel, out_shape=[jax.ShapeDtypeStruct((n,) + arrived.sha...  9.25 us
  transfers between devices with their start and end apart: 22, of which 10 were waited for; matrix products, arithmetic and copies ran while one was open for 1% of the time, Pallas kernels for 17%

profile of v2, /device:TPU:67, one launch (start us, length us, event | category | flops | bytes accessed | tf_op | source)
XLA Modules:
  0.0 207.6 jit_solution(9957799750311757118)
XLA Ops:
  0.6 0.8 collective-permute-start
  1.4 0.6 pad_add_fusion.pos_ref
  2.0 5.0 %tables.1 = (s32[32]{0:T(128)}, s32[32]{0:T(128)}, s32[48]{0:T(128)}, s32[16]{0:T(128)}, s32[48]{0:T(128)}) custom-call(s32[2,64]{1,0:T(2,128)} %map_ref.1, s32[2]{0:T(128)} %pad_add_fusion.pos_ref), custom_call_target="tpu_custom_call" | custom-call | tf_op jit(solution)/shard_map/tables/pallas_call | solution.py:90
  7.0 1.5 collective-permute-done.other_ref
  8.5 2.9 %shard_map.61 = bf16[16,64,512]{2,1,0:T(8,128)(2,1)} custom-call(s32[32]{0:T(128)} %get-tuple-element.19.sel_ref, s32[32]{0:T(128)} %get-tuple-element.20.jsel_ref, s32[2]{0:T(128)} %pad_add_fusion.pos_ref, bf16[1024,2048]{1,0:T(8,128)(2,1)} %own_ref.5, bf16[1024,2048]{1,0:T(8,128)(2,1)} %collective-permute-done.other_ref), custom_call_target="tpu_custom_call" | custom-call | tf_op jit(solution)/shard_map/pallas_call | solution.py:127
  11.4 6.9 %all-to-all-start.1 = ((bf16[16,64,512]{2,1,0:T(8,128)(2,1)}), bf16[16,64,512]{2,1,0:T(8,128)(2,1)}, u32[]{:S(2)}, u32[]{:S(2)}) async-start(bf16[16,64,512]{2,1,0:T(8,128)(2,1)} %shard_map.61), calls=%async_computation.1 | async-start | bytes 2097152 | tf_op jit(solution)/shard_map/all_to_all | solution.py:355
  18.4 2.9 %shard_map.59 = bf16[16,64,512]{2,1,0:T(8,128)(2,1)} custom-call(s32[32]{0:T(128)} %get-tuple-element.19.sel_ref, s32[32]{0:T(128)} %get-tuple-element.20.jsel_ref, s32[2]{0:T(128)} %pad_add_fusion.pos_ref, bf16[1024,2048]{1,0:T(8,128)(2,1)} %own_ref.5, bf16[1024,2048]{1,0:T(8,128)(2,1)} %collective-permute-done.other_ref), custom_call_target="tpu_custom_call" | custom-call | tf_op jit(solution)/shard_map/pallas_call | solution.py:127
  21.2 11.3 %all-to-all-done.1.in_ref = bf16[16,64,512]{2,1,0:T(8,128)(2,1)} async-done(((bf16[16,64,512]{2,1,0:T(8,128)(2,1)}), bf16[16,64,512]{2,1,0:T(8,128)(2,1)}, u32[]{:S(2)}, u32[]{:S(2)}) %all-to-all-start.1) | async-done | bytes 1048608 | tf_op jit(solution)/shard_map/all_to_all | solution.py:355
  32.5 6.1 %all-to-all-start = ((bf16[16,64,512]{2,1,0:T(8,128)(2,1)}), bf16[16,64,512]{2,1,0:T(8,128)(2,1)}, u32[]{:S(2)}, u32[]{:S(2)}) async-start(bf16[16,64,512]{2,1,0:T(8,128)(2,1)} %shard_map.59), calls=%async_computation | async-start | bytes 2097152 | tf_op jit(solution)/shard_map/all_to_all | solution.py:355
  38.6 3.6 %shard_map.63 = bf16[16,128,512]{2,1,0:T(8,128)(2,1)} custom-call(s32[32]{0:T(128)} %get-tuple-element.19.sel_ref, s32[32]{0:T(128)} %get-tuple-element.20.jsel_ref, s32[2]{0:T(128)} %pad_add_fusion.pos_ref, bf16[1024,2048]{1,0:T(8,128)(2,1)} %own_ref.5, bf16[1024,2048]{1,0:T(8,128)(2,1)} %collective-permute-done.other_ref), custom_call_target="tpu_custom_call" | custom-call | tf_op jit(solution)/shard_map/pallas_call | solution.py:127
  42.2 9.1 %all-to-all-done.in_ref = bf16[16,64,512]{2,1,0:T(8,128)(2,1)} async-done(((bf16[16,64,512]{2,1,0:T(8,128)(2,1)}), bf16[16,64,512]{2,1,0:T(8,128)(2,1)}, u32[]{:S(2)}, u32[]{:S(2)}) %all-to-all-start) | async-done | bytes 1048608 | tf_op jit(solution)/shard_map/all_to_all | solution.py:355
  51.3 7.1 %all-to-all-start.2 = ((bf16[16,128,512]{2,1,0:T(8,128)(2,1)}), bf16[16,128,512]{2,1,0:T(8,128)(2,1)}, u32[]{:S(2)}, u32[]{:S(2)}) async-start(bf16[16,128,512]{2,1,0:T(8,128)(2,1)} %shard_map.63), calls=%async_computation.2 | async-start | bytes 4194304 | tf_op jit(solution)/shard_map/all_to_all | solution.py:355
  58.4 2.8 %shard_map.62 = (bf16[4,64,512]{2,1,0:T(8,128)(2,1)}, bf16[4,64,512]{2,1,0:T(8,128)(2,1)}, bf16[8,64,512]{2,1,0:T(8,128)(2,1)}) custom-call(s32[48]{0:T(128)} %get-tuple-element.18.jl_ref, s32[2]{0:T(128)} %pad_add_fusion.pos_ref, bf16[16,64,512]{2,1,0:T(8,128)(2,1)} %all-to-all-done.1.in_ref), custom_call_target="tpu_custom_call" | custom-call | tf_op jit(solution)/shard_map/pallas_call | solution.py:151
  61.2 5.1 %collective-permute-start.5 = (bf16[8,64,512]{2,1,0:T(8,128)(2,1)}, bf16[8,64,512]{2,1,0:T(8,128)(2,1)S(1)}, u32[]{:S(2)}, u32[]{:S(2)}) collective-permute-start(bf16[8,64,512]{2,1,0:T(8,128)(2,1)} %get-tuple-element.26), channel_id=1, source_target_pairs={{0,8},{4,12},{8,0},{12,4},{1,9},{5,13},{9,1},{13,5},{2,10},{6,14},... | collective-permute-start | bytes 1572872 | tf_op jit(solution)/shard_map/ppermute | solution.py:340
  66.3 2.8 %shard_map.60 = (bf16[4,64,512]{2,1,0:T(8,128)(2,1)}, bf16[4,64,512]{2,1,0:T(8,128)(2,1)}, bf16[8,64,512]{2,1,0:T(8,128)(2,1)}) custom-call(s32[48]{0:T(128)} %get-tuple-element.18.jl_ref, s32[2]{0:T(128)} %pad_add_fusion.pos_ref, bf16[16,64,512]{2,1,0:T(8,128)(2,1)} %all-to-all-done.in_ref), custom_call_target="tpu_custom_call" | custom-call | tf_op jit(solution)/shard_map/pallas_call | solution.py:151
  69.1 0.3 collective-permute-start.2
  69.3 31.7 %collective-permute-done.5.refs_6_ = bf16[8,64,512]{2,1,0:T(8,128)(2,1)S(1)} collective-permute-done((bf16[8,64,512]{2,1,0:T(8,128)(2,1)}, bf16[8,64,512]{2,1,0:T(8,128)(2,1)S(1)}, u32[]{:S(2)}, u32[]{:S(2)}) %collective-permute-start.5) | collective-permute-done | bytes 524320 | tf_op jit(solution)/shard_map/ppermute | solution.py:340
  101.0 0.0 copy-start
  101.0 2.0 collective-permute-start.6
  103.0 9.3 %collective-permute-done.2.refs_2_ = bf16[8,64,512]{2,1,0:T(8,128)(2,1)} collective-permute-done((bf16[8,64,512]{2,1,0:T(8,128)(2,1)}, bf16[8,64,512]{2,1,0:T(8,128)(2,1)}, u32[]{:S(2)}, u32[]{:S(2)}) %collective-permute-start.2) | collective-permute-done | bytes 524320 | tf_op jit(solution)/shard_map/ppermute | solution.py:340
  112.3 1.3 collective-permute-start.3
  113.6 0.0 all-to-all-done.2.in_ref
  113.6 3.7 %shard_map.64 = (bf16[4,128,512]{2,1,0:T(8,128)(2,1)}, bf16[4,128,512]{2,1,0:T(8,128)(2,1)}, bf16[8,128,512]{2,1,0:T(8,128)(2,1)}) custom-call(s32[48]{0:T(128)} %get-tuple-element.18.jl_ref, s32[2]{0:T(128)} %pad_add_fusion.pos_ref, bf16[16,128,512]{2,1,0:T(8,128)(2,1)} %all-to-all-done.2.in_ref), custom_call_target="tpu_custom_call" | custom-call | tf_op jit(solution)/shard_map/pallas_call | solution.py:151
  117.3 4.7 %collective-permute-start.8 = (bf16[8,128,512]{2,1,0:T(8,128)(2,1)}, bf16[8,128,512]{2,1,0:T(8,128)(2,1)}, u32[]{:S(2)}, u32[]{:S(2)}) collective-permute-start(bf16[8,128,512]{2,1,0:T(8,128)(2,1)} %get-tuple-element.29), channel_id=1, source_target_pairs={{0,8},{4,12},{8,0},{12,4},{1,9},{5,13},{9,1},{13,5},{2,10},{6,14},... | collective-permute-start | bytes 3145736 | tf_op jit(solution)/shard_map/ppermute | solution.py:340
  122.0 0.3 collective-permute-start.4
  122.2 0.2 collective-permute-start.1
  122.5 1.2 collective-permute-done.4.refs_5_
  123.7 0.4 collective-permute-done.1.refs_1_
  124.1 0.0 collective-permute-done.6.refs_7_
  124.1 0.7 copy-done.3
  124.8 0.0 collective-permute-done.3.refs_3_
  124.8 0.0 copy-done
  124.8 0.0 copy-done.2
  124.8 4.3 %strip_panel.1 = bf16[640,256]{1,0:T(8,128)(2,1)} custom-call(s32[16]{0:T(128)} %get-tuple-element.16.krow_ref, s32[48]{0:T(128)} %get-tuple-element.17.kcol_ref, bf16[4,64,512]{2,1,0:T(8,128)(2,1)} %get-tuple-element.21.refs_0_, bf16[4,64,512]{2,1,0:T(8,128)(2,1)} %copy-done.3, bf16[8,64,512]{2,1,0:T(8,128)(2,1)} %collective-permute-done.2.refs_2_, ...), custom_call_target="tpu_custom_call" | custom-call | tf_op jit(solution)/shard_map/strip_panel/pallas_call | solution.py:226
  129.1 3.1 %collective-permute-start.10 = (bf16[640,256]{1,0:T(8,128)(2,1)}, bf16[640,256]{1,0:T(8,128)(2,1)S(1)}, u32[]{:S(2)}, u32[]{:S(2)}) collective-permute-start(bf16[640,256]{1,0:T(8,128)(2,1)} %strip_panel.1), channel_id=1, source_target_pairs={{0,1},{4,5},{8,9},{12,13},{16,17},{20,21},{24,25},{28,29},{32,33},... | collective-permute-start | bytes 983048 | tf_op jit(solution)/shard_map/ppermute | solution.py:336
  132.2 2.2 %collective-permute-start.11 = (bf16[640,256]{1,0:T(8,128)(2,1)}, bf16[640,256]{1,0:T(8,128)(2,1)S(1)}, u32[]{:S(2)}, u32[]{:S(2)}) collective-permute-start(bf16[640,256]{1,0:T(8,128)(2,1)} %strip_panel.1), channel_id=1, source_target_pairs={{0,2},{4,6},{8,10},{12,14},{16,18},{20,22},{24,26},{28,30},{32,34}... | collective-permute-start | bytes 983048 | tf_op jit(solution)/shard_map/ppermute | solution.py:336
  134.4 1.3 collective-permute-start.12
  135.7 1.9 collective-permute-start.13
  137.6 1.6 collective-permute-done.10
  139.3 12.6 %collective-permute-start.14 = (bf16[640,256]{1,0:T(8,128)(2,1)}, bf16[640,256]{1,0:T(8,128)(2,1)S(1)}, u32[]{:S(2)}, u32[]{:S(2)}) collective-permute-start(bf16[640,256]{1,0:T(8,128)(2,1)} %strip_panel.1), channel_id=1, source_target_pairs={{0,32},{4,36},{8,40},{12,44},{16,49},{20,53},{24,57},{28,61},{32,2... | collective-permute-start | bytes 983048 | tf_op jit(solution)/shard_map/ppermute | solution.py:336
  151.9 0.0 collective-permute-done.11
  151.9 1.3 collective-permute-start.15
  153.2 15.9 %collective-permute-done.8.refs_10_ = bf16[8,128,512]{2,1,0:T(8,128)(2,1)} collective-permute-done((bf16[8,128,512]{2,1,0:T(8,128)(2,1)}, bf16[8,128,512]{2,1,0:T(8,128)(2,1)}, u32[]{:S(2)}, u32[]{:S(2)}) %collective-permute-start.8) | collective-permute-done | bytes 1048608 | tf_op jit(solution)/shard_map/ppermute | solution.py:340
  169.1 0.6 collective-permute-start.9
  169.7 0.0 collective-permute-done.12
  169.7 0.0 collective-permute-done.13
  169.7 0.0 collective-permute-done.14
  169.7 0.0 collective-permute-done.15
  169.7 1.8 add_select_fusion
  171.5 4.2 %collective-permute-start.17 = (bf16[640,256]{1,0:T(8,128)(2,1)S(1)}, bf16[640,256]{1,0:T(8,128)(2,1)}, u32[]{:S(2)}, u32[]{:S(2)}) collective-permute-start(bf16[640,256]{1,0:T(8,128)(2,1)S(1)} %get-tuple-element.30.refs_14_), channel_id=1, source_target_pairs={{0,8},{4,12},{8,0},{12,4},{1,9},{5,13},{9,1},{13,5},{2,10},{6,14},... | collective-permute-start | bytes 983048 | tf_op jit(solution)/shard_map/ppermute | solution.py:340
  175.8 0.3 collective-permute-start.7
  176.1 0.2 collective-permute-start.16
  176.3 16.0 %collective-permute-done.17.own_ref = bf16[640,256]{1,0:T(8,128)(2,1)} collective-permute-done((bf16[640,256]{1,0:T(8,128)(2,1)S(1)}, bf16[640,256]{1,0:T(8,128)(2,1)}, u32[]{:S(2)}, u32[]{:S(2)}) %collective-permute-start.17) | collective-permute-done | bytes 327712 | tf_op jit(solution)/shard_map/ppermute | solution.py:340
  192.3 0.6 collective-permute-start.18
  192.9 0.0 collective-permute-done.7.refs_9_
  192.9 0.0 collective-permute-done.16.refs_15_
  192.9 0.0 copy-start.5
  192.9 0.7 copy-done.5
  193.6 0.0 collective-permute-done.9.refs_11_
  193.6 0.0 copy-done.1
  193.6 0.2 copy-done.4
  193.8 9.8 %assemble.1.front_ref = bf16[640,2560]{1,0:T(8,128)(2,1)} custom-call(s32[2]{0:T(128)} %pad_add_fusion.pos_ref, s32[16]{0:T(128)} %get-tuple-element.16.krow_ref, s32[48]{0:T(128)} %get-tuple-element.17.kcol_ref, bf16[4,64,512]{2,1,0:T(8,128)(2,1)} %get-tuple-element.21.refs_0_, bf16[4,64,512]{2,1,0:T(8,128)(2,1)} %copy-done.3, ...), custom_call_target="tpu_custom_call" | custom-call | tf_op jit(solution)/shard_map/assemble/pallas_call | solution.py:275
  203.6 0.0 collective-permute-done.18.twin_ref
  203.6 4.0 %finish.1 = bf16[640,2560]{1,0:T(8,128)(2,1)} custom-call(s32[2]{0:T(128)} %pad_add_fusion.pos_ref, bf16[640,2560]{1,0:T(8,128)(2,1)} %assemble.1.front_ref, bf16[640,256]{1,0:T(8,128)(2,1)} %get-tuple-element.31.refs_13_.row_ref, bf16[640,256]{1,0:T(8,128)(2,1)} %collective-permute-done.17.own_ref, ...), custom_call_target="tpu_custom_call", output_to_operand_aliasing={{}: (1, {})} | custom-call | tf_op jit(solution)/shard_map/finish/pallas_call | solution.py:316
  (4 shorter events, 0.0 us)
Async XLA Ops:
  0.6 7.9 %collective-permute-start = (bf16[1024,2048]{1,0:T(8,128)(2,1)}, bf16[1024,2048]{1,0:T(8,128)(2,1)}, u32[]{:S(2)}, u32[]{:S(2)}) collective-permute-start(bf16[1024,2048]{1,0:T(8,128)(2,1)} %own_ref.5), channel_id=1, source_target_pairs={{0,4},{4,0},{8,12},{12,8},{1,5},{5,1},{9,13},{13,9},{2,6},{6,2},{1... | collective-permute-start | bytes 12582920 | tf_op jit(solution)/shard_map/ppermute | solution.py:340
  11.4 21.1 %all-to-all-start.1 = ((bf16[16,64,512]{2,1,0:T(8,128)(2,1)}), bf16[16,64,512]{2,1,0:T(8,128)(2,1)}, u32[]{:S(2)}, u32[]{:S(2)}) async-start(bf16[16,64,512]{2,1,0:T(8,128)(2,1)} %shard_map.61), calls=%async_computation.1 | async-start | bytes 2097152 | tf_op jit(solution)/shard_map/all_to_all | solution.py:355
  32.5 18.8 %all-to-all-start = ((bf16[16,64,512]{2,1,0:T(8,128)(2,1)}), bf16[16,64,512]{2,1,0:T(8,128)(2,1)}, u32[]{:S(2)}, u32[]{:S(2)}) async-start(bf16[16,64,512]{2,1,0:T(8,128)(2,1)} %shard_map.59), calls=%async_computation | async-start | bytes 2097152 | tf_op jit(solution)/shard_map/all_to_all | solution.py:355
  51.3 62.3 %all-to-all-start.2 = ((bf16[16,128,512]{2,1,0:T(8,128)(2,1)}), bf16[16,128,512]{2,1,0:T(8,128)(2,1)}, u32[]{:S(2)}, u32[]{:S(2)}) async-start(bf16[16,128,512]{2,1,0:T(8,128)(2,1)} %shard_map.63), calls=%async_computation.2 | async-start | bytes 4194304 | tf_op jit(solution)/shard_map/all_to_all | solution.py:355
  61.2 39.8 %collective-permute-start.5 = (bf16[8,64,512]{2,1,0:T(8,128)(2,1)}, bf16[8,64,512]{2,1,0:T(8,128)(2,1)S(1)}, u32[]{:S(2)}, u32[]{:S(2)}) collective-permute-start(bf16[8,64,512]{2,1,0:T(8,128)(2,1)} %get-tuple-element.26), channel_id=1, source_target_pairs={{0,8},{4,12},{8,0},{12,4},{1,9},{5,13},{9,1},{13,5},{2,10},{6,14},... | collective-permute-start | bytes 1572872 | tf_op jit(solution)/shard_map/ppermute | solution.py:340
  69.1 43.3 %collective-permute-start.2 = (bf16[8,64,512]{2,1,0:T(8,128)(2,1)}, bf16[8,64,512]{2,1,0:T(8,128)(2,1)}, u32[]{:S(2)}, u32[]{:S(2)}) collective-permute-start(bf16[8,64,512]{2,1,0:T(8,128)(2,1)} %get-tuple-element.23), channel_id=1, source_target_pairs={{0,8},{4,12},{8,0},{12,4},{1,9},{5,13},{9,1},{13,5},{2,10},{6,14},... | collective-permute-start | bytes 1572872 | tf_op jit(solution)/shard_map/ppermute | solution.py:340
  101.0 23.8 %copy-start = (bf16[8,64,512]{2,1,0:T(8,128)(2,1)}, bf16[8,64,512]{2,1,0:T(8,128)(2,1)S(1)}, u32[]{:S(2)}) copy-start(bf16[8,64,512]{2,1,0:T(8,128)(2,1)S(1)} %collective-permute-done.5.refs_6_) | copy-start | bytes 1572868
  101.0 23.1 %collective-permute-start.6 = (bf16[8,64,512]{2,1,0:T(8,128)(2,1)S(1)}, bf16[8,64,512]{2,1,0:T(8,128)(2,1)}, u32[]{:S(2)}, u32[]{:S(2)}) collective-permute-start(bf16[8,64,512]{2,1,0:T(8,128)(2,1)S(1)} %collective-permute-done.5.refs_6_), channel_id=1, source_target_pairs={{0,4},{4,0},{8,12},{12,8},{1,5},{5,1},{9,13},{13,9},{2,6},{6,2},{1... | collective-permute-start | bytes 1572872 | tf_op jit(solution)/shard_map/ppermute | solution.py:340
  112.3 12.4 %collective-permute-start.3 = (bf16[8,64,512]{2,1,0:T(8,128)(2,1)}, bf16[8,64,512]{2,1,0:T(8,128)(2,1)}, u32[]{:S(2)}, u32[]{:S(2)}) collective-permute-start(bf16[8,64,512]{2,1,0:T(8,128)(2,1)} %collective-permute-done.2.refs_2_), channel_id=1, source_target_pairs={{0,4},{4,0},{8,12},{12,8},{1,5},{5,1},{9,13},{13,9},{2,6},{6,2},{1... | collective-permute-start | bytes 1572872 | tf_op jit(solution)/shard_map/ppermute | solution.py:340
  117.3 51.8 %collective-permute-start.8 = (bf16[8,128,512]{2,1,0:T(8,128)(2,1)}, bf16[8,128,512]{2,1,0:T(8,128)(2,1)}, u32[]{:S(2)}, u32[]{:S(2)}) collective-permute-start(bf16[8,128,512]{2,1,0:T(8,128)(2,1)} %get-tuple-element.29), channel_id=1, source_target_pairs={{0,8},{4,12},{8,0},{12,4},{1,9},{5,13},{9,1},{13,5},{2,10},{6,14},... | collective-permute-start | bytes 3145736 | tf_op jit(solution)/shard_map/ppermute | solution.py:340
  122.0 1.7 collective-permute-start.4
  122.2 1.8 collective-permute-start.1
  123.7 1.1 copy-start.2
  124.1 0.7 copy-start.3
  129.1 10.2 %collective-permute-start.10 = (bf16[640,256]{1,0:T(8,128)(2,1)}, bf16[640,256]{1,0:T(8,128)(2,1)S(1)}, u32[]{:S(2)}, u32[]{:S(2)}) collective-permute-start(bf16[640,256]{1,0:T(8,128)(2,1)} %strip_panel.1), channel_id=1, source_target_pairs={{0,1},{4,5},{8,9},{12,13},{16,17},{20,21},{24,25},{28,29},{32,33},... | collective-permute-start | bytes 983048 | tf_op jit(solution)/shard_map/ppermute | solution.py:336
  132.2 19.7 %collective-permute-start.11 = (bf16[640,256]{1,0:T(8,128)(2,1)}, bf16[640,256]{1,0:T(8,128)(2,1)S(1)}, u32[]{:S(2)}, u32[]{:S(2)}) collective-permute-start(bf16[640,256]{1,0:T(8,128)(2,1)} %strip_panel.1), channel_id=1, source_target_pairs={{0,2},{4,6},{8,10},{12,14},{16,18},{20,22},{24,26},{28,30},{32,34}... | collective-permute-start | bytes 983048 | tf_op jit(solution)/shard_map/ppermute | solution.py:336
  134.4 35.3 %collective-permute-start.12 = (bf16[640,256]{1,0:T(8,128)(2,1)}, bf16[640,256]{1,0:T(8,128)(2,1)S(1)}, u32[]{:S(2)}, u32[]{:S(2)}) collective-permute-start(bf16[640,256]{1,0:T(8,128)(2,1)} %strip_panel.1), channel_id=1, source_target_pairs={{0,3},{4,7},{8,11},{12,15},{16,19},{20,23},{24,27},{28,31},{32,35}... | collective-permute-start | bytes 983048 | tf_op jit(solution)/shard_map/ppermute | solution.py:336
  135.7 34.0 %collective-permute-start.13 = (bf16[640,256]{1,0:T(8,128)(2,1)}, bf16[640,256]{1,0:T(8,128)(2,1)S(1)}, u32[]{:S(2)}, u32[]{:S(2)}) collective-permute-start(bf16[640,256]{1,0:T(8,128)(2,1)} %strip_panel.1), channel_id=1, source_target_pairs={{0,16},{4,20},{8,24},{12,28},{16,33},{20,37},{24,41},{28,45},{32,5... | collective-permute-start | bytes 983048 | tf_op jit(solution)/shard_map/ppermute | solution.py:336
  139.3 30.5 %collective-permute-start.14 = (bf16[640,256]{1,0:T(8,128)(2,1)}, bf16[640,256]{1,0:T(8,128)(2,1)S(1)}, u32[]{:S(2)}, u32[]{:S(2)}) collective-permute-start(bf16[640,256]{1,0:T(8,128)(2,1)} %strip_panel.1), channel_id=1, source_target_pairs={{0,32},{4,36},{8,40},{12,44},{16,49},{20,53},{24,57},{28,61},{32,2... | collective-permute-start | bytes 983048 | tf_op jit(solution)/shard_map/ppermute | solution.py:336
  151.9 17.8 %collective-permute-start.15 = (bf16[640,256]{1,0:T(8,128)(2,1)}, bf16[640,256]{1,0:T(8,128)(2,1)S(1)}, u32[]{:S(2)}, u32[]{:S(2)}) collective-permute-start(bf16[640,256]{1,0:T(8,128)(2,1)} %strip_panel.1), channel_id=1, source_target_pairs={{0,48},{4,52},{8,56},{12,60},{16,1},{20,5},{24,9},{28,13},{32,18},... | collective-permute-start | bytes 983048 | tf_op jit(solution)/shard_map/ppermute | solution.py:336
  169.1 24.5 %collective-permute-start.9 = (bf16[8,128,512]{2,1,0:T(8,128)(2,1)}, bf16[8,128,512]{2,1,0:T(8,128)(2,1)}, u32[]{:S(2)}, u32[]{:S(2)}) collective-permute-start(bf16[8,128,512]{2,1,0:T(8,128)(2,1)} %collective-permute-done.8.refs_10_), channel_id=1, source_target_pairs={{0,4},{4,0},{8,12},{12,8},{1,5},{5,1},{9,13},{13,9},{2,6},{6,2},{1... | collective-permute-start | bytes 3145736 | tf_op jit(solution)/shard_map/ppermute | solution.py:340
  171.5 22.1 %copy-start.1 = (bf16[640,256]{1,0:T(8,128)(2,1)}, bf16[640,256]{1,0:T(8,128)(2,1)S(1)}, u32[]{:S(2)}) copy-start(bf16[640,256]{1,0:T(8,128)(2,1)S(1)} %get-tuple-element.30.refs_14_) | copy-start | bytes 983044
  171.5 20.7 %collective-permute-start.17 = (bf16[640,256]{1,0:T(8,128)(2,1)S(1)}, bf16[640,256]{1,0:T(8,128)(2,1)}, u32[]{:S(2)}, u32[]{:S(2)}) collective-permute-start(bf16[640,256]{1,0:T(8,128)(2,1)S(1)} %get-tuple-element.30.refs_14_), channel_id=1, source_target_pairs={{0,8},{4,12},{8,0},{12,4},{1,9},{5,13},{9,1},{13,5},{2,10},{6,14},... | collective-permute-start | bytes 983048 | tf_op jit(solution)/shard_map/ppermute | solution.py:340
  175.8 17.1 %collective-permute-start.7 = (bf16[4,128,512]{2,1,0:T(8,128)(2,1)}, bf16[4,128,512]{2,1,0:T(8,128)(2,1)S(1)}, u32[]{:S(2)}, u32[]{:S(2)}) collective-permute-start(bf16[4,128,512]{2,1,0:T(8,128)(2,1)} %get-tuple-element.28), channel_id=1, source_target_pairs={{0,4},{4,0},{8,12},{12,8},{1,5},{5,1},{9,13},{13,9},{2,6},{6,2},{1... | collective-permute-start | bytes 1572872 | tf_op jit(solution)/shard_map/ppermute | solution.py:340
  176.1 16.8 %collective-permute-start.16 = (bf16[640,256]{1,0:T(8,128)(2,1)S(1)}, bf16[640,256]{1,0:T(8,128)(2,1)S(1)}, u32[]{:S(2)}, u32[]{:S(2)}) collective-permute-start(bf16[640,256]{1,0:T(8,128)(2,1)S(1)} %get-tuple-element.30.refs_14_), channel_id=1, source_target_pairs={{0,4},{4,0},{8,12},{12,8},{1,5},{5,1},{9,13},{13,9},{2,6},{6,2},{1... | collective-permute-start | bytes 983048 | tf_op jit(solution)/shard_map/ppermute | solution.py:340
  192.3 11.3 %collective-permute-start.18 = (bf16[640,256]{1,0:T(8,128)(2,1)}, bf16[640,256]{1,0:T(8,128)(2,1)}, u32[]{:S(2)}, u32[]{:S(2)}) collective-permute-start(bf16[640,256]{1,0:T(8,128)(2,1)} %collective-permute-done.17.own_ref), channel_id=1, source_target_pairs={{0,4},{4,0},{8,12},{12,8},{1,5},{5,1},{9,13},{13,9},{2,6},{6,2},{1... | collective-permute-start | bytes 983048 | tf_op jit(solution)/shard_map/ppermute | solution.py:340
  192.9 0.9 copy-start.4
  192.9 0.8 copy-start.5

commit v3 on v2

--- a/solution.py
+++ b/solution.py
@@ -12,7 +12,7 @@
 MB = 5
 QB = 20
 FB = 80
-CHUNKS = ((0, 0, 1), (0, 1, 2), (1, 0, 2))
+CHUNKS = ((0, 0, 1), (0, 1, 2), (1, 0, 1), (1, 1, 2))
 PLACES = [(x, z, core) for x in range(4) for z in range(2) for core in range(2)]
 
 
@@ -249,13 +249,13 @@
     rows, cols = front_orig.shape
 
     def kernel(pos_ref, krow_ref, kcol_ref, *refs):
-        orig_ref, row_ref, own_ref, twin_ref, out_ref, buf_ref, eye_ref, sem = refs[12:]
+        orig_ref, row_ref, own_ref, twin_ref, out_ref, buf_ref, eye_ref, sem = refs[16:]
         step = pl.program_id(0)
         first = ((pos_ref[0] % 4) ^ step) * (QB // 4)
 
         @pl.when(step == 0)
         def _():
-            gather(refs[:12], buf_ref, sem, lambda: fill_eyes(eye_ref))
+            gather(refs[:16], buf_ref, sem, lambda: fill_eyes(eye_ref))
 
         for q in range(QB // 4):
             side = slice(q * block, (q + 1) * block)
@@ -278,14 +278,14 @@
             num_scalar_prefetch=1,
             grid=(4,),
             in_specs=[pl.BlockSpec(memory_space=SMEM)] * 2
-            + [pl.BlockSpec(memory_space=pl.ANY)] * 12
+            + [pl.BlockSpec(memory_space=pl.ANY)] * 16
             + [turned]
             + [whole] * 3,
             out_specs=turned,
             scratch_shapes=[
                 pltpu.VMEM((32, block, 4 * block), jnp.bfloat16),
                 pltpu.VMEM((4, block, 2 * block), jnp.bfloat16),
-                pltpu.SemaphoreType.DMA((12,)),
+                pltpu.SemaphoreType.DMA((16,)),
             ],
         ),
         out_shape=jax.ShapeDtypeStruct(front_orig.shape, jnp.bfloat16),

time: 209 us -> 240 us (1.15)
  the two profiles are of different devices: /device:TPU:67 before, /device:TPU:1 now
where the time goes in v3:
time: 240 us; the launch traced here: 238 us
  starting transfers between devices  122 us (51%)
  waiting for transfers between devices  65.5 us (27%)
  Pallas kernels  45.9 us (19%)
  other arithmetic  2.95 us (1%)
    ppermute x16, starting transfers between devices, over_zk(): return lax.ppermute(array, ('z', 'core'), [(r, r ^ d) for r in range(4)])  81.6 us
    ppermute x16, waiting for transfers between devices, over_zk(): return lax.ppermute(array, ('z', 'core'), [(r, r ^ d) for r in range(4)])  34.9 us
    all_to_all x4, waiting for transfers between devices, local(): part = lax.all_to_all(sent, ('x', 'col'), 0, 0, tiled=True)  24.3 us
    all_to_all x4, starting transfers between devices, local(): part = lax.all_to_all(sent, ('x', 'col'), 0, 0, tiled=True)  21.7 us
    ppermute x6, starting transfers between devices, moved(): return lax.ppermute(array, ('x', 'z', 'core', 'col'), pairs)  18.2 us
    pallas_call x4, Pallas kernels, pack_first(): pl.pallas_call(kernel, out_shape=jax.ShapeDtypeStruct((16, last - first,...  11.6 us
    pallas_call x4, Pallas kernels, pack_second(): pl.pallas_call(kernel, out_shape=[jax.ShapeDtypeStruct((n,) + arrived.sha...  11.3 us
    pallas_call x1, Pallas kernels, assemble(): pl.pallas_call(kernel, grid_spec=pltpu.PrefetchScalarGridSpec(num_scalar_...  9.81 us
  transfers between devices with their start and end apart: 26, of which 11 were waited for; matrix products, arithmetic and copies ran while one was open for 1% of the time, Pallas kernels for 16%

profile of v3, /device:TPU:1, one launch (start us, length us, event | category | flops | bytes accessed | tf_op | source)
XLA Modules:
  0.0 238.4 jit_solution(5612306900888109255)
XLA Ops:
  0.6 3.3 %collective-permute-start = (bf16[1024,2048]{1,0:T(8,128)(2,1)}, bf16[1024,2048]{1,0:T(8,128)(2,1)}, u32[]{:S(2)}, u32[]{:S(2)}) collective-permute-start(bf16[1024,2048]{1,0:T(8,128)(2,1)} %own_ref.7), channel_id=1, source_target_pairs={{0,4},{4,0},{8,12},{12,8},{1,5},{5,1},{9,13},{13,9},{2,6},{6,2},{1... | collective-permute-start | bytes 12582920 | tf_op jit(solution)/shard_map/ppermute | solution.py:340
  3.9 0.6 pad_add_fusion.pos_ref
  4.5 5.0 %tables.1 = (s32[32]{0:T(128)}, s32[32]{0:T(128)}, s32[48]{0:T(128)}, s32[16]{0:T(128)}, s32[48]{0:T(128)}) custom-call(s32[2,64]{1,0:T(2,128)} %map_ref.1, s32[2]{0:T(128)} %pad_add_fusion.pos_ref), custom_call_target="tpu_custom_call" | custom-call | tf_op jit(solution)/shard_map/tables/pallas_call | solution.py:90
  9.5 1.6 collective-permute-done.other_ref
  11.0 2.9 %shard_map.59 = bf16[16,64,512]{2,1,0:T(8,128)(2,1)} custom-call(s32[32]{0:T(128)} %get-tuple-element.22.sel_ref, s32[32]{0:T(128)} %get-tuple-element.23.jsel_ref, s32[2]{0:T(128)} %pad_add_fusion.pos_ref, bf16[1024,2048]{1,0:T(8,128)(2,1)} %own_ref.7, bf16[1024,2048]{1,0:T(8,128)(2,1)} %collective-permute-done.other_ref), custom_call_target="tpu_custom_call" | custom-call | tf_op jit(solution)/shard_map/pallas_call | solution.py:127
  13.9 5.1 %all-to-all-start = ((bf16[16,64,512]{2,1,0:T(8,128)(2,1)}), bf16[16,64,512]{2,1,0:T(8,128)(2,1)}, u32[]{:S(2)}, u32[]{:S(2)}) async-start(bf16[16,64,512]{2,1,0:T(8,128)(2,1)} %shard_map.59), calls=%async_computation | async-start | bytes 2097152 | tf_op jit(solution)/shard_map/all_to_all | solution.py:355
  19.1 2.9 %shard_map.61 = bf16[16,64,512]{2,1,0:T(8,128)(2,1)} custom-call(s32[32]{0:T(128)} %get-tuple-element.22.sel_ref, s32[32]{0:T(128)} %get-tuple-element.23.jsel_ref, s32[2]{0:T(128)} %pad_add_fusion.pos_ref, bf16[1024,2048]{1,0:T(8,128)(2,1)} %own_ref.7, bf16[1024,2048]{1,0:T(8,128)(2,1)} %collective-permute-done.other_ref), custom_call_target="tpu_custom_call" | custom-call | tf_op jit(solution)/shard_map/pallas_call | solution.py:127
  22.0 12.8 %all-to-all-done.in_ref = bf16[16,64,512]{2,1,0:T(8,128)(2,1)} async-done(((bf16[16,64,512]{2,1,0:T(8,128)(2,1)}), bf16[16,64,512]{2,1,0:T(8,128)(2,1)}, u32[]{:S(2)}, u32[]{:S(2)}) %all-to-all-start) | async-done | bytes 1048608 | tf_op jit(solution)/shard_map/all_to_all | solution.py:355
  34.8 4.6 %all-to-all-start.1 = ((bf16[16,64,512]{2,1,0:T(8,128)(2,1)}), bf16[16,64,512]{2,1,0:T(8,128)(2,1)}, u32[]{:S(2)}, u32[]{:S(2)}) async-start(bf16[16,64,512]{2,1,0:T(8,128)(2,1)} %shard_map.61), calls=%async_computation.1 | async-start | bytes 2097152 | tf_op jit(solution)/shard_map/all_to_all | solution.py:355
  39.3 2.9 %shard_map.63 = bf16[16,64,512]{2,1,0:T(8,128)(2,1)} custom-call(s32[32]{0:T(128)} %get-tuple-element.22.sel_ref, s32[32]{0:T(128)} %get-tuple-element.23.jsel_ref, s32[2]{0:T(128)} %pad_add_fusion.pos_ref, bf16[1024,2048]{1,0:T(8,128)(2,1)} %own_ref.7, bf16[1024,2048]{1,0:T(8,128)(2,1)} %collective-permute-done.other_ref), custom_call_target="tpu_custom_call" | custom-call | tf_op jit(solution)/shard_map/pallas_call | solution.py:127
  42.2 11.5 %all-to-all-done.1.in_ref = bf16[16,64,512]{2,1,0:T(8,128)(2,1)} async-done(((bf16[16,64,512]{2,1,0:T(8,128)(2,1)}), bf16[16,64,512]{2,1,0:T(8,128)(2,1)}, u32[]{:S(2)}, u32[]{:S(2)}) %all-to-all-start.1) | async-done | bytes 1048608 | tf_op jit(solution)/shard_map/all_to_all | solution.py:355
  53.7 5.3 %all-to-all-start.2 = ((bf16[16,64,512]{2,1,0:T(8,128)(2,1)}), bf16[16,64,512]{2,1,0:T(8,128)(2,1)}, u32[]{:S(2)}, u32[]{:S(2)}) async-start(bf16[16,64,512]{2,1,0:T(8,128)(2,1)} %shard_map.63), calls=%async_computation.2 | async-start | bytes 2097152 | tf_op jit(solution)/shard_map/all_to_all | solution.py:355
  59.1 2.8 %shard_map.60 = (bf16[4,64,512]{2,1,0:T(8,128)(2,1)}, bf16[4,64,512]{2,1,0:T(8,128)(2,1)}, bf16[8,64,512]{2,1,0:T(8,128)(2,1)}) custom-call(s32[48]{0:T(128)} %get-tuple-element.21.jl_ref, s32[2]{0:T(128)} %pad_add_fusion.pos_ref, bf16[16,64,512]{2,1,0:T(8,128)(2,1)} %all-to-all-done.in_ref), custom_call_target="tpu_custom_call" | custom-call | tf_op jit(solution)/shard_map/pallas_call | solution.py:151
  61.9 6.9 %collective-permute-start.2 = (bf16[8,64,512]{2,1,0:T(8,128)(2,1)}, bf16[8,64,512]{2,1,0:T(8,128)(2,1)S(1)}, u32[]{:S(2)}, u32[]{:S(2)}) collective-permute-start(bf16[8,64,512]{2,1,0:T(8,128)(2,1)} %get-tuple-element.26), channel_id=1, source_target_pairs={{0,8},{4,12},{8,0},{12,4},{1,9},{5,13},{9,1},{13,5},{2,10},{6,14},... | collective-permute-start | bytes 1572872 | tf_op jit(solution)/shard_map/ppermute | solution.py:340
  68.8 2.8 %shard_map.62 = (bf16[4,64,512]{2,1,0:T(8,128)(2,1)}, bf16[4,64,512]{2,1,0:T(8,128)(2,1)}, bf16[8,64,512]{2,1,0:T(8,128)(2,1)}) custom-call(s32[48]{0:T(128)} %get-tuple-element.21.jl_ref, s32[2]{0:T(128)} %pad_add_fusion.pos_ref, bf16[16,64,512]{2,1,0:T(8,128)(2,1)} %all-to-all-done.1.in_ref), custom_call_target="tpu_custom_call" | custom-call | tf_op jit(solution)/shard_map/pallas_call | solution.py:151
  71.6 0.0 collective-permute-start.5
  71.6 8.0 %collective-permute-done.2.refs_2_ = bf16[8,64,512]{2,1,0:T(8,128)(2,1)S(1)} collective-permute-done((bf16[8,64,512]{2,1,0:T(8,128)(2,1)}, bf16[8,64,512]{2,1,0:T(8,128)(2,1)S(1)}, u32[]{:S(2)}, u32[]{:S(2)}) %collective-permute-start.2) | collective-permute-done | bytes 524320 | tf_op jit(solution)/shard_map/ppermute | solution.py:340
  79.6 8.6 %collective-permute-start.3 = (bf16[8,64,512]{2,1,0:T(8,128)(2,1)S(1)}, bf16[8,64,512]{2,1,0:T(8,128)(2,1)}, u32[]{:S(2)}, u32[]{:S(2)}) collective-permute-start(bf16[8,64,512]{2,1,0:T(8,128)(2,1)S(1)} %collective-permute-done.2.refs_2_), channel_id=1, source_target_pairs={{0,4},{4,0},{8,12},{12,8},{1,5},{5,1},{9,13},{13,9},{2,6},{6,2},{1... | collective-permute-start | bytes 1572872 | tf_op jit(solution)/shard_map/ppermute | solution.py:340
  88.2 6.3 %collective-permute-done.5.refs_6_ = bf16[8,64,512]{2,1,0:T(8,128)(2,1)} collective-permute-done((bf16[8,64,512]{2,1,0:T(8,128)(2,1)}, bf16[8,64,512]{2,1,0:T(8,128)(2,1)}, u32[]{:S(2)}, u32[]{:S(2)}) %collective-permute-start.5) | collective-permute-done | bytes 524320 | tf_op jit(solution)/shard_map/ppermute | solution.py:340
  94.5 20.0 %collective-permute-start.6 = (bf16[8,64,512]{2,1,0:T(8,128)(2,1)}, bf16[8,64,512]{2,1,0:T(8,128)(2,1)}, u32[]{:S(2)}, u32[]{:S(2)}) collective-permute-start(bf16[8,64,512]{2,1,0:T(8,128)(2,1)} %collective-permute-done.5.refs_6_), channel_id=1, source_target_pairs={{0,4},{4,0},{8,12},{12,8},{1,5},{5,1},{9,13},{13,9},{2,6},{6,2},{1... | collective-permute-start | bytes 1572872 | tf_op jit(solution)/shard_map/ppermute | solution.py:340
  114.5 2.9 %shard_map.65 = bf16[16,64,512]{2,1,0:T(8,128)(2,1)} custom-call(s32[32]{0:T(128)} %get-tuple-element.22.sel_ref, s32[32]{0:T(128)} %get-tuple-element.23.jsel_ref, s32[2]{0:T(128)} %pad_add_fusion.pos_ref, bf16[1024,2048]{1,0:T(8,128)(2,1)} %own_ref.7, bf16[1024,2048]{1,0:T(8,128)(2,1)} %collective-permute-done.other_ref), custom_call_target="tpu_custom_call" | custom-call | tf_op jit(solution)/shard_map/pallas_call | solution.py:127
  117.4 0.0 all-to-all-done.2.in_ref
  117.4 6.7 %all-to-all-start.3 = ((bf16[16,64,512]{2,1,0:T(8,128)(2,1)}), bf16[16,64,512]{2,1,0:T(8,128)(2,1)}, u32[]{:S(2)}, u32[]{:S(2)}) async-start(bf16[16,64,512]{2,1,0:T(8,128)(2,1)} %shard_map.65), calls=%async_computation.3 | async-start | bytes 2097152 | tf_op jit(solution)/shard_map/all_to_all | solution.py:355
  124.1 0.4 collective-permute-start.1
  124.4 0.2 collective-permute-start.4
  124.7 1.2 collective-permute-done.1.refs_1_
  125.9 0.4 collective-permute-done.4.refs_5_
  126.3 0.0 collective-permute-done.3.refs_3_
  126.3 0.7 copy-done.3
  127.0 4.2 %strip_panel.1 = bf16[640,256]{1,0:T(8,128)(2,1)} custom-call(s32[16]{0:T(128)} %get-tuple-element.19.krow_ref, s32[48]{0:T(128)} %get-tuple-element.20.kcol_ref, bf16[4,64,512]{2,1,0:T(8,128)(2,1)} %get-tuple-element.24.refs_0_, bf16[4,64,512]{2,1,0:T(8,128)(2,1)} %copy-done.2, bf16[8,64,512]{2,1,0:T(8,128)(2,1)} %copy-done, ...), custom_call_target="tpu_custom_call" | custom-call | tf_op jit(solution)/shard_map/strip_panel/pallas_call | solution.py:226
  131.2 5.3 %collective-permute-start.18 = (bf16[640,256]{1,0:T(8,128)(2,1)}, bf16[640,256]{1,0:T(8,128)(2,1)}, u32[]{:S(2)}, u32[]{:S(2)}) collective-permute-start(bf16[640,256]{1,0:T(8,128)(2,1)} %strip_panel.1), channel_id=1, source_target_pairs={{0,48},{4,52},{8,56},{12,60},{16,1},{20,5},{24,9},{28,13},{32,18},... | collective-permute-start | bytes 983048 | tf_op jit(solution)/shard_map/ppermute | solution.py:336
  136.5 1.9 collective-permute-start.16
  138.4 5.0 %collective-permute-start.17 = (bf16[640,256]{1,0:T(8,128)(2,1)}, bf16[640,256]{1,0:T(8,128)(2,1)}, u32[]{:S(2)}, u32[]{:S(2)}) collective-permute-start(bf16[640,256]{1,0:T(8,128)(2,1)} %strip_panel.1), channel_id=1, source_target_pairs={{0,32},{4,36},{8,40},{12,44},{16,49},{20,53},{24,57},{28,61},{32,2... | collective-permute-start | bytes 983048 | tf_op jit(solution)/shard_map/ppermute | solution.py:336
  143.4 2.0 collective-permute-start.15
  145.5 2.0 collective-permute-start.13
  147.5 0.0 collective-permute-done.18
  147.5 2.0 collective-permute-start.14
  149.5 2.8 %shard_map.64 = (bf16[4,64,512]{2,1,0:T(8,128)(2,1)}, bf16[4,64,512]{2,1,0:T(8,128)(2,1)}, bf16[8,64,512]{2,1,0:T(8,128)(2,1)}) custom-call(s32[48]{0:T(128)} %get-tuple-element.21.jl_ref, s32[2]{0:T(128)} %pad_add_fusion.pos_ref, bf16[16,64,512]{2,1,0:T(8,128)(2,1)} %all-to-all-done.2.in_ref), custom_call_target="tpu_custom_call" | custom-call | tf_op jit(solution)/shard_map/pallas_call | solution.py:151
  152.3 2.8 %shard_map.66 = (bf16[4,64,512]{2,1,0:T(8,128)(2,1)}, bf16[4,64,512]{2,1,0:T(8,128)(2,1)}, bf16[8,64,512]{2,1,0:T(8,128)(2,1)}) custom-call(s32[48]{0:T(128)} %get-tuple-element.21.jl_ref, s32[2]{0:T(128)} %pad_add_fusion.pos_ref, bf16[16,64,512]{2,1,0:T(8,128)(2,1)} %all-to-all-done.3.in_ref), custom_call_target="tpu_custom_call" | custom-call | tf_op jit(solution)/shard_map/pallas_call | solution.py:151
  155.1 6.2 %collective-permute-start.8 = (bf16[8,64,512]{2,1,0:T(8,128)(2,1)}, bf16[8,64,512]{2,1,0:T(8,128)(2,1)S(1)}, u32[]{:S(2)}, u32[]{:S(2)}) collective-permute-start(bf16[8,64,512]{2,1,0:T(8,128)(2,1)} %get-tuple-element.32), channel_id=1, source_target_pairs={{0,8},{4,12},{8,0},{12,4},{1,9},{5,13},{9,1},{13,5},{2,10},{6,14},... | collective-permute-start | bytes 1572872 | tf_op jit(solution)/shard_map/ppermute | solution.py:340
  161.3 0.3 collective-permute-start.11
  161.6 0.0 collective-permute-done.15
  161.6 0.0 collective-permute-done.13
  161.6 6.2 %collective-permute-done.14 = bf16[640,256]{1,0:T(8,128)(2,1)} collective-permute-done((bf16[640,256]{1,0:T(8,128)(2,1)}, bf16[640,256]{1,0:T(8,128)(2,1)}, u32[]{:S(2)}, u32[]{:S(2)}) %collective-permute-start.14) | collective-permute-done | bytes 327712 | tf_op jit(solution)/shard_map/ppermute | solution.py:336
  167.8 2.4 %add_select_fusion = (bf16[640,256]{1,0:T(8,128)(2,1)S(1)}, bf16[640,256]{1,0:T(8,128)(2,1)}) fusion(bf16[640,256]{1,0:T(8,128)(2,1)} %collective-permute-done.18, bf16[640,256]{1,0:T(8,128)(2,1)} %copy-done.9, bf16[640,256]{1,0:T(8,128)(2,1)} %collective-permute-done.17, pred[]{:T(512)S(6)} %eq.7, bf16[640,256]{1,0:T(8,128)(2,1)} %strip_panel.1, ...), kind=kLoop, calls=%fused_computation | loop fusion | flops 983040 | bytes 2949122 | tf_op jit(solution)/shard_map/jit(_where)/select_n | solution.py:372
  170.2 6.1 %collective-permute-start.20 = (bf16[640,256]{1,0:T(8,128)(2,1)S(1)}, bf16[640,256]{1,0:T(8,128)(2,1)}, u32[]{:S(2)}, u32[]{:S(2)}) collective-permute-start(bf16[640,256]{1,0:T(8,128)(2,1)S(1)} %get-tuple-element.36.refs_18_), channel_id=1, source_target_pairs={{0,8},{4,12},{8,0},{12,4},{1,9},{5,13},{9,1},{13,5},{2,10},{6,14},... | collective-permute-start | bytes 983048 | tf_op jit(solution)/shard_map/ppermute | solution.py:340
  176.4 1.5 collective-permute-start.7
  177.8 0.0 collective-permute-done.8.refs_10_
  177.8 0.1 collective-permute-start.9
  177.9 10.0 %collective-permute-done.11.refs_14_ = bf16[8,64,512]{2,1,0:T(8,128)(2,1)S(1)} collective-permute-done((bf16[8,64,512]{2,1,0:T(8,128)(2,1)}, bf16[8,64,512]{2,1,0:T(8,128)(2,1)S(1)}, u32[]{:S(2)}, u32[]{:S(2)}) %collective-permute-start.11) | collective-permute-done | bytes 524320 | tf_op jit(solution)/shard_map/ppermute | solution.py:340
  187.9 3.9 %collective-permute-start.12 = (bf16[8,64,512]{2,1,0:T(8,128)(2,1)S(1)}, bf16[8,64,512]{2,1,0:T(8,128)(2,1)S(1)}, u32[]{:S(2)}, u32[]{:S(2)}) collective-permute-start(bf16[8,64,512]{2,1,0:T(8,128)(2,1)S(1)} %collective-permute-done.11.refs_14_), channel_id=1, source_target_pairs={{0,4},{4,0},{8,12},{12,8},{1,5},{5,1},{9,13},{13,9},{2,6},{6,2},{1... | collective-permute-start | bytes 1572872 | tf_op jit(solution)/shard_map/ppermute | solution.py:340
  191.9 0.0 collective-permute-start.19
  191.9 5.6 %collective-permute-done.20.own_ref = bf16[640,256]{1,0:T(8,128)(2,1)} collective-permute-done((bf16[640,256]{1,0:T(8,128)(2,1)S(1)}, bf16[640,256]{1,0:T(8,128)(2,1)}, u32[]{:S(2)}, u32[]{:S(2)}) %collective-permute-start.20) | collective-permute-done | bytes 327712 | tf_op jit(solution)/shard_map/ppermute | solution.py:340
  197.5 24.1 %collective-permute-start.21 = (bf16[640,256]{1,0:T(8,128)(2,1)}, bf16[640,256]{1,0:T(8,128)(2,1)}, u32[]{:S(2)}, u32[]{:S(2)}) collective-permute-start(bf16[640,256]{1,0:T(8,128)(2,1)} %collective-permute-done.20.own_ref), channel_id=1, source_target_pairs={{0,4},{4,0},{8,12},{12,8},{1,5},{5,1},{9,13},{13,9},{2,6},{6,2},{1... | collective-permute-start | bytes 983048 | tf_op jit(solution)/shard_map/ppermute | solution.py:340
  221.6 0.1 collective-permute-start.10
  221.7 1.8 collective-permute-done.10.refs_13_
  223.5 0.0 collective-permute-done.9.refs_11_
  223.5 0.0 collective-permute-done.12.refs_15_
  223.5 0.8 copy-done.6
  224.3 0.1 copy-done.11
  224.4 0.2 copy-done.7
  224.5 0.1 copy-done.8
  224.6 9.8 %assemble.1.front_ref = bf16[640,2560]{1,0:T(8,128)(2,1)} custom-call(s32[2]{0:T(128)} %pad_add_fusion.pos_ref, s32[16]{0:T(128)} %get-tuple-element.19.krow_ref, s32[48]{0:T(128)} %get-tuple-element.20.kcol_ref, bf16[4,64,512]{2,1,0:T(8,128)(2,1)} %get-tuple-element.24.refs_0_, bf16[4,64,512]{2,1,0:T(8,128)(2,1)} %copy-done.2, bf16[8,64,512]{2,1,0:T(8,128)(2,1)} %copy-done, ...), custom_call_target="tpu_custom_call" | custom-call | tf_op jit(solution)/shard_map/assemble/pallas_call | solution.py:275
  234.5 4.0 %finish.1 = bf16[640,2560]{1,0:T(8,128)(2,1)} custom-call(s32[2]{0:T(128)} %pad_add_fusion.pos_ref, bf16[640,2560]{1,0:T(8,128)(2,1)} %assemble.1.front_ref, bf16[640,256]{1,0:T(8,128)(2,1)} %get-tuple-element.37.refs_17_.row_ref, bf16[640,256]{1,0:T(8,128)(2,1)} %collective-permute-done.20.own_ref, ...), custom_call_target="tpu_custom_call", output_to_operand_aliasing={{}: (1, {})} | custom-call | tf_op jit(solution)/shard_map/finish/pallas_call | solution.py:316
  (26 shorter events, 0.1 us)
Async XLA Ops:
  0.6 10.4 %collective-permute-start = (bf16[1024,2048]{1,0:T(8,128)(2,1)}, bf16[1024,2048]{1,0:T(8,128)(2,1)}, u32[]{:S(2)}, u32[]{:S(2)}) collective-permute-start(bf16[1024,2048]{1,0:T(8,128)(2,1)} %own_ref.7), channel_id=1, source_target_pairs={{0,4},{4,0},{8,12},{12,8},{1,5},{5,1},{9,13},{13,9},{2,6},{6,2},{1... | collective-permute-start | bytes 12582920 | tf_op jit(solution)/shard_map/ppermute | solution.py:340
  13.9 20.8 %all-to-all-start = ((bf16[16,64,512]{2,1,0:T(8,128)(2,1)}), bf16[16,64,512]{2,1,0:T(8,128)(2,1)}, u32[]{:S(2)}, u32[]{:S(2)}) async-start(bf16[16,64,512]{2,1,0:T(8,128)(2,1)} %shard_map.59), calls=%async_computation | async-start | bytes 2097152 | tf_op jit(solution)/shard_map/all_to_all | solution.py:355
  34.8 19.0 %all-to-all-start.1 = ((bf16[16,64,512]{2,1,0:T(8,128)(2,1)}), bf16[16,64,512]{2,1,0:T(8,128)(2,1)}, u32[]{:S(2)}, u32[]{:S(2)}) async-start(bf16[16,64,512]{2,1,0:T(8,128)(2,1)} %shard_map.61), calls=%async_computation.1 | async-start | bytes 2097152 | tf_op jit(solution)/shard_map/all_to_all | solution.py:355
  53.7 63.7 %all-to-all-start.2 = ((bf16[16,64,512]{2,1,0:T(8,128)(2,1)}), bf16[16,64,512]{2,1,0:T(8,128)(2,1)}, u32[]{:S(2)}, u32[]{:S(2)}) async-start(bf16[16,64,512]{2,1,0:T(8,128)(2,1)} %shard_map.63), calls=%async_computation.2 | async-start | bytes 2097152 | tf_op jit(solution)/shard_map/all_to_all | solution.py:355
  61.9 17.7 %collective-permute-start.2 = (bf16[8,64,512]{2,1,0:T(8,128)(2,1)}, bf16[8,64,512]{2,1,0:T(8,128)(2,1)S(1)}, u32[]{:S(2)}, u32[]{:S(2)}) collective-permute-start(bf16[8,64,512]{2,1,0:T(8,128)(2,1)} %get-tuple-element.26), channel_id=1, source_target_pairs={{0,8},{4,12},{8,0},{12,4},{1,9},{5,13},{9,1},{13,5},{2,10},{6,14},... | collective-permute-start | bytes 1572872 | tf_op jit(solution)/shard_map/ppermute | solution.py:340
  71.6 22.9 %collective-permute-start.5 = (bf16[8,64,512]{2,1,0:T(8,128)(2,1)}, bf16[8,64,512]{2,1,0:T(8,128)(2,1)}, u32[]{:S(2)}, u32[]{:S(2)}) collective-permute-start(bf16[8,64,512]{2,1,0:T(8,128)(2,1)} %get-tuple-element.29), channel_id=1, source_target_pairs={{0,8},{4,12},{8,0},{12,4},{1,9},{5,13},{9,1},{13,5},{2,10},{6,14},... | collective-permute-start | bytes 1572872 | tf_op jit(solution)/shard_map/ppermute | solution.py:340
  79.6 37.8 %copy-start = (bf16[8,64,512]{2,1,0:T(8,128)(2,1)}, bf16[8,64,512]{2,1,0:T(8,128)(2,1)S(1)}, u32[]{:S(2)}) copy-start(bf16[8,64,512]{2,1,0:T(8,128)(2,1)S(1)} %collective-permute-done.2.refs_2_) | copy-start | bytes 1572868
  79.6 46.7 %collective-permute-start.3 = (bf16[8,64,512]{2,1,0:T(8,128)(2,1)S(1)}, bf16[8,64,512]{2,1,0:T(8,128)(2,1)}, u32[]{:S(2)}, u32[]{:S(2)}) collective-permute-start(bf16[8,64,512]{2,1,0:T(8,128)(2,1)S(1)} %collective-permute-done.2.refs_2_), channel_id=1, source_target_pairs={{0,4},{4,0},{8,12},{12,8},{1,5},{5,1},{9,13},{13,9},{2,6},{6,2},{1... | collective-permute-start | bytes 1572872 | tf_op jit(solution)/shard_map/ppermute | solution.py:340
  94.5 32.5 %collective-permute-start.6 = (bf16[8,64,512]{2,1,0:T(8,128)(2,1)}, bf16[8,64,512]{2,1,0:T(8,128)(2,1)}, u32[]{:S(2)}, u32[]{:S(2)}) collective-permute-start(bf16[8,64,512]{2,1,0:T(8,128)(2,1)} %collective-permute-done.5.refs_6_), channel_id=1, source_target_pairs={{0,4},{4,0},{8,12},{12,8},{1,5},{5,1},{9,13},{13,9},{2,6},{6,2},{1... | collective-permute-start | bytes 1572872 | tf_op jit(solution)/shard_map/ppermute | solution.py:340
  117.4 34.9 %all-to-all-start.3 = ((bf16[16,64,512]{2,1,0:T(8,128)(2,1)}), bf16[16,64,512]{2,1,0:T(8,128)(2,1)}, u32[]{:S(2)}, u32[]{:S(2)}) async-start(bf16[16,64,512]{2,1,0:T(8,128)(2,1)} %shard_map.65), calls=%async_computation.3 | async-start | bytes 2097152 | tf_op jit(solution)/shard_map/all_to_all | solution.py:355
  124.1 1.8 collective-permute-start.1
  124.4 1.8 collective-permute-start.4
  125.9 1.1 copy-start.2
  126.3 0.7 copy-start.3
  131.2 16.2 %collective-permute-start.18 = (bf16[640,256]{1,0:T(8,128)(2,1)}, bf16[640,256]{1,0:T(8,128)(2,1)}, u32[]{:S(2)}, u32[]{:S(2)}) collective-permute-start(bf16[640,256]{1,0:T(8,128)(2,1)} %strip_panel.1), channel_id=1, source_target_pairs={{0,48},{4,52},{8,56},{12,60},{16,1},{20,5},{24,9},{28,13},{32,18},... | collective-permute-start | bytes 983048 | tf_op jit(solution)/shard_map/ppermute | solution.py:336
  136.5 18.6 %collective-permute-start.16 = (bf16[640,256]{1,0:T(8,128)(2,1)}, bf16[640,256]{1,0:T(8,128)(2,1)S(1)}, u32[]{:S(2)}, u32[]{:S(2)}) collective-permute-start(bf16[640,256]{1,0:T(8,128)(2,1)} %strip_panel.1), channel_id=1, source_target_pairs={{0,16},{4,20},{8,24},{12,28},{16,33},{20,37},{24,41},{28,45},{32,5... | collective-permute-start | bytes 983048 | tf_op jit(solution)/shard_map/ppermute | solution.py:336
  138.4 22.9 %collective-permute-start.17 = (bf16[640,256]{1,0:T(8,128)(2,1)}, bf16[640,256]{1,0:T(8,128)(2,1)}, u32[]{:S(2)}, u32[]{:S(2)}) collective-permute-start(bf16[640,256]{1,0:T(8,128)(2,1)} %strip_panel.1), channel_id=1, source_target_pairs={{0,32},{4,36},{8,40},{12,44},{16,49},{20,53},{24,57},{28,61},{32,2... | collective-permute-start | bytes 983048 | tf_op jit(solution)/shard_map/ppermute | solution.py:336
  143.4 18.2 %collective-permute-start.15 = (bf16[640,256]{1,0:T(8,128)(2,1)}, bf16[640,256]{1,0:T(8,128)(2,1)}, u32[]{:S(2)}, u32[]{:S(2)}) collective-permute-start(bf16[640,256]{1,0:T(8,128)(2,1)} %strip_panel.1), channel_id=1, source_target_pairs={{0,3},{4,7},{8,11},{12,15},{16,19},{20,23},{24,27},{28,31},{32,35}... | collective-permute-start | bytes 983048 | tf_op jit(solution)/shard_map/ppermute | solution.py:336
  145.5 16.1 %collective-permute-start.13 = (bf16[640,256]{1,0:T(8,128)(2,1)}, bf16[640,256]{1,0:T(8,128)(2,1)}, u32[]{:S(2)}, u32[]{:S(2)}) collective-permute-start(bf16[640,256]{1,0:T(8,128)(2,1)} %strip_panel.1), channel_id=1, source_target_pairs={{0,1},{4,5},{8,9},{12,13},{16,17},{20,21},{24,25},{28,29},{32,33},... | collective-permute-start | bytes 983048 | tf_op jit(solution)/shard_map/ppermute | solution.py:336
  147.5 20.4 %collective-permute-start.14 = (bf16[640,256]{1,0:T(8,128)(2,1)}, bf16[640,256]{1,0:T(8,128)(2,1)}, u32[]{:S(2)}, u32[]{:S(2)}) collective-permute-start(bf16[640,256]{1,0:T(8,128)(2,1)} %strip_panel.1), channel_id=1, source_target_pairs={{0,2},{4,6},{8,10},{12,14},{16,18},{20,22},{24,26},{28,30},{32,34}... | collective-permute-start | bytes 983048 | tf_op jit(solution)/shard_map/ppermute | solution.py:336
  155.1 6.5 %copy-start.9 = (bf16[640,256]{1,0:T(8,128)(2,1)}, bf16[640,256]{1,0:T(8,128)(2,1)S(1)}, u32[]{:S(2)}) copy-start(bf16[640,256]{1,0:T(8,128)(2,1)S(1)} %collective-permute-done.16) | copy-start | bytes 983044
  155.1 22.7 %collective-permute-start.8 = (bf16[8,64,512]{2,1,0:T(8,128)(2,1)}, bf16[8,64,512]{2,1,0:T(8,128)(2,1)S(1)}, u32[]{:S(2)}, u32[]{:S(2)}) collective-permute-start(bf16[8,64,512]{2,1,0:T(8,128)(2,1)} %get-tuple-element.32), channel_id=1, source_target_pairs={{0,8},{4,12},{8,0},{12,4},{1,9},{5,13},{9,1},{13,5},{2,10},{6,14},... | collective-permute-start | bytes 1572872 | tf_op jit(solution)/shard_map/ppermute | solution.py:340
  161.3 26.6 %collective-permute-start.11 = (bf16[8,64,512]{2,1,0:T(8,128)(2,1)}, bf16[8,64,512]{2,1,0:T(8,128)(2,1)S(1)}, u32[]{:S(2)}, u32[]{:S(2)}) collective-permute-start(bf16[8,64,512]{2,1,0:T(8,128)(2,1)} %get-tuple-element.35), channel_id=1, source_target_pairs={{0,8},{4,12},{8,0},{12,4},{1,9},{5,13},{9,1},{13,5},{2,10},{6,14},... | collective-permute-start | bytes 1572872 | tf_op jit(solution)/shard_map/ppermute | solution.py:340
  170.2 54.4 %copy-start.1 = (bf16[640,256]{1,0:T(8,128)(2,1)}, bf16[640,256]{1,0:T(8,128)(2,1)S(1)}, u32[]{:S(2)}) copy-start(bf16[640,256]{1,0:T(8,128)(2,1)S(1)} %get-tuple-element.36.refs_18_) | copy-start | bytes 983044
  170.2 27.3 %collective-permute-start.20 = (bf16[640,256]{1,0:T(8,128)(2,1)S(1)}, bf16[640,256]{1,0:T(8,128)(2,1)}, u32[]{:S(2)}, u32[]{:S(2)}) collective-permute-start(bf16[640,256]{1,0:T(8,128)(2,1)S(1)} %get-tuple-element.36.refs_18_), channel_id=1, source_target_pairs={{0,8},{4,12},{8,0},{12,4},{1,9},{5,13},{9,1},{13,5},{2,10},{6,14},... | collective-permute-start | bytes 983048 | tf_op jit(solution)/shard_map/ppermute | solution.py:340
  176.4 45.2 %collective-permute-start.7 = (bf16[4,64,512]{2,1,0:T(8,128)(2,1)}, bf16[4,64,512]{2,1,0:T(8,128)(2,1)S(1)}, u32[]{:S(2)}, u32[]{:S(2)}) collective-permute-start(bf16[4,64,512]{2,1,0:T(8,128)(2,1)} %get-tuple-element.31), channel_id=1, source_target_pairs={{0,4},{4,0},{8,12},{12,8},{1,5},{5,1},{9,13},{13,9},{2,6},{6,2},{1... | collective-permute-start | bytes 786440 | tf_op jit(solution)/shard_map/ppermute | solution.py:340
  177.8 46.8 %copy-start.4 = (bf16[8,64,512]{2,1,0:T(8,128)(2,1)}, bf16[8,64,512]{2,1,0:T(8,128)(2,1)S(1)}, u32[]{:S(2)}) copy-start(bf16[8,64,512]{2,1,0:T(8,128)(2,1)S(1)} %collective-permute-done.8.refs_10_) | copy-start | bytes 1572868
  177.8 45.6 %collective-permute-start.9 = (bf16[8,64,512]{2,1,0:T(8,128)(2,1)S(1)}, bf16[8,64,512]{2,1,0:T(8,128)(2,1)S(1)}, u32[]{:S(2)}, u32[]{:S(2)}) collective-permute-start(bf16[8,64,512]{2,1,0:T(8,128)(2,1)S(1)} %collective-permute-done.8.refs_10_), channel_id=1, source_target_pairs={{0,4},{4,0},{8,12},{12,8},{1,5},{5,1},{9,13},{13,9},{2,6},{6,2},{1... | collective-permute-start | bytes 1572872 | tf_op jit(solution)/shard_map/ppermute | solution.py:340
  187.9 35.6 %copy-start.5 = (bf16[8,64,512]{2,1,0:T(8,128)(2,1)}, bf16[8,64,512]{2,1,0:T(8,128)(2,1)S(1)}, u32[]{:S(2)}) copy-start(bf16[8,64,512]{2,1,0:T(8,128)(2,1)S(1)} %collective-permute-done.11.refs_14_) | copy-start | bytes 1572868
  187.9 35.5 %collective-permute-start.12 = (bf16[8,64,512]{2,1,0:T(8,128)(2,1)S(1)}, bf16[8,64,512]{2,1,0:T(8,128)(2,1)S(1)}, u32[]{:S(2)}, u32[]{:S(2)}) collective-permute-start(bf16[8,64,512]{2,1,0:T(8,128)(2,1)S(1)} %collective-permute-done.11.refs_14_), channel_id=1, source_target_pairs={{0,4},{4,0},{8,12},{12,8},{1,5},{5,1},{9,13},{13,9},{2,6},{6,2},{1... | collective-permute-start | bytes 1572872 | tf_op jit(solution)/shard_map/ppermute | solution.py:340
  191.9 31.6 %collective-permute-start.19 = (bf16[640,256]{1,0:T(8,128)(2,1)S(1)}, bf16[640,256]{1,0:T(8,128)(2,1)S(1)}, u32[]{:S(2)}, u32[]{:S(2)}) collective-permute-start(bf16[640,256]{1,0:T(8,128)(2,1)S(1)} %get-tuple-element.36.refs_18_), channel_id=1, source_target_pairs={{0,4},{4,0},{8,12},{12,8},{1,5},{5,1},{9,13},{13,9},{2,6},{6,2},{1... | collective-permute-start | bytes 983048 | tf_op jit(solution)/shard_map/ppermute | solution.py:340
  197.5 36.9 %collective-permute-start.21 = (bf16[640,256]{1,0:T(8,128)(2,1)}, bf16[640,256]{1,0:T(8,128)(2,1)}, u32[]{:S(2)}, u32[]{:S(2)}) collective-permute-start(bf16[640,256]{1,0:T(8,128)(2,1)} %collective-permute-done.20.own_ref), channel_id=1, source_target_pairs={{0,4},{4,0},{8,12},{12,8},{1,5},{5,1},{9,13},{13,9},{2,6},{6,2},{1... | collective-permute-start | bytes 983048 | tf_op jit(solution)/shard_map/ppermute | solution.py:340
  221.6 2.7 %copy-start.10 = (bf16[4,64,512]{2,1,0:T(8,128)(2,1)}, bf16[4,64,512]{2,1,0:T(8,128)(2,1)S(1)}, u32[]{:S(2)}) copy-start(bf16[4,64,512]{2,1,0:T(8,128)(2,1)S(1)} %collective-permute-done.7.refs_9_) | copy-start | bytes 786436
  221.6 1.8 collective-permute-start.10
  223.5 0.9 copy-start.11
  223.5 0.8 copy-start.6
  223.5 1.1 copy-start.7
  223.5 1.1 copy-start.8

commit v4 on v1

--- a/solution.py
+++ b/solution.py
@@ -283,32 +283,23 @@
 
 
 def finish(pos, front, row_panel, pieces):
-    rows, cols = front.shape
+    _, cols = front.shape
     wide = cols // 4
 
-    def kernel(pos_ref, front_ref, row_ref, *refs):
-        out_ref = refs[4]
-        for w in range(4):
-
-            @pl.when(pl.program_id(0) == w)
-            def _():
-                update = lax.dot_general(
-                    row_ref[...], refs[w][...], (((1,), (1,)), ((), ())),
-                    preferred_element_type=jnp.float32,
-                )
-                out_ref[...] = (front_ref[...].astype(jnp.float32) - update).astype(jnp.bfloat16)
-
-    whole = pl.BlockSpec(row_panel.shape, lambda w, pos_ref: (0, 0))
-    turned = pl.BlockSpec((rows, wide), lambda w, pos_ref: (0, (pos_ref[0] % 4) ^ w))
-    return pl.pallas_call(
-        kernel,
-        grid_spec=pltpu.PrefetchScalarGridSpec(
-            num_scalar_prefetch=1,
-            grid=(4,),
-            in_specs=[turned] + [whole] * 5,
-            out_specs=turned,
-        ),
+    def kernel(pos_ref, front_ref, row_ref, p0, p1, p2, p3, out_ref):
+        zk = pos_ref[0] % 4
+        for w, ref in enumerate((p0, p1, p2, p3)):
+            here = pl.ds(pl.multiple_of((zk ^ w) * wide, wide), wide)
+            update = lax.dot_general(
+                row_ref[...], ref[...], (((1,), (1,)), ((), ())), preferred_element_type=jnp.float32
+            )
+            out_ref[:, here] = (front_ref[:, here].astype(jnp.float32) - update).astype(jnp.bfloat16)
+
+    return pl.pallas_call(
+        kernel,
         out_shape=jax.ShapeDtypeStruct(front.shape, jnp.bfloat16),
+        in_specs=[pl.BlockSpec(memory_space=SMEM)] + [pl.BlockSpec(memory_space=VMEM)] * 6,
+        out_specs=pl.BlockSpec(memory_space=VMEM),
         compiler_params=params(63),
         name="finish",
     )(pos, front, row_panel, *pieces)
@@ -341,7 +332,8 @@
         part = lax.all_to_all(sent, ("x", "col"), 0, 0, tiled=True)
         stay, swap, out = pack_second(jl, pos, part)
         crossed = over_zk(out, 2)
-        arrived += [stay, over_zk(swap, 1), crossed, over_zk(crossed, 1)]
+        near = over_zk(swap, 1)
+        arrived += [stay, near, crossed, over_zk(crossed, 1)]
     first = arrived[:8]
 
     panel_0 = strip_panel(krow, kcol, first, front_orig, panel_inverse)

time: 209 us -> 208 us (level)
  no operation moved by 1% of the time
where the time goes in v4:
time: 208 us; the launch traced here: 207 us
  waiting for transfers between devices  107 us (51%)
  starting transfers between devices  54.4 us (26%)
  Pallas kernels  41.1 us (20%)
  other arithmetic  2.47 us (1%)
    ppermute x13, waiting for transfers between devices, over_zk(): return lax.ppermute(array, ('z', 'core'), [(r, r ^ d) for r in range(4)])  81.2 us
    ppermute x13, starting transfers between devices, over_zk(): return lax.ppermute(array, ('z', 'core'), [(r, r ^ d) for r in range(4)])  20.5 us
    all_to_all x3, waiting for transfers between devices, local(): part = lax.all_to_all(sent, ('x', 'col'), 0, 0, tiled=True)  20.4 us
    all_to_all x3, starting transfers between devices, local(): part = lax.all_to_all(sent, ('x', 'col'), 0, 0, tiled=True)  20.1 us
    ppermute x6, starting transfers between devices, moved(): return lax.ppermute(array, ('x', 'z', 'core', 'col'), pairs)  13.8 us
    pallas_call x3, Pallas kernels, pack_first(): pl.pallas_call(kernel, out_shape=jax.ShapeDtypeStruct((16, last - first,...  9.35 us
    pallas_call x3, Pallas kernels, pack_second(): pl.pallas_call(kernel, out_shape=[jax.ShapeDtypeStruct((n,) + arrived.sha...  9.25 us
    pallas_call x1, Pallas kernels, assemble(): pl.pallas_call(kernel, grid=(4,), out_shape=jax.ShapeDtypeStruct(front_or...  7.87 us
  transfers between devices with their start and end apart: 22, of which 11 were waited for; matrix products, arithmetic and copies ran while one was open for 1% of the time, Pallas kernels for 16%

profile of v4, /device:TPU:67, one launch (start us, length us, event | category | flops | bytes accessed | tf_op | source)
XLA Modules:
  0.0 207.0 jit_solution(16533488711362243327)
XLA Ops:
  0.6 0.8 collective-permute-start
  1.4 0.7 pad_add_fusion.pos_ref
  2.0 5.0 %tables.1 = (s32[32]{0:T(128)}, s32[32]{0:T(128)}, s32[48]{0:T(128)}, s32[16]{0:T(128)}, s32[48]{0:T(128)}) custom-call(s32[2,64]{1,0:T(2,128)} %map_ref.1, s32[2]{0:T(128)} %pad_add_fusion.pos_ref), custom_call_target="tpu_custom_call" | custom-call | tf_op jit(solution)/shard_map/tables/pallas_call | solution.py:90
  7.0 1.5 collective-permute-done.other_ref
  8.5 2.9 %shard_map.59 = bf16[16,64,512]{2,1,0:T(8,128)(2,1)} custom-call(s32[32]{0:T(128)} %get-tuple-element.19.sel_ref, s32[32]{0:T(128)} %get-tuple-element.20.jsel_ref, s32[2]{0:T(128)} %pad_add_fusion.pos_ref, bf16[1024,2048]{1,0:T(8,128)(2,1)} %own_ref.5, bf16[1024,2048]{1,0:T(8,128)(2,1)} %collective-permute-done.other_ref), custom_call_target="tpu_custom_call" | custom-call | tf_op jit(solution)/shard_map/pallas_call | solution.py:127
  11.4 6.9 %all-to-all-start = ((bf16[16,64,512]{2,1,0:T(8,128)(2,1)}), bf16[16,64,512]{2,1,0:T(8,128)(2,1)}, u32[]{:S(2)}, u32[]{:S(2)}) async-start(bf16[16,64,512]{2,1,0:T(8,128)(2,1)} %shard_map.59), calls=%async_computation | async-start | bytes 2097152 | tf_op jit(solution)/shard_map/all_to_all | solution.py:332
  18.3 2.9 %shard_map.61 = bf16[16,64,512]{2,1,0:T(8,128)(2,1)} custom-call(s32[32]{0:T(128)} %get-tuple-element.19.sel_ref, s32[32]{0:T(128)} %get-tuple-element.20.jsel_ref, s32[2]{0:T(128)} %pad_add_fusion.pos_ref, bf16[1024,2048]{1,0:T(8,128)(2,1)} %own_ref.5, bf16[1024,2048]{1,0:T(8,128)(2,1)} %collective-permute-done.other_ref), custom_call_target="tpu_custom_call" | custom-call | tf_op jit(solution)/shard_map/pallas_call | solution.py:127
  21.2 11.3 %all-to-all-done.in_ref = bf16[16,64,512]{2,1,0:T(8,128)(2,1)} async-done(((bf16[16,64,512]{2,1,0:T(8,128)(2,1)}), bf16[16,64,512]{2,1,0:T(8,128)(2,1)}, u32[]{:S(2)}, u32[]{:S(2)}) %all-to-all-start) | async-done | bytes 1048608 | tf_op jit(solution)/shard_map/all_to_all | solution.py:332
  32.5 6.1 %all-to-all-start.1 = ((bf16[16,64,512]{2,1,0:T(8,128)(2,1)}), bf16[16,64,512]{2,1,0:T(8,128)(2,1)}, u32[]{:S(2)}, u32[]{:S(2)}) async-start(bf16[16,64,512]{2,1,0:T(8,128)(2,1)} %shard_map.61), calls=%async_computation.1 | async-start | bytes 2097152 | tf_op jit(solution)/shard_map/all_to_all | solution.py:332
  38.6 3.6 %shard_map.63 = bf16[16,128,512]{2,1,0:T(8,128)(2,1)} custom-call(s32[32]{0:T(128)} %get-tuple-element.19.sel_ref, s32[32]{0:T(128)} %get-tuple-element.20.jsel_ref, s32[2]{0:T(128)} %pad_add_fusion.pos_ref, bf16[1024,2048]{1,0:T(8,128)(2,1)} %own_ref.5, bf16[1024,2048]{1,0:T(8,128)(2,1)} %collective-permute-done.other_ref), custom_call_target="tpu_custom_call" | custom-call | tf_op jit(solution)/shard_map/pallas_call | solution.py:127
  42.2 9.1 %all-to-all-done.1.in_ref = bf16[16,64,512]{2,1,0:T(8,128)(2,1)} async-done(((bf16[16,64,512]{2,1,0:T(8,128)(2,1)}), bf16[16,64,512]{2,1,0:T(8,128)(2,1)}, u32[]{:S(2)}, u32[]{:S(2)}) %all-to-all-start.1) | async-done | bytes 1048608 | tf_op jit(solution)/shard_map/all_to_all | solution.py:332
  51.3 7.1 %all-to-all-start.2 = ((bf16[16,128,512]{2,1,0:T(8,128)(2,1)}), bf16[16,128,512]{2,1,0:T(8,128)(2,1)}, u32[]{:S(2)}, u32[]{:S(2)}) async-start(bf16[16,128,512]{2,1,0:T(8,128)(2,1)} %shard_map.63), calls=%async_computation.2 | async-start | bytes 4194304 | tf_op jit(solution)/shard_map/all_to_all | solution.py:332
  58.4 2.8 %shard_map.60 = (bf16[4,64,512]{2,1,0:T(8,128)(2,1)}, bf16[4,64,512]{2,1,0:T(8,128)(2,1)}, bf16[8,64,512]{2,1,0:T(8,128)(2,1)}) custom-call(s32[48]{0:T(128)} %get-tuple-element.18.jl_ref, s32[2]{0:T(128)} %pad_add_fusion.pos_ref, bf16[16,64,512]{2,1,0:T(8,128)(2,1)} %all-to-all-done.in_ref), custom_call_target="tpu_custom_call" | custom-call | tf_op jit(solution)/shard_map/pallas_call | solution.py:151
  61.1 5.1 %collective-permute-start.2 = (bf16[8,64,512]{2,1,0:T(8,128)(2,1)}, bf16[8,64,512]{2,1,0:T(8,128)(2,1)S(1)}, u32[]{:S(2)}, u32[]{:S(2)}) collective-permute-start(bf16[8,64,512]{2,1,0:T(8,128)(2,1)} %get-tuple-element.23), channel_id=1, source_target_pairs={{0,8},{4,12},{8,0},{12,4},{1,9},{5,13},{9,1},{13,5},{2,10},{6,14},... | collective-permute-start | bytes 1572872 | tf_op jit(solution)/shard_map/ppermute | solution.py:317
  66.3 2.8 %shard_map.62 = (bf16[4,64,512]{2,1,0:T(8,128)(2,1)}, bf16[4,64,512]{2,1,0:T(8,128)(2,1)}, bf16[8,64,512]{2,1,0:T(8,128)(2,1)}) custom-call(s32[48]{0:T(128)} %get-tuple-element.18.jl_ref, s32[2]{0:T(128)} %pad_add_fusion.pos_ref, bf16[16,64,512]{2,1,0:T(8,128)(2,1)} %all-to-all-done.1.in_ref), custom_call_target="tpu_custom_call" | custom-call | tf_op jit(solution)/shard_map/pallas_call | solution.py:151
  69.1 0.3 collective-permute-start.5
  69.3 31.7 %collective-permute-done.2.refs_2_ = bf16[8,64,512]{2,1,0:T(8,128)(2,1)S(1)} collective-permute-done((bf16[8,64,512]{2,1,0:T(8,128)(2,1)}, bf16[8,64,512]{2,1,0:T(8,128)(2,1)S(1)}, u32[]{:S(2)}, u32[]{:S(2)}) %collective-permute-start.2) | collective-permute-done | bytes 524320 | tf_op jit(solution)/shard_map/ppermute | solution.py:317
  101.0 0.0 copy-start
  101.0 2.0 collective-permute-start.3
  103.0 9.3 %collective-permute-done.5.refs_6_ = bf16[8,64,512]{2,1,0:T(8,128)(2,1)} collective-permute-done((bf16[8,64,512]{2,1,0:T(8,128)(2,1)}, bf16[8,64,512]{2,1,0:T(8,128)(2,1)}, u32[]{:S(2)}, u32[]{:S(2)}) %collective-permute-start.5) | collective-permute-done | bytes 524320 | tf_op jit(solution)/shard_map/ppermute | solution.py:317
  112.3 1.3 collective-permute-start.6
  113.6 0.0 all-to-all-done.2.in_ref
  113.6 3.7 %shard_map.64 = (bf16[4,128,512]{2,1,0:T(8,128)(2,1)}, bf16[4,128,512]{2,1,0:T(8,128)(2,1)}, bf16[8,128,512]{2,1,0:T(8,128)(2,1)}) custom-call(s32[48]{0:T(128)} %get-tuple-element.18.jl_ref, s32[2]{0:T(128)} %pad_add_fusion.pos_ref, bf16[16,128,512]{2,1,0:T(8,128)(2,1)} %all-to-all-done.2.in_ref), custom_call_target="tpu_custom_call" | custom-call | tf_op jit(solution)/shard_map/pallas_call | solution.py:151
  117.3 4.7 %collective-permute-start.8 = (bf16[8,128,512]{2,1,0:T(8,128)(2,1)}, bf16[8,128,512]{2,1,0:T(8,128)(2,1)}, u32[]{:S(2)}, u32[]{:S(2)}) collective-permute-start(bf16[8,128,512]{2,1,0:T(8,128)(2,1)} %get-tuple-element.29), channel_id=1, source_target_pairs={{0,8},{4,12},{8,0},{12,4},{1,9},{5,13},{9,1},{13,5},{2,10},{6,14},... | collective-permute-start | bytes 3145736 | tf_op jit(solution)/shard_map/ppermute | solution.py:317
  122.0 0.3 collective-permute-start.1
  122.2 0.2 collective-permute-start.4
  122.5 1.2 collective-permute-done.1.refs_1_
  123.7 0.0 copy-start.2
  123.7 0.4 collective-permute-done.4.refs_5_
  124.1 0.0 copy-start.3
  124.1 0.0 collective-permute-done.3.refs_3_
  124.1 0.7 copy-done.3
  124.8 0.0 collective-permute-done.6.refs_7_
  124.8 0.0 copy-done
  124.8 0.0 copy-done.2
  124.8 4.3 %strip_panel.1 = bf16[640,256]{1,0:T(8,128)(2,1)} custom-call(s32[16]{0:T(128)} %get-tuple-element.16.krow_ref, s32[48]{0:T(128)} %get-tuple-element.17.kcol_ref, bf16[4,64,512]{2,1,0:T(8,128)(2,1)} %get-tuple-element.21.refs_0_, bf16[4,64,512]{2,1,0:T(8,128)(2,1)} %copy-done.2, bf16[8,64,512]{2,1,0:T(8,128)(2,1)} %copy-done, ...), custom_call_target="tpu_custom_call" | custom-call | tf_op jit(solution)/shard_map/strip_panel/pallas_call | solution.py:226
  129.1 3.1 %collective-permute-start.15 = (bf16[640,256]{1,0:T(8,128)(2,1)}, bf16[640,256]{1,0:T(8,128)(2,1)S(1)}, u32[]{:S(2)}, u32[]{:S(2)}) collective-permute-start(bf16[640,256]{1,0:T(8,128)(2,1)} %strip_panel.1), channel_id=1, source_target_pairs={{0,48},{4,52},{8,56},{12,60},{16,1},{20,5},{24,9},{28,13},{32,18},... | collective-permute-start | bytes 983048 | tf_op jit(solution)/shard_map/ppermute | solution.py:313
  132.2 1.9 collective-permute-start.13
  134.1 1.3 collective-permute-start.14
  135.4 1.3 collective-permute-start.12
  136.7 2.5 %collective-permute-done.15 = bf16[640,256]{1,0:T(8,128)(2,1)S(1)} collective-permute-done((bf16[640,256]{1,0:T(8,128)(2,1)}, bf16[640,256]{1,0:T(8,128)(2,1)S(1)}, u32[]{:S(2)}, u32[]{:S(2)}) %collective-permute-start.15) | collective-permute-done | bytes 327712 | tf_op jit(solution)/shard_map/ppermute | solution.py:313
  139.2 1.3 collective-permute-start.10
  140.5 2.5 %collective-permute-done.13 = bf16[640,256]{1,0:T(8,128)(2,1)S(1)} collective-permute-done((bf16[640,256]{1,0:T(8,128)(2,1)}, bf16[640,256]{1,0:T(8,128)(2,1)S(1)}, u32[]{:S(2)}, u32[]{:S(2)}) %collective-permute-start.13) | collective-permute-done | bytes 327712 | tf_op jit(solution)/shard_map/ppermute | solution.py:313
  143.1 4.9 %collective-permute-start.11 = (bf16[640,256]{1,0:T(8,128)(2,1)}, bf16[640,256]{1,0:T(8,128)(2,1)S(1)}, u32[]{:S(2)}, u32[]{:S(2)}) collective-permute-start(bf16[640,256]{1,0:T(8,128)(2,1)} %strip_panel.1), channel_id=1, source_target_pairs={{0,2},{4,6},{8,10},{12,14},{16,18},{20,22},{24,26},{28,30},{32,34}... | collective-permute-start | bytes 983048 | tf_op jit(solution)/shard_map/ppermute | solution.py:313
  148.0 21.1 %collective-permute-done.8.refs_10_ = bf16[8,128,512]{2,1,0:T(8,128)(2,1)} collective-permute-done((bf16[8,128,512]{2,1,0:T(8,128)(2,1)}, bf16[8,128,512]{2,1,0:T(8,128)(2,1)}, u32[]{:S(2)}, u32[]{:S(2)}) %collective-permute-start.8) | collective-permute-done | bytes 1048608 | tf_op jit(solution)/shard_map/ppermute | solution.py:317
  169.1 0.6 collective-permute-start.9
  169.7 0.0 collective-permute-done.14
  169.7 0.0 collective-permute-done.12
  169.7 0.0 collective-permute-done.10
  169.7 0.0 collective-permute-done.11
  169.7 1.8 add_select_fusion
  171.5 4.2 %collective-permute-start.17 = (bf16[640,256]{1,0:T(8,128)(2,1)S(1)}, bf16[640,256]{1,0:T(8,128)(2,1)}, u32[]{:S(2)}, u32[]{:S(2)}) collective-permute-start(bf16[640,256]{1,0:T(8,128)(2,1)S(1)} %get-tuple-element.30.p0), channel_id=1, source_target_pairs={{0,8},{4,12},{8,0},{12,4},{1,9},{5,13},{9,1},{13,5},{2,10},{6,14},... | collective-permute-start | bytes 983048 | tf_op jit(solution)/shard_map/ppermute | solution.py:317
  175.8 0.3 collective-permute-start.7
  176.1 0.2 collective-permute-start.16
  176.3 16.0 %collective-permute-done.17.p2 = bf16[640,256]{1,0:T(8,128)(2,1)} collective-permute-done((bf16[640,256]{1,0:T(8,128)(2,1)S(1)}, bf16[640,256]{1,0:T(8,128)(2,1)}, u32[]{:S(2)}, u32[]{:S(2)}) %collective-permute-start.17) | collective-permute-done | bytes 327712 | tf_op jit(solution)/shard_map/ppermute | solution.py:317
  192.3 0.6 collective-permute-start.18
  192.8 0.0 collective-permute-done.7.refs_9_
  192.9 0.0 collective-permute-done.9.refs_11_
  192.9 0.8 copy-done.4
  193.6 7.9 %assemble.1.front_ref = bf16[640,2560]{1,0:T(8,128)(2,1)} custom-call(s32[16]{0:T(128)} %get-tuple-element.16.krow_ref, s32[48]{0:T(128)} %get-tuple-element.17.kcol_ref, bf16[4,64,512]{2,1,0:T(8,128)(2,1)} %get-tuple-element.21.refs_0_, bf16[4,64,512]{2,1,0:T(8,128)(2,1)} %copy-done.2, bf16[8,64,512]{2,1,0:T(8,128)(2,1)} %copy-done, ...), custom_call_target="tpu_custom_call" | custom-call | tf_op jit(solution)/shard_map/assemble/pallas_call | solution.py:267
  201.5 0.0 copy-done.1
  201.5 0.0 collective-permute-done.16.p1
  201.5 0.0 collective-permute-done.18.p3
  201.6 5.4 %finish.1 = bf16[640,2560]{1,0:T(8,128)(2,1)} custom-call(s32[2]{0:T(128)} %pad_add_fusion.pos_ref, bf16[640,2560]{1,0:T(8,128)(2,1)} %assemble.1.front_ref, bf16[640,256]{1,0:T(8,128)(2,1)} %get-tuple-element.31.row_ref, bf16[640,256]{1,0:T(8,128)(2,1)} %copy-done.1, bf16[640,256]{1,0:T(8,128)(2,1)} %collective-permute-done.16.p1, ...), custom_call_target="tpu_custom_call" | custom-call | tf_op jit(solution)/shard_map/finish/pallas_call | solution.py:298
  (2 shorter events, 0.0 us)
Async XLA Ops:
  0.6 7.9 %collective-permute-start = (bf16[1024,2048]{1,0:T(8,128)(2,1)}, bf16[1024,2048]{1,0:T(8,128)(2,1)}, u32[]{:S(2)}, u32[]{:S(2)}) collective-permute-start(bf16[1024,2048]{1,0:T(8,128)(2,1)} %own_ref.5), channel_id=1, source_target_pairs={{0,4},{4,0},{8,12},{12,8},{1,5},{5,1},{9,13},{13,9},{2,6},{6,2},{1... | collective-permute-start | bytes 12582920 | tf_op jit(solution)/shard_map/ppermute | solution.py:317
  11.4 21.1 %all-to-all-start = ((bf16[16,64,512]{2,1,0:T(8,128)(2,1)}), bf16[16,64,512]{2,1,0:T(8,128)(2,1)}, u32[]{:S(2)}, u32[]{:S(2)}) async-start(bf16[16,64,512]{2,1,0:T(8,128)(2,1)} %shard_map.59), calls=%async_computation | async-start | bytes 2097152 | tf_op jit(solution)/shard_map/all_to_all | solution.py:332
  32.5 18.8 %all-to-all-start.1 = ((bf16[16,64,512]{2,1,0:T(8,128)(2,1)}), bf16[16,64,512]{2,1,0:T(8,128)(2,1)}, u32[]{:S(2)}, u32[]{:S(2)}) async-start(bf16[16,64,512]{2,1,0:T(8,128)(2,1)} %shard_map.61), calls=%async_computation.1 | async-start | bytes 2097152 | tf_op jit(solution)/shard_map/all_to_all | solution.py:332
  51.3 62.3 %all-to-all-start.2 = ((bf16[16,128,512]{2,1,0:T(8,128)(2,1)}), bf16[16,128,512]{2,1,0:T(8,128)(2,1)}, u32[]{:S(2)}, u32[]{:S(2)}) async-start(bf16[16,128,512]{2,1,0:T(8,128)(2,1)} %shard_map.63), calls=%async_computation.2 | async-start | bytes 4194304 | tf_op jit(solution)/shard_map/all_to_all | solution.py:332
  61.1 39.8 %collective-permute-start.2 = (bf16[8,64,512]{2,1,0:T(8,128)(2,1)}, bf16[8,64,512]{2,1,0:T(8,128)(2,1)S(1)}, u32[]{:S(2)}, u32[]{:S(2)}) collective-permute-start(bf16[8,64,512]{2,1,0:T(8,128)(2,1)} %get-tuple-element.23), channel_id=1, source_target_pairs={{0,8},{4,12},{8,0},{12,4},{1,9},{5,13},{9,1},{13,5},{2,10},{6,14},... | collective-permute-start | bytes 1572872 | tf_op jit(solution)/shard_map/ppermute | solution.py:317
  69.1 43.3 %collective-permute-start.5 = (bf16[8,64,512]{2,1,0:T(8,128)(2,1)}, bf16[8,64,512]{2,1,0:T(8,128)(2,1)}, u32[]{:S(2)}, u32[]{:S(2)}) collective-permute-start(bf16[8,64,512]{2,1,0:T(8,128)(2,1)} %get-tuple-element.26), channel_id=1, source_target_pairs={{0,8},{4,12},{8,0},{12,4},{1,9},{5,13},{9,1},{13,5},{2,10},{6,14},... | collective-permute-start | bytes 1572872 | tf_op jit(solution)/shard_map/ppermute | solution.py:317
  101.0 23.8 %copy-start = (bf16[8,64,512]{2,1,0:T(8,128)(2,1)}, bf16[8,64,512]{2,1,0:T(8,128)(2,1)S(1)}, u32[]{:S(2)}) copy-start(bf16[8,64,512]{2,1,0:T(8,128)(2,1)S(1)} %collective-permute-done.2.refs_2_) | copy-start | bytes 1572868
  101.0 23.1 %collective-permute-start.3 = (bf16[8,64,512]{2,1,0:T(8,128)(2,1)S(1)}, bf16[8,64,512]{2,1,0:T(8,128)(2,1)}, u32[]{:S(2)}, u32[]{:S(2)}) collective-permute-start(bf16[8,64,512]{2,1,0:T(8,128)(2,1)S(1)} %collective-permute-done.2.refs_2_), channel_id=1, source_target_pairs={{0,4},{4,0},{8,12},{12,8},{1,5},{5,1},{9,13},{13,9},{2,6},{6,2},{1... | collective-permute-start | bytes 1572872 | tf_op jit(solution)/shard_map/ppermute | solution.py:317
  112.3 12.5 %collective-permute-start.6 = (bf16[8,64,512]{2,1,0:T(8,128)(2,1)}, bf16[8,64,512]{2,1,0:T(8,128)(2,1)}, u32[]{:S(2)}, u32[]{:S(2)}) collective-permute-start(bf16[8,64,512]{2,1,0:T(8,128)(2,1)} %collective-permute-done.5.refs_6_), channel_id=1, source_target_pairs={{0,4},{4,0},{8,12},{12,8},{1,5},{5,1},{9,13},{13,9},{2,6},{6,2},{1... | collective-permute-start | bytes 1572872 | tf_op jit(solution)/shard_map/ppermute | solution.py:317
  117.3 51.8 %collective-permute-start.8 = (bf16[8,128,512]{2,1,0:T(8,128)(2,1)}, bf16[8,128,512]{2,1,0:T(8,128)(2,1)}, u32[]{:S(2)}, u32[]{:S(2)}) collective-permute-start(bf16[8,128,512]{2,1,0:T(8,128)(2,1)} %get-tuple-element.29), channel_id=1, source_target_pairs={{0,8},{4,12},{8,0},{12,4},{1,9},{5,13},{9,1},{13,5},{2,10},{6,14},... | collective-permute-start | bytes 3145736 | tf_op jit(solution)/shard_map/ppermute | solution.py:317
  122.0 1.7 collective-permute-start.1
  122.2 1.8 collective-permute-start.4
  123.7 1.1 copy-start.2
  124.1 0.7 copy-start.3
  129.1 10.2 %collective-permute-start.15 = (bf16[640,256]{1,0:T(8,128)(2,1)}, bf16[640,256]{1,0:T(8,128)(2,1)S(1)}, u32[]{:S(2)}, u32[]{:S(2)}) collective-permute-start(bf16[640,256]{1,0:T(8,128)(2,1)} %strip_panel.1), channel_id=1, source_target_pairs={{0,48},{4,52},{8,56},{12,60},{16,1},{20,5},{24,9},{28,13},{32,18},... | collective-permute-start | bytes 983048 | tf_op jit(solution)/shard_map/ppermute | solution.py:313
  132.2 10.9 %collective-permute-start.13 = (bf16[640,256]{1,0:T(8,128)(2,1)}, bf16[640,256]{1,0:T(8,128)(2,1)S(1)}, u32[]{:S(2)}, u32[]{:S(2)}) collective-permute-start(bf16[640,256]{1,0:T(8,128)(2,1)} %strip_panel.1), channel_id=1, source_target_pairs={{0,16},{4,20},{8,24},{12,28},{16,33},{20,37},{24,41},{28,45},{32,5... | collective-permute-start | bytes 983048 | tf_op jit(solution)/shard_map/ppermute | solution.py:313
  134.1 35.6 %collective-permute-start.14 = (bf16[640,256]{1,0:T(8,128)(2,1)}, bf16[640,256]{1,0:T(8,128)(2,1)S(1)}, u32[]{:S(2)}, u32[]{:S(2)}) collective-permute-start(bf16[640,256]{1,0:T(8,128)(2,1)} %strip_panel.1), channel_id=1, source_target_pairs={{0,32},{4,36},{8,40},{12,44},{16,49},{20,53},{24,57},{28,61},{32,2... | collective-permute-start | bytes 983048 | tf_op jit(solution)/shard_map/ppermute | solution.py:313
  135.4 34.3 %collective-permute-start.12 = (bf16[640,256]{1,0:T(8,128)(2,1)}, bf16[640,256]{1,0:T(8,128)(2,1)S(1)}, u32[]{:S(2)}, u32[]{:S(2)}) collective-permute-start(bf16[640,256]{1,0:T(8,128)(2,1)} %strip_panel.1), channel_id=1, source_target_pairs={{0,3},{4,7},{8,11},{12,15},{16,19},{20,23},{24,27},{28,31},{32,35}... | collective-permute-start | bytes 983048 | tf_op jit(solution)/shard_map/ppermute | solution.py:313
  139.2 30.5 %collective-permute-start.10 = (bf16[640,256]{1,0:T(8,128)(2,1)}, bf16[640,256]{1,0:T(8,128)(2,1)S(1)}, u32[]{:S(2)}, u32[]{:S(2)}) collective-permute-start(bf16[640,256]{1,0:T(8,128)(2,1)} %strip_panel.1), channel_id=1, source_target_pairs={{0,1},{4,5},{8,9},{12,13},{16,17},{20,21},{24,25},{28,29},{32,33},... | collective-permute-start | bytes 983048 | tf_op jit(solution)/shard_map/ppermute | solution.py:313
  143.1 26.6 %collective-permute-start.11 = (bf16[640,256]{1,0:T(8,128)(2,1)}, bf16[640,256]{1,0:T(8,128)(2,1)S(1)}, u32[]{:S(2)}, u32[]{:S(2)}) collective-permute-start(bf16[640,256]{1,0:T(8,128)(2,1)} %strip_panel.1), channel_id=1, source_target_pairs={{0,2},{4,6},{8,10},{12,14},{16,18},{20,22},{24,26},{28,30},{32,34}... | collective-permute-start | bytes 983048 | tf_op jit(solution)/shard_map/ppermute | solution.py:313
  169.1 23.8 %collective-permute-start.9 = (bf16[8,128,512]{2,1,0:T(8,128)(2,1)}, bf16[8,128,512]{2,1,0:T(8,128)(2,1)}, u32[]{:S(2)}, u32[]{:S(2)}) collective-permute-start(bf16[8,128,512]{2,1,0:T(8,128)(2,1)} %collective-permute-done.8.refs_10_), channel_id=1, source_target_pairs={{0,4},{4,0},{8,12},{12,8},{1,5},{5,1},{9,13},{13,9},{2,6},{6,2},{1... | collective-permute-start | bytes 3145736 | tf_op jit(solution)/shard_map/ppermute | solution.py:317
  171.5 30.0 %copy-start.1 = (bf16[640,256]{1,0:T(8,128)(2,1)}, bf16[640,256]{1,0:T(8,128)(2,1)S(1)}, u32[]{:S(2)}) copy-start(bf16[640,256]{1,0:T(8,128)(2,1)S(1)} %get-tuple-element.30.p0) | copy-start | bytes 983044
  171.5 20.7 %collective-permute-start.17 = (bf16[640,256]{1,0:T(8,128)(2,1)S(1)}, bf16[640,256]{1,0:T(8,128)(2,1)}, u32[]{:S(2)}, u32[]{:S(2)}) collective-permute-start(bf16[640,256]{1,0:T(8,128)(2,1)S(1)} %get-tuple-element.30.p0), channel_id=1, source_target_pairs={{0,8},{4,12},{8,0},{12,4},{1,9},{5,13},{9,1},{13,5},{2,10},{6,14},... | collective-permute-start | bytes 983048 | tf_op jit(solution)/shard_map/ppermute | solution.py:317
  175.8 17.1 %collective-permute-start.7 = (bf16[4,128,512]{2,1,0:T(8,128)(2,1)}, bf16[4,128,512]{2,1,0:T(8,128)(2,1)S(1)}, u32[]{:S(2)}, u32[]{:S(2)}) collective-permute-start(bf16[4,128,512]{2,1,0:T(8,128)(2,1)} %get-tuple-element.28), channel_id=1, source_target_pairs={{0,4},{4,0},{8,12},{12,8},{1,5},{5,1},{9,13},{13,9},{2,6},{6,2},{1... | collective-permute-start | bytes 1572872 | tf_op jit(solution)/shard_map/ppermute | solution.py:317
  176.1 25.5 %collective-permute-start.16 = (bf16[640,256]{1,0:T(8,128)(2,1)S(1)}, bf16[640,256]{1,0:T(8,128)(2,1)}, u32[]{:S(2)}, u32[]{:S(2)}) collective-permute-start(bf16[640,256]{1,0:T(8,128)(2,1)S(1)} %get-tuple-element.30.p0), channel_id=1, source_target_pairs={{0,4},{4,0},{8,12},{12,8},{1,5},{5,1},{9,13},{13,9},{2,6},{6,2},{1... | collective-permute-start | bytes 983048 | tf_op jit(solution)/shard_map/ppermute | solution.py:317
  192.3 9.3 %collective-permute-start.18 = (bf16[640,256]{1,0:T(8,128)(2,1)}, bf16[640,256]{1,0:T(8,128)(2,1)}, u32[]{:S(2)}, u32[]{:S(2)}) collective-permute-start(bf16[640,256]{1,0:T(8,128)(2,1)} %collective-permute-done.17.p2), channel_id=1, source_target_pairs={{0,4},{4,0},{8,12},{12,8},{1,5},{5,1},{9,13},{13,9},{2,6},{6,2},{1... | collective-permute-start | bytes 983048 | tf_op jit(solution)/shard_map/ppermute | solution.py:317
  192.9 0.8 copy-start.4
